TPU v7x, 128 devices: a whole 4x4x4 slice. The times are simulated.
128 devices in a mesh: elem: 32 (over y, x, core), face: 4 (over z).
Axes of the slice: x: 4, y: 4, z: 4, core: 2. Of those that a mesh axis runs over, the one named last changes fastest.
Arguments:
- state: float32 [10, 72, 65536], P(None, None, ('elem', 'face')), may hold values from -6 to 6
- metric: float32 [16, 4096], P(None, ('elem', 'face')), may hold values from 0.5 to 2
- neighbours: int32 [4, 4096], P(None, ('elem', 'face')), may hold values from 0 to 4095, as said below
- cost_class: int32 [16, 4096], P(None, ('elem', 'face')), may hold values from 1 to 4
- batch_slot: int32 [16, 4096], replicated, may hold values from 0 to 65535, as said below
- level_mix: float32 [10, 72, 72], replicated, may hold values from -0.75 to 0.75
- field_coupling_matrix: float32 [10, 10], replicated, may hold values from -2 to 2
Outputs:
- state_out: float32 [10, 72, 65536], P(None, None, ('elem', 'face'))
- physics_state: float32 [10, 72, 65536], P(None, None, ('elem', 'face'))
Inputs may be any that keep to these rules, and one draw needn't show every extreme that they name: Blocks are the element ranges [b * 32, (b + 1) * 32), in the order of the devices. The elements form a closed grid of rows of 8 elements, 4 rows a block; neighbours[0], [1], [2], [3] name the elements east, west, north and south, which are mutual (the west neighbour of the east one is the element itself, likewise north and south, and east of north is north of east). East and west neighbours lie in the element's own block; a north neighbour lies in the same block or in the next one, a south neighbour in the same block or the previous one, cyclically over the blocks; in each block exactly 8 elements have their north neighbour in the next block and 8 their south neighbour in the previous one. `batch_slot`: A permutation of the columns; batch c holds the places [c * 512, (c + 1) * 512). Every batch holds exactly 4 columns of every block, and within a batch cost_class never rises from one place to the next.
All inputs are finite; a program needn't handle non-finite values.
Results may differ from a plain program's by a relative error of at most 0.0001.
Values sent between devices are 32-bit elements; how exact they have to be, the bound alone decides.
No kernel may reach another device: no remote copies, remote signals or barrier semaphores. Data moves between devices by JAX's collectives and lax.ppermute only.
A program may use at most 128 MiB of HBM per device.

v0:
```python
from functools import partial
import math

import jax
import jax.numpy as jnp
import numpy as np
from jax import lax
from jax.sharding import PartitionSpec as P

ROWS_DEV = 4
SUBSTEPS = 3
SWEEPS = 4


PHYSICS_RATE = 0.1
TIME_STEP = 0.02


def from_behind(array, axis, by):
    length = lax.axis_size(axis)
    return lax.ppermute(array, axis, [(i, (i + by) % length) for i in range(length)])


def side_by_side(arrays, axis, split_dim, concat_dim, along):
    widths = [a.shape[along] for a in arrays]
    both = jnp.concatenate(arrays, axis=along)
    result = lax.all_to_all(both, axis, split_axis=split_dim, concat_axis=concat_dim, tiled=True)
    return tuple(jnp.split(result, [sum(widths[:k]) for k in range(1, len(widths))], axis=along))


def gll_matrices():
    gll_nodes = np.array([-1.0, -1.0 / np.sqrt(5.0), 1.0 / np.sqrt(5.0), 1.0])
    derivative = np.zeros((4, 4))
    for target in range(4):
        for source in range(4):
            if target == source:
                derivative[target, source] = sum(
                    (
                        1.0 / (gll_nodes[source] - gll_nodes[middle])
                        for middle in range(4)
                        if middle != source
                    )
                )
            else:
                numerator = np.prod(
                    [
                        gll_nodes[target] - gll_nodes[middle]
                        for middle in range(4)
                        if middle != source and middle != target
                    ]
                )
                denominator = np.prod(
                    [
                        gll_nodes[source] - gll_nodes[middle]
                        for middle in range(4)
                        if middle != source
                    ]
                )
                derivative[target, source] = numerator / denominator
    across = np.kron(np.eye(4), derivative).astype(np.float32)
    upward = np.kron(derivative, np.eye(4)).astype(np.float32)
    return (jnp.asarray(across), jnp.asarray(upward))


def invert(permutation):
    extent = permutation.shape[0]
    return jnp.zeros((extent,), jnp.int32).at[permutation].set(jnp.arange(extent, dtype=jnp.int32))


def advect(current, across, upward):
    along_x = jnp.einsum("pq,...qe->...pe", across, current, precision=lax.Precision.HIGHEST)
    along_y = jnp.einsum("pq,...qe->...pe", upward, current, precision=lax.Precision.HIGHEST)
    return -(current[0:1] * along_x + current[1:2] * along_y)


def rank_of(targets, remote):
    smaller = (targets[None, :] < targets[:, None]) & remote[None, :]
    return jnp.sum(smaller.astype(jnp.int32), axis=1)


def cross_rows(south_row, north_row, neighbours, myself):
    members = south_row.shape[-1]
    boundary = members // ROWS_DEV
    sequence = jnp.arange(members, dtype=jnp.int32)
    remote_up = neighbours[2] // members != myself
    remote_down = neighbours[3] // members != myself
    up_list = jnp.argsort(jnp.where(remote_up, sequence, sequence + members))[:boundary]
    down_list = jnp.argsort(jnp.where(remote_down, sequence, sequence + members))[:boundary]
    from_prev = from_behind(jnp.take(north_row, up_list, axis=-1), ("elem", "face"), 1)
    from_next = from_behind(jnp.take(south_row, down_list, axis=-1), ("elem", "face"), -1)
    up_rank = jnp.where(remote_up, rank_of(neighbours[2], remote_up), 0)
    down_rank = jnp.where(remote_down, rank_of(neighbours[3], remote_down), 0)
    local_up = jnp.where(remote_up, 0, neighbours[2] - myself * members)
    local_down = jnp.where(remote_down, 0, neighbours[3] - myself * members)
    north_side = jnp.where(
        remote_up, jnp.take(from_next, up_rank, axis=-1), jnp.take(south_row, local_up, axis=-1)
    )
    south_side = jnp.where(
        remote_down,
        jnp.take(from_prev, down_rank, axis=-1),
        jnp.take(north_row, local_down, axis=-1),
    )
    return (north_side, south_side)


def combine(values, neighbours, myself):
    leading = values.shape[:-2]
    members = values.shape[-1]
    layout = values.reshape(leading + (4, 4, members))
    west_edge = layout[..., :, 0, :]
    east_edge = layout[..., :, 3, :]
    base_id = myself * members
    new_east = east_edge + jnp.take(west_edge, neighbours[0] - base_id, axis=-1)
    new_west = west_edge + jnp.take(east_edge, neighbours[1] - base_id, axis=-1)
    stepped = jnp.stack([new_west, layout[..., :, 1, :], layout[..., :, 2, :], new_east], axis=-2)
    south_row = stepped[..., 0, :, :]
    north_row = stepped[..., 3, :, :]
    north_side, south_side = cross_rows(south_row, north_row, neighbours, myself)
    physics_output = jnp.stack(
        [
            south_row + south_side,
            stepped[..., 1, :, :],
            stepped[..., 2, :, :],
            north_row + north_side,
        ],
        axis=-3,
    )
    return physics_output.reshape(values.shape)


def relax(segment, active, level_mix, field_coupling_matrix):
    level_blended = jnp.einsum("flm,fmc->flc", level_mix, segment, precision=lax.Precision.HIGHEST)
    field_coupled = jnp.einsum(
        "mx,xaq->maq", field_coupling_matrix, level_blended, precision=lax.Precision.HIGHEST
    )
    return jnp.where(
        active[None, None, :], segment + PHYSICS_RATE * jnp.tanh(field_coupled), segment
    )


def advance_block(
    threshold, block_cols, weighted, level_mix, field_coupling_matrix, block_index, current
):
    offset_cols = block_index * block_cols
    segment = lax.dynamic_slice_in_dim(current, offset_cols, block_cols, axis=2)
    active = lax.dynamic_slice_in_dim(weighted, offset_cols, block_cols) > threshold
    return lax.dynamic_update_slice_in_dim(
        current, relax(segment, active, level_mix, field_coupling_matrix), offset_cols, axis=2
    )


def advance_sorted(columns, classes, level_mix, field_coupling_matrix):
    width = columns.shape[-1]
    block_cols = math.gcd(width, 256)
    weighted = classes * SWEEPS

    def physics_pass(threshold, current):
        live_count = jnp.sum((weighted > threshold).astype(jnp.int32))
        trip_count = (live_count + block_cols - 1) // block_cols
        return lax.fori_loop(
            0,
            trip_count,
            partial(
                advance_block, threshold, block_cols, weighted, level_mix, field_coupling_matrix
            ),
            current,
        )

    return lax.fori_loop(0, 4 * SWEEPS, physics_pass, columns)


def per_device(state, metric, neighbours, cost_class, batch_slot, level_mix, field_coupling_matrix):
    fields, levels, columns_dev = state.shape
    points, members = metric.shape
    grid_state = jnp.transpose(state.reshape(fields, levels, members, points), (0, 1, 3, 2))
    devices = lax.axis_size(("elem", "face"))
    myself = lax.axis_index(("elem", "face"))
    sequence = jnp.arange(columns_dev, dtype=jnp.int32)
    columns = grid_state.reshape(fields, levels, columns_dev)
    own_class = cost_class.reshape(columns_dev)
    my_slots = lax.dynamic_slice_in_dim(batch_slot, myself * members, members, axis=1).reshape(
        columns_dev
    )
    send_order = jnp.argsort(my_slots)
    send_back = invert(send_order)
    column_of = invert(batch_slot.reshape(batch_slot.size))
    owned = lax.dynamic_slice_in_dim(column_of, myself * columns_dev, columns_dev)
    source = owned % (members * devices) // members
    arrival = jnp.argsort(source * columns_dev + sequence)
    arrival_back = invert(arrival)
    outgoing = jnp.take(columns, send_order, axis=2).reshape(fields * levels, columns_dev)
    class_row = jnp.take(own_class, send_order).astype(jnp.float32)[None, :]
    arrived, arrived_class = side_by_side((outgoing, class_row), ("elem", "face"), 1, 1, 0)
    batch_cols = jnp.take(arrived, arrival_back, axis=1).reshape(fields, levels, columns_dev)
    batch_class = jnp.take(arrived_class[0], arrival_back).astype(jnp.int32)
    physics_state = advance_sorted(batch_cols, batch_class, level_mix, field_coupling_matrix)
    change = jnp.take(
        (physics_state - batch_cols).reshape(fields * levels, columns_dev), arrival, axis=1
    )
    returned = lax.all_to_all(change, ("elem", "face"), split_axis=1, concat_axis=1, tiled=True)
    physics_tendency = jnp.take(returned, send_back, axis=1)
    physics_tendency = physics_tendency.reshape(grid_state.shape)
    across, upward = gll_matrices()
    mass_total = combine(metric[None, None], neighbours, myself)
    current = grid_state
    for advection_substep in range(SUBSTEPS):
        rate = advect(current, across, upward)
        updated = current + TIME_STEP * rate + physics_tendency / SUBSTEPS
        current = combine(metric * updated, neighbours, myself) / mass_total
    state_out = jnp.transpose(current, (0, 1, 3, 2)).reshape(fields, levels, columns_dev)
    return (state_out, physics_state)


def solution(mesh):
    placed = (
        P(None, None, ("elem", "face")),
        P(None, ("elem", "face")),
        P(None, ("elem", "face")),
        P(None, ("elem", "face")),
        P(),
        P(),
        P(),
    )
    return jax.shard_map(
        per_device,
        mesh=mesh,
        in_specs=placed,
        out_specs=(P(None, None, ("elem", "face")), P(None, None, ("elem", "face"))),
        check_vma=False,
    )
```

profile of v0, /device:TPU:0, one launch (start us, length us, event | category | flops | bytes accessed | tf_op | source)
XLA Modules:
  0.0 602.7 jit_solution(9789559072760586803)
XLA Ops:
  13.1 3.8 sort.74
  16.9 3.5 gather_fusion.1
  24.4 3.5 copy.180
  28.0 5.2 gather_fusion
  33.1 3.9 gather.36
  39.0 10.6 %all-to-all-start = ((f32[721,128,4]{0,2,1:T(4,128)}), f32[721,128,4]{0,2,1:T(4,128)S(1)}, u32[]{:S(2)}, u32[]{:S(2)}) async-start(f32[721,128,4]{0,2,1:T(4,128)} %pad_maximum_fusion), calls=%async_computation | async-start | bytes 3145728 | tf_op jit(solution)/shard_map/all_to_all | solution.py:27
  51.0 239.6 %scatter_custom_fusion = s32[65536]{0:T(1024)S(1)} fusion(s32[65536]{0:T(1024)S(1)} %bitcast.432, s32[65536]{0:T(1024)S(1)} %iota.45, s32[]{:T(128)} %constant.280.clone.1), kind=kCustom, calls=%fused_computation.156 | custom fusion | bytes 262148 | tf_op jit(solution)/shard_map/scatter | solution.py:67
  290.6 3.8 sort.75
  294.5 2.9 scatter_custom_fusion.2
  303.2 3.5 gather_fusion.2
  312.5 78.3 %while.53 = (s32[]{:T(128)}, f32[10,72,512]{2,1,0:T(8,128)S(1)}, s32[512]{0:T(512)S(1)}, f32[10,72,72]{2,1,0:T(8,128)S(1)}, f32[10,10]{1,0:T(8,128)S(1)}, /*inde...) while((s32[]{:T(128)}, f32[10,72,512]{2,1,0:T(8,128)S(1)}, ...), condition=%wide.region_8.10_spmd, body=%wide.region_4.9_spmd.sunk | while | flops 181925648 | bytes 5976802 | solution.py:169
  313.9 5.7 while.54
  320.9 5.7 while.54
  327.9 5.7 while.54
  335.0 5.7 while.54
  342.0 2.9 while.54
  346.2 2.9 while.54
  350.4 2.9 while.54
  354.6 2.9 while.54
  358.7 2.9 while.54
  362.9 2.9 while.54
  367.1 2.9 while.54
  371.2 2.9 while.54
  375.4 2.9 while.54
  379.6 2.9 while.54
  383.8 2.9 while.54
  387.9 2.9 while.54
  396.9 2.7 select_bitcast_fusion
  399.6 2.9 all_to_all.13
  402.6 10.2 %all-to-all-start.1 = ((f32[720,128,4]{0,2,1:T(4,128)}), f32[720,128,4]{0,2,1:T(4,128)}, u32[]{:S(2)}, u32[]{:S(2)}) async-start(f32[720,128,4]{0,2,1:T(4,128)} %all_to_all.13), calls=%async_computation.1 | async-start | bytes 3145728 | tf_op jit(solution)/shard_map/all_to_all | solution.py:200
  414.2 3.8 fusion.84
  420.7 7.2 %collective-permute-start.3 = (f32[1,1,4,8]{3,2,1,0:T(4,128)S(1)}, f32[1,1,4,8]{3,2,1,0:T(4,128)S(1)}, u32[]{:S(2)}, u32[]{:S(2)}) collective-permute-start(f32[1,1,4,8]{3,2,1,0:T(4,128)S(1)} %bitcast_select_fusion.8), channel_id=1, source_target_pairs={{0,127},{1,0},{2,1},{3,2},{4,3},{5,4},{6,5},{7,6},{8,7},{9,8},{10,... | collective-permute-start | bytes 392 | tf_op jit(solution)/shard_map/ppermute | solution.py:21
  430.6 6.1 %all-to-all-done.1 = f32[720,128,4]{0,2,1:T(4,128)} async-done(((f32[720,128,4]{0,2,1:T(4,128)}), f32[720,128,4]{0,2,1:T(4,128)}, u32[]{:S(2)}, u32[]{:S(2)}) %all-to-all-start.1) | async-done | bytes 1474592 | tf_op jit(solution)/shard_map/all_to_all | solution.py:200
  441.8 4.9 div.102
  446.7 7.1 %fusion.30 = f32[10,72,16,32]{1,2,3,0:T(8,128)S(1)} fusion(f32[10,72,16,32]{1,2,3,0:T(8,128)S(1)} %bitcast.399, f32[16,10,72,32]{2,0,3,1:T(8,128)} %fusion.84, f32[16,16,1,1]{1,0,3,2:T(8,128)S(1)} %copy-done.29, f32[72,16,32]{0,1,2:T(8,128)S(1)} %copy-done.27, f32[72,16,32]{0,1,2:T(8,128)S(1)} %get-tuple-element.337, f32[16,32]{0,1:T(8,128)S(1)} %copy.177, ...), kind=kOutput, calls=%fused_computation.89 | convolution fusion | flops 73728000 | bytes 6196224 | tf_op jit(solution)/shard_map/pq,...qe->...pe/dot_general | solution.py:72
  471.8 6.5 %collective-permute-done = f32[10,72,4,8]{1,2,0,3:T(4,128)S(1)} collective-permute-done((f32[10,72,4,8]{1,2,0,3:T(4,128)}, f32[10,72,4,8]{1,2,0,3:T(4,128)S(1)}, u32[]{:S(2)}, u32[]{:S(2)}) %collective-permute-start) | collective-permute-done | bytes 92192 | tf_op jit(solution)/shard_map/ppermute | solution.py:21
  480.1 3.3 fusion.51
  488.8 2.9 gather_fusion.13
  501.3 4.3 fusion.24
  509.6 3.0 gather_fusion.22
  523.3 6.6 %collective-permute-done.4 = f32[10,72,4,8]{1,2,0,3:T(4,128)S(1)} collective-permute-done((f32[10,72,4,8]{1,2,0,3:T(4,128)}, f32[10,72,4,8]{1,2,0,3:T(4,128)S(1)}, u32[]{:S(2)}, u32[]{:S(2)}) %collective-permute-start.4) | collective-permute-done | bytes 92192 | tf_op jit(solution)/shard_map/ppermute | solution.py:21
  531.7 3.3 fusion.46
  538.2 2.8 gather_fusion.29
  552.3 4.3 fusion.18
  560.5 2.9 gather_fusion.30
  572.8 8.6 %collective-permute-done.6 = f32[10,72,4,8]{1,2,0,3:T(4,128)S(1)} collective-permute-done((f32[10,72,4,8]{1,2,0,3:T(4,128)}, f32[10,72,4,8]{1,2,0,3:T(4,128)S(1)}, u32[]{:S(2)}, u32[]{:S(2)}) %collective-permute-start.6) | collective-permute-done | bytes 92192 | tf_op jit(solution)/shard_map/ppermute | solution.py:21
  583.1 3.3 fusion.41
  589.0 2.8 gather_fusion.37
  (346 shorter events, 209.6 us)
Async XLA Ops:
  6.0 16.9 %copy-start.32 = (pred[8]{0:T(512)(128)(4,1)}, pred[8]{0:T(512)(128)(4,1)S(1)}, u32[]{:S(2)}) copy-start(pred[8]{0:T(512)(128)(4,1)S(1)} %get-tuple-element.309) | copy-start | bytes 28
  9.5 408.6 %collective-permute-start.2 = (f32[1,1,4,8]{3,2,1,0:T(4,128)S(1)}, f32[1,1,4,8]{3,2,1,0:T(4,128)S(1)}, u32[]{:S(2)}, u32[]{:S(2)}) collective-permute-start(f32[1,1,4,8]{3,2,1,0:T(4,128)S(1)} %bitcast_select_fusion.11), channel_id=1, source_target_pairs={{0,1},{1,2},{2,3},{3,4},{4,5},{5,6},{6,7},{7,8},{8,9},{9,10},{10,1... | collective-permute-start | bytes 392 | tf_op jit(solution)/shard_map/ppermute | solution.py:21
  22.9 1.6 copy-start.2
  37.4 12.9 %copy-start.28 = (s32[16,4096]{1,0:T(8,128)S(1)}, s32[16,4096]{1,0:T(8,128)}, u32[]{:S(2)}) copy-start(s32[16,4096]{1,0:T(8,128)} %param.31) | copy-start | bytes 786436
  39.0 255.4 %copy-start.31 = (f32[16,32]{1,0:T(8,128)S(1)}, f32[16,32]{1,0:T(8,128)}, u32[]{:S(2)}) copy-start(f32[16,32]{1,0:T(8,128)} %param.28) | copy-start | bytes 6148
  39.0 263.7 %all-to-all-start = ((f32[721,128,4]{0,2,1:T(4,128)}), f32[721,128,4]{0,2,1:T(4,128)S(1)}, u32[]{:S(2)}, u32[]{:S(2)}) async-start(f32[721,128,4]{0,2,1:T(4,128)} %pad_maximum_fusion), calls=%async_computation | async-start | bytes 3145728 | tf_op jit(solution)/shard_map/all_to_all | solution.py:27
  310.5 2.0 copy-start.1
  310.5 2.0 copy-start.23
  390.8 3.4 copy-start
  399.6 13.8 %copy-start.3 = (f32[10,72,512]{1,2,0:T(8,128)S(1)}, f32[10,72,512]{1,2,0:T(8,128)}, u32[]{:S(2)}) copy-start(f32[10,72,512]{1,2,0:T(8,128)} %copy-done.2) | copy-start | bytes 4423684
  402.6 11.6 %copy-start.30 = (f32[16,16,1,1]{1,0,3,2:T(8,128)S(1)}, f32[16,16,1,1]{1,0,3,2:T(8,128)}, u32[]{:S(2)}) copy-start(f32[16,16,1,1]{1,0,3,2:T(8,128)} %constant.303) | copy-start | bytes 3076
  402.6 34.0 %all-to-all-start.1 = ((f32[720,128,4]{0,2,1:T(4,128)}), f32[720,128,4]{0,2,1:T(4,128)}, u32[]{:S(2)}, u32[]{:S(2)}) async-start(f32[720,128,4]{0,2,1:T(4,128)} %all_to_all.13), calls=%async_computation.1 | async-start | bytes 3145728 | tf_op jit(solution)/shard_map/all_to_all | solution.py:200
  414.2 6.5 %copy-start.34 = (pred[8]{0:T(512)(128)(4,1)S(1)}, pred[8]{0:T(512)(128)(4,1)}, u32[]{:S(2)}) copy-start(pred[8]{0:T(512)(128)(4,1)} %get-tuple-element.317) | copy-start | bytes 28
  420.7 8.5 %collective-permute-start.3 = (f32[1,1,4,8]{3,2,1,0:T(4,128)S(1)}, f32[1,1,4,8]{3,2,1,0:T(4,128)S(1)}, u32[]{:S(2)}, u32[]{:S(2)}) collective-permute-start(f32[1,1,4,8]{3,2,1,0:T(4,128)S(1)} %bitcast_select_fusion.8), channel_id=1, source_target_pairs={{0,127},{1,0},{2,1},{3,2},{4,3},{5,4},{6,5},{7,6},{8,7},{9,8},{10,... | collective-permute-start | bytes 392 | tf_op jit(solution)/shard_map/ppermute | solution.py:21
  438.4 1.9 copy-start.37
  441.8 4.9 copy-start.4
  441.8 4.9 copy-start.27
  441.8 4.9 copy-start.29
  453.8 1.5 copy-start.7
  456.6 2.0 copy-start.22
  460.3 4.5 copy-start.8
  463.1 0.8 copy-start.9
  464.0 0.8 copy-start.11
  467.5 10.8 %collective-permute-start = (f32[10,72,4,8]{1,2,0,3:T(4,128)}, f32[10,72,4,8]{1,2,0,3:T(4,128)S(1)}, u32[]{:S(2)}, u32[]{:S(2)}) collective-permute-start(f32[10,72,4,8]{1,2,0,3:T(4,128)} %select_bitcast_fusion.7), channel_id=1, source_target_pairs={{0,1},{1,2},{2,3},{3,4},{4,5},{5,6},{6,7},{7,8},{8,9},{9,10},{10,1... | collective-permute-start | bytes 276488 | tf_op jit(solution)/shard_map/ppermute | solution.py:21
  483.4 1.7 copy-start.35
  485.9 5.8 collective-permute-start.1
  494.5 1.8 copy-start.10
  494.5 1.8 copy-start.12
  494.5 1.9 copy-start.24
  498.9 2.4 copy-start.5
  512.5 2.3 copy-start.21
  514.8 1.0 copy-start.17
  515.8 0.9 copy-start.19
  519.6 10.4 %collective-permute-start.4 = (f32[10,72,4,8]{1,2,0,3:T(4,128)}, f32[10,72,4,8]{1,2,0,3:T(4,128)S(1)}, u32[]{:S(2)}, u32[]{:S(2)}) collective-permute-start(f32[10,72,4,8]{1,2,0,3:T(4,128)} %select_bitcast_fusion.5), channel_id=1, source_target_pairs={{0,1},{1,2},{2,3},{3,4},{4,5},{5,6},{6,7},{7,8},{8,9},{9,10},{10,1... | collective-permute-start | bytes 276488 | tf_op jit(solution)/shard_map/ppermute | solution.py:21
  538.2 5.5 collective-permute-start.5
  545.5 1.8 copy-start.18
  545.5 1.8 copy-start.20
  545.5 1.9 copy-start.26
  549.9 2.4 copy-start.6
  567.1 0.9 copy-start.13
  567.9 0.8 copy-start.15
  568.8 1.5 copy-start.33
  571.0 10.4 %collective-permute-start.6 = (f32[10,72,4,8]{1,2,0,3:T(4,128)}, f32[10,72,4,8]{1,2,0,3:T(4,128)S(1)}, u32[]{:S(2)}, u32[]{:S(2)}) collective-permute-start(f32[10,72,4,8]{1,2,0,3:T(4,128)} %select_bitcast_fusion.3), channel_id=1, source_target_pairs={{0,1},{1,2},{2,3},{3,4},{4,5},{5,6},{6,7},{7,8},{8,9},{9,10},{10,1... | collective-permute-start | bytes 276488 | tf_op jit(solution)/shard_map/ppermute | solution.py:21
  586.5 1.7 copy-start.36
  589.0 5.5 collective-permute-start.7
  596.3 1.8 copy-start.14
  596.3 1.8 copy-start.16
  596.3 1.9 copy-start.25
where the time goes:
time: 612 us; the launch traced here: 603 us
  local copies, waits for them, and re-layouts  367 us (60%)
  other arithmetic  87.9 us (14%)
  matrix products  67.5 us (11%)
  waiting for transfers between devices  33.8 us (6%)
  starting transfers between devices  33.3 us (5%)
  loops' own time  11.4 us (2%)
    scatter x3, local copies, waits for them, and re-layouts, invert(): jnp.zeros((extent,), jnp.int32).at[permutation]  245 us
    ppermute x8, waiting for transfers between devices, from_behind(): lax.ppermute(array, axis, [(i, (i + by) % length) for i in range(length)])  27.8 us
    dot_general x20, matrix products, relax(): jnp.einsum('mx,xaq->maq', field_coupling_matrix, level_blended, precision...  27.4 us
    another operation x12, other arithmetic, combine(): jnp.stack([south_row + south_side, stepped[..., 1, :, :], stepped[..., 2,...  22.7 us
    dot_general x20, matrix products, relax(): jnp.einsum('flm,fmc->flc', level_mix, segment, precision=lax.Precision.HI...  15.9 us
    dot_general x3, matrix products, advect(): jnp.einsum('pq,...qe->...pe', upward, current, precision=lax.Precision.HI...  15.7 us
    ppermute x8, starting transfers between devices, from_behind(): lax.ppermute(array, axis, [(i, (i + by) % length) for i in range(length)])  12.5 us
  transfers between devices with their start and end apart: 10, of which 7 were waited for; matrix products, arithmetic and copies ran while one was open for 65% of the time, Pallas kernels for 0%

commit v1 on v0

v1 whole, which is shorter than its diff:
```python
from functools import partial

import jax
import jax.numpy as jnp
import numpy as np
from jax import lax
from jax.experimental import pallas as pl
from jax.experimental.pallas import tpu as pltpu
from jax.sharding import PartitionSpec as P

AXES = ("elem", "face")
F32 = jnp.float32
BF16 = jnp.bfloat16
HIGHEST = lax.Precision.HIGHEST
FIELDS, LEVELS, SUBSTEPS = 10, 72, 3
ROWS, COLS, MEMBERS, WIDE = 720, 512, 32, 768
TALL = ROWS + 8
PHYSICS_RATE, TIME_STEP = 0.1, 0.02
VM = pl.BlockSpec(memory_space=pltpu.VMEM)
SM = pl.BlockSpec(memory_space=pltpu.SMEM)
PARAMS = pltpu.CompilerParams(vmem_limit_bytes=60 << 20)


def gll_matrix():
    nodes = np.array([-1.0, -1.0 / np.sqrt(5.0), 1.0 / np.sqrt(5.0), 1.0])
    derivative = np.zeros((4, 4))
    for i in range(4):
        for j in range(4):
            others = [k for k in range(4) if k != j]
            if i == j:
                derivative[i, j] = sum(1.0 / (nodes[j] - nodes[k]) for k in others)
            else:
                top = np.prod([nodes[i] - nodes[k] for k in others if k != i])
                derivative[i, j] = top / np.prod([nodes[j] - nodes[k] for k in others])
    return derivative


def derivative_blocks():
    d = gll_matrix()
    across = np.kron(np.eye(4), d).astype(np.float32).T
    upward = np.kron(d, np.eye(4)).astype(np.float32).T
    return np.kron(np.eye(16), across).astype(np.float32), np.kron(np.eye(16), upward).astype(np.float32)

def split2(v):
    hi = v.astype(BF16)
    return hi, (v - hi.astype(F32)).astype(BF16)


def dot(a, b):
    return jnp.dot(a, b, preferred_element_type=F32)


def dot_nt(a, b):
    return lax.dot_general(a, b, (((1,), (1,)), ((), ())), preferred_element_type=F32)


def iota(shape, dim):
    return lax.broadcasted_iota(jnp.int32, shape, dim)


def expand_points(table):
    spread = jnp.where(iota((32, COLS), 1) // 16 == iota((32, COLS), 0), 1.0, 0.0)
    wide = jnp.dot(table, spread, precision=HIGHEST, preferred_element_type=F32)
    wide = jnp.where(iota((16, COLS), 1) % 16 == iota((16, COLS), 0), wide, 0.0)
    return jnp.sum(wide, axis=0, keepdims=True)


def as_column(row):
    return jnp.transpose(jnp.broadcast_to(row, (8, COLS)))[:, 0:1]


def rank_row(key_row):
    key_col = as_column(key_row)
    return jnp.sum(jnp.where(key_col < key_row, 1.0, 0.0), axis=0, keepdims=True)


def physics_kernel(fcm_ref, state_ref, class_ref, slot_ref, mix_ref, send_ref, tend_ref,
                   k32, kh, kl, x0, yy, tt, rr, qq, pp):
    rep = jnp.where(
        (iota((72, WIDE), 1) % 72 == iota((72, WIDE), 0)) & (iota((72, WIDE), 1) < ROWS), 1.0, 0.0)
    lane = iota((1, WIDE), 1)
    for f in range(10):
        crow = jnp.zeros((1, WIDE), F32)
        for g in range(10):
            crow = jnp.where((lane >= 72 * g) & (lane < 72 * g + 72), fcm_ref[g, f], crow)
        tiled = jnp.dot(jnp.transpose(mix_ref[f]), rep, precision=HIGHEST, preferred_element_type=F32)
        k32[72 * f:72 * f + 72, :] = tiled * crow
    k32[ROWS:WIDE, :] = jnp.zeros((WIDE - ROWS, WIDE), F32)
    hi, lo = split2(k32[...])
    kh[...] = hi
    kl[...] = lo
    cls = expand_points(class_ref[...].astype(F32))
    slot = expand_points(slot_ref[...].astype(F32))
    col = iota((1, COLS), 1).astype(F32)
    crank = rank_row((4.0 - cls) * COLS + col)
    srank = rank_row(slot)
    place = slot - jnp.floor(slot * (1.0 / COLS)) * COLS
    perm = jnp.where(iota((COLS, COLS), 0).astype(F32) == crank, 1.0, 0.0).astype(BF16)
    pp[...] = perm
    sh, sl = split2(state_ref[...])
    x0[:, 0:ROWS] = dot_nt(perm, sh) + dot_nt(perm, sl)
    extra = jnp.where(iota((128, COLS), 0) == 0, place, jnp.where(iota((128, COLS), 0) == 1, srank, 0.0))
    eh, el = split2(extra)
    tail = dot_nt(perm, eh) + dot_nt(perm, el)
    x0[:, ROWS:WIDE] = tail[:, 0:WIDE - ROWS]
    eh8, el8 = split2(jnp.broadcast_to(srank, (16, COLS)))
    srank_sorted = (dot_nt(eh8, perm) + dot_nt(el8, perm))[0:1, :]
    n1 = jnp.sum(jnp.where(cls > 1.5, 1, 0))
    n2 = jnp.sum(jnp.where(cls > 2.5, 1, 0))
    n3 = jnp.sum(jnp.where(cls > 3.5, 1, 0))
    xh, xl = split2(x0[...])
    yy[...] = dot(xh, kh[...]) + dot(xl, kh[...]) + dot(xh, kl[...])
    tt[...] = jnp.zeros((COLS, WIDE), F32)
    rr[...] = jnp.zeros((COLS, WIDE), F32)

    def rows_step(rows, live):
        for b in range(0, rows, 64):
            at = pl.ds(b, 64)
            t = jnp.tanh(yy[at, :])
            active = iota((64, WIDE), 0) + b < live
            tt[at, :] += jnp.where(active, t, 0.0)
            s = t + rr[at, :]
            q = s.astype(BF16)
            rr[at, :] = s - q.astype(F32)
            qq[at, :] = q
        q = qq[0:rows, :]
        yy[0:rows, :] += 0.1 * (dot(q, kh[...]) + dot(q, kl[...]))

    def sweep(k, _):
        live = jnp.where(k < 4, COLS, jnp.where(k < 8, n1, jnp.where(k < 12, n2, n3)))
        sizes = [64 * (i + 1) for i in range(8)]
        which = (live + 63) // 64
        for i, rows in enumerate(sizes):
            @pl.when(which == i + 1)
            def _():
                rows_step(rows, live)
        return 0

    lax.fori_loop(0, 16, sweep, 0)
    q_send = jnp.where(iota((COLS, COLS), 0).astype(F32) == srank_sorted, 1.0, 0.0).astype(BF16)
    fh, fl = split2(x0[...] + 0.1 * tt[...])
    out = dot(q_send, fh) + dot(q_send, fl)
    send_ref[...] = out.reshape(COLS // 4, 4, WIDE)
    th, tl = split2(jnp.transpose(tt[...])[0:ROWS, :] * (0.1 / 3.0))
    tend_ref[...] = dot(th, perm) + dot(tl, perm)


def physics_call(state2, cost_class, slots, level_mix, fcm):
    return call(
        physics_kernel, "physics", [((COLS // 4, 4, WIDE), F32), ((ROWS, COLS), F32)], [SM, VM, VM, VM, VM],
        [((WIDE, WIDE), F32), ((WIDE, WIDE), BF16), ((WIDE, WIDE), BF16)] + [((COLS, WIDE), F32)] * 4
        + [((COLS, WIDE), BF16), ((COLS, COLS), BF16)],
    )(fcm, state2, cost_class, slots, level_mix)


def element_tables(neighbours_ref, base_ref):
    local = neighbours_ref[...] - base_ref[0]
    outside = (local < 0) | (local >= MEMBERS)
    wide = jnp.concatenate([local.astype(F32), jnp.where(outside, 1.0, 0.0)], axis=0)
    spread = jnp.where(iota((MEMBERS, COLS), 1) // 16 == iota((MEMBERS, COLS), 0), 1.0, 0.0)
    by_column = jnp.dot(wide, spread, precision=HIGHEST, preferred_element_type=F32)
    return wide, by_column, spread


def east_west(by_column):
    col = iota((1, COLS), 1)
    ix, line = col % 4, (col % 16) // 4 * 4
    source = jnp.where(ix == 3, 16.0 * by_column[0:1] + line.astype(F32),
                       jnp.where(ix == 0, 16.0 * by_column[1:2] + (line + 3).astype(F32), -1.0))
    row = iota((COLS, COLS), 0)
    hit = (row.astype(F32) == source) | (row == iota((COLS, COLS), 1))
    return jnp.where(hit, 1.0, 0.0).astype(BF16)


def north_south(by_column):
    col = iota((1, COLS), 1)
    ix, iy = (col % 4).astype(F32), (col % 16) // 4
    north = jnp.where(by_column[6:7] > 0.5, -1.0, 16.0 * by_column[2:3] + ix)
    south = jnp.where(by_column[7:8] > 0.5, -1.0, 16.0 * by_column[3:4] + 12.0 + ix)
    source = jnp.where(iy == 3, north, jnp.where(iy == 0, south, -1.0))
    row = iota((COLS, COLS), 0)
    hit = (row.astype(F32) == source) | (row == iota((COLS, COLS), 1))
    return jnp.where(hit, 1.0, 0.0).astype(BF16)


def rank_among(key, member, spread):
    key8 = jnp.broadcast_to(jnp.where(member > 0.5, key, 1e9), (8, MEMBERS))
    key_col = jnp.transpose(key8)[:, 0:1]
    rank = jnp.sum(jnp.where(key_col < key, 1.0, 0.0), axis=0, keepdims=True)
    return jnp.dot(jnp.broadcast_to(rank, (8, MEMBERS)), spread, precision=HIGHEST,
                   preferred_element_type=F32)[0:1]


def halo_targets(wide, by_column, spread):
    col = iota((1, COLS), 1)
    ix, iy = (col % 4).astype(F32), (col % 16) // 4
    own = iota((1, MEMBERS), 1).astype(F32)
    up, down = by_column[6:7] > 0.5, by_column[7:8] > 0.5
    to_north = jnp.where((iy == 3) & up, 8.0 * ix + rank_among(own, wide[6:7], spread), -1.0)
    to_south = jnp.where((iy == 0) & down, 8.0 * ix + rank_among(own, wide[7:8], spread), -1.0)
    from_south = jnp.where((iy == 0) & down, 8.0 * ix + rank_among(wide[3:4], wide[7:8], spread), -1.0)
    from_north = jnp.where((iy == 3) & up, 8.0 * ix + rank_among(wide[2:3], wide[6:7], spread), -1.0)
    return to_north, to_south, from_south, from_north


def two_selections(first, second):
    row = iota((2 * MEMBERS, COLS), 0).astype(F32)
    hit = (row == first) | ((row - MEMBERS == second) & (second > -0.5))
    return jnp.where(hit, 1.0, 0.0).astype(BF16)


def tables_kernel(base_ref, neighbours_ref, metric_ref, whole_ref, out_ref, in_ref, mrow_ref):
    wide, by_column, spread = element_tables(neighbours_ref, base_ref)
    along = east_west(by_column)
    whole_ref[...] = dot(along, north_south(by_column)).astype(BF16)
    to_north, to_south, from_south, from_north = halo_targets(wide, by_column, spread)
    out_ref[...] = dot_nt(two_selections(to_north, to_south), along).astype(BF16)
    in_ref[...] = two_selections(from_south, from_north)
    mrow_ref[...] = jnp.broadcast_to(expand_points(metric_ref[...]), (8, COLS))


def move(read, tend_ref, mrow_ref, dx_ref, dy_ref, out_ref, dxs, dys, m_ref, north_ref, south_ref):
    vh, vl = split2(read(0, ROWS))
    for half in (0, 256):
        at = slice(half, half + 256)
        for d_ref, acc in ((dx_ref, dxs), (dy_ref, dys)):
            dh, dl = split2(d_ref[...])
            acc[:, at] = dot(vh[:, at], dh) + dot(vl[:, at], dh) + dot(vh[:, at], dl)
    metric = mrow_ref[0:1, :]
    u, v = read(0, LEVELS), read(LEVELS, LEVELS)
    for f in range(FIELDS):
        at = pl.ds(LEVELS * f, LEVELS)
        rate = u * dxs[at, :] + v * dys[at, :]
        m_ref[at, :] = metric * ((read(LEVELS * f, LEVELS) - TIME_STEP * rate) + tend_ref[at, :])
    m_ref[ROWS:TALL, :] = mrow_ref[...]
    mh, ml = split2(m_ref[...])
    halo = dot_nt(out_ref[...], mh) + dot_nt(out_ref[...], ml)
    north_ref[:, 0:TALL] = halo[0:MEMBERS]
    south_ref[:, 0:TALL] = halo[MEMBERS:]
    north_ref[:, TALL:WIDE] = jnp.zeros((MEMBERS, WIDE - TALL), F32)
    south_ref[:, TALL:WIDE] = jnp.zeros((MEMBERS, WIDE - TALL), F32)


def first_kernel(state_ref, tend_ref, mrow_ref, dx_ref, dy_ref, out_ref, m_ref, north_ref, south_ref, dxs, dys):
    move(lambda at, n: state_ref[pl.ds(at, n), :], tend_ref, mrow_ref, dx_ref, dy_ref, out_ref,
         dxs, dys, m_ref, north_ref, south_ref)


def sum_kernel(m_ref, whole_ref, l_ref):
    mh, ml = split2(m_ref[...])
    l_ref[...] = dot(mh, whole_ref[...]) + dot(ml, whole_ref[...])


def finish(l_ref, prev_ref, next_ref, in_ref, c_ref):
    halo = jnp.concatenate([prev_ref[...], next_ref[...]], axis=0)
    hh, hl = split2(jnp.transpose(halo)[0:TALL, :])
    total = l_ref[...] + dot(hh, in_ref[...]) + dot(hl, in_ref[...])
    c_ref[...] = total[0:ROWS, :] / total[ROWS:ROWS + 1, :]


def next_kernel(l_ref, prev_ref, next_ref, in_ref, tend_ref, mrow_ref, dx_ref, dy_ref, out_ref,
                m_ref, north_ref, south_ref, cur, dxs, dys):
    finish(l_ref, prev_ref, next_ref, in_ref, cur)
    move(lambda at, n: cur[pl.ds(at, n), :], tend_ref, mrow_ref, dx_ref, dy_ref, out_ref,
         dxs, dys, m_ref, north_ref, south_ref)


def place_kernel(arrived_ref, out_ref):
    rows = arrived_ref[...].reshape(COLS, WIDE)
    turned = jnp.transpose(rows)
    place_col = rows[:, ROWS:ROWS + 1]
    pick = jnp.where(iota((COLS, COLS), 1).astype(F32) == place_col, 1.0, 0.0).astype(BF16)
    hi, lo = split2(turned[0:ROWS, :])
    out_ref[...] = dot(hi, pick) + dot(lo, pick)


def call(kernel, name, out, specs, scratch=()):
    shapes = tuple(jax.ShapeDtypeStruct(s, t) for s, t in out)
    return pl.pallas_call(
        kernel, out_shape=shapes, in_specs=specs, out_specs=(VM,) * len(out),
        scratch_shapes=[pltpu.VMEM(s, t) for s, t in scratch], compiler_params=PARAMS, name=name)


def shifted(array, by):
    length = lax.axis_size(AXES)
    return lax.ppermute(array, AXES, [(i, (i + by) % length) for i in range(length)])


def per_device(state, metric, neighbours, cost_class, batch_slot, level_mix, field_coupling_matrix):
    myself = lax.axis_index(AXES)
    state2 = state.reshape(ROWS, COLS)
    slots = lax.dynamic_slice_in_dim(batch_slot, myself * MEMBERS, MEMBERS, axis=1)
    base = (myself * MEMBERS).astype(jnp.int32).reshape(1)
    dx, dy = (jnp.asarray(a) for a in derivative_blocks())
    send, tend = physics_call(state2, cost_class, slots, level_mix, field_coupling_matrix)
    whole, out_rows, in_rows, mrow = call(
        tables_kernel, "tables",
        [((COLS, COLS), BF16), ((2 * MEMBERS, COLS), BF16), ((2 * MEMBERS, COLS), BF16), ((8, COLS), F32)],
        [SM, VM, VM])(base, neighbours, metric)
    moved_out = [((TALL, COLS), F32), ((MEMBERS, WIDE), F32), ((MEMBERS, WIDE), F32)]
    work = [((ROWS, COLS), F32)] * 2
    arrived = lax.all_to_all(send, AXES, split_axis=0, concat_axis=0, tiled=True)
    m, north, south = call(first_kernel, "first", moved_out, [VM] * 6, work)(
        state2, tend, mrow, dx, dy, out_rows)
    for substep in range(SUBSTEPS):
        from_prev, from_next = shifted(north, 1), shifted(south, -1)
        (total,) = call(sum_kernel, "sum", [((TALL, COLS), F32)], [VM, VM])(m, whole)
        if substep < SUBSTEPS - 1:
            m, north, south = call(next_kernel, "next", moved_out, [VM] * 9, work + work[:1])(
                total, from_prev, from_next, in_rows, tend, mrow, dx, dy, out_rows)
    (state_out,) = call(finish, "finish", [((ROWS, COLS), F32)], [VM] * 4)(total, from_prev, from_next, in_rows)
    (physics_state,) = call(place_kernel, "place", [((ROWS, COLS), F32)], [VM])(arrived)
    return state_out.reshape(state.shape), physics_state.reshape(state.shape)


def solution(mesh):
    split = P(None, AXES)
    whole = P(None, None, AXES)
    return jax.shard_map(
        per_device, mesh=mesh, in_specs=(whole, split, split, split, P(), P(), P()),
        out_specs=(whole, whole), check_vma=False)
```

time: 612 us -> 111 us (0.18); the launches traced: 603 us -> 110 us
  local copies, waits for them, and re-layouts: 367 us -> 5.99 us
  other arithmetic: 87.9 us -> 0 us
  matrix products: 67.5 us -> 0 us
  Pallas kernels: 0 us -> 53.5 us
  waiting for transfers between devices: 33.8 us -> 7.74 us
  loops' own time: 11.4 us -> 0 us
  starting transfers between devices: 33.3 us -> 42 us
    scatter x3 -> x0, local copies, waits for them, and re-layouts: 245 us -> none  [invert(): jnp.zeros((extent,), jnp.int32).at[permutation]]
    gather x47 -> x0, local copies, waits for them, and re-layouts: 73.6 us -> none  [the longest x5 9.85 us: cross_rows(): jnp.take(south_row, local_up, axis=-1)]
    dot_general x46 -> x0, matrix products: 67.5 us -> none  [the longest x20 27.4 us: relax(): jnp.einsum('mx,xaq->maq', field_coupling_matrix, level_blended, precision...]
    pallas_call x0 -> x10, Pallas kernels: none -> 53.5 us  [the longest x1 17.9 us: physics_call(): call(physics_kernel, 'physics', [((COLS // 4, 4, WIDE), F32), ((ROWS, COL...]
    another operation x17 -> x0, other arithmetic: 29.6 us -> none  [the longest x12 22.7 us: combine(): jnp.stack([south_row + south_side, stepped[..., 1, :, :], stepped[..., 2,...]
    ppermute x8 -> x6, waiting for transfers between devices: 27.8 us -> 7.73 us  [shifted(): lax.ppermute(array, AXES, [(i, (i + by) % length) for i in range(length)])]
    select_n x18 -> x0, other arithmetic: 12.1 us -> none  [the longest x4 3.64 us: cross_rows(): jnp.take(north_row, up_list, axis=-1)]
    dynamic_update_slice x20 -> x0, other arithmetic: 11.4 us -> none  [advance_block(): lax.dynamic_update_slice_in_dim(current, relax(segment, active, level_mix...]
  transfers between devices with their start and end apart: 10 -> 7, of which waited for: 7 -> 1; matrix products, arithmetic and copies ran while one was open for 65% -> 0% of each run, Pallas kernels for 0% -> 29%
where the time goes in v1:
time: 111 us; the launch traced here: 110 us
  Pallas kernels  53.5 us (48%)
  starting transfers between devices  42 us (38%)
  waiting for transfers between devices  7.74 us (7%)
  local copies, waits for them, and re-layouts  5.99 us (5%)
    ppermute x6, starting transfers between devices, shifted(): lax.ppermute(array, AXES, [(i, (i + by) % length) for i in range(length)])  21.5 us
    all_to_all x1, starting transfers between devices, per_device(): lax.all_to_all(send, AXES, split_axis=0, concat_axis=0, tiled=True)  20.4 us
    pallas_call x1, Pallas kernels, physics_call(): call(physics_kernel, 'physics', [((COLS // 4, 4, WIDE), F32), ((ROWS, COL...  17.9 us
    pallas_call x2, Pallas kernels, per_device(): call(next_kernel, 'next', moved_out, [VM] * 9, work + work[:1])  10.8 us
    pallas_call x3, Pallas kernels, per_device(): total, = call(sum_kernel, 'sum', [((TALL, COLS), F32)], [VM, VM])(m, whole)  10.7 us
    ppermute x6, waiting for transfers between devices, shifted(): lax.ppermute(array, AXES, [(i, (i + by) % length) for i in range(length)])  7.73 us
    unnamed x16, local copies, waits for them, and re-layouts  5.31 us
    pallas_call x1, Pallas kernels, per_device(): call(first_kernel, 'first', moved_out, [VM] * 6, work)  4.73 us
  transfers between devices with their start and end apart: 7, of which 1 were waited for; matrix products, arithmetic and copies ran while one was open for 0% of the time, Pallas kernels for 29%

profile of v1, /device:TPU:0, one launch (start us, length us, event | category | flops | bytes accessed | tf_op | source)
XLA Modules:
  0.0 109.9 jit_solution(13532683765761737750)
XLA Ops:
  0.6 0.0 copy-start
  0.7 0.9 copy-done
  1.6 0.7 constant_dynamic-slice_fusion.slot_ref
  2.3 17.9 %physics.1 = (f32[128,4,768]{2,1,0:T(4,128)}, f32[720,512]{1,0:T(8,128)}) custom-call(f32[10,10]{1,0:T(8,128)} %fcm_ref.1, f32[720,512]{1,0:T(8,128)} %bitcast.4, s32[16,32]{1,0:T(8,128)} %class_ref.1, s32[16,32]{1,0:T(8,128)} %constant_dynamic-slice_fusion.slot_ref, f32[10,72,72]{2,1,0:T(8,128)} %mix_ref.1), custom_call_target="tpu_custom_call" | custom-call | tf_op jit(solution)/shard_map/physics/pallas_call | solution.py:149
  20.2 20.4 %all-to-all-start = ((f32[128,4,768]{2,1,0:T(4,128)}), f32[128,4,768]{2,1,0:T(4,128)S(1)}, u32[]{:S(2)}, u32[]{:S(2)}) async-start(f32[128,4,768]{2,1,0:T(4,128)} %get-tuple-element.31), calls=%async_computation | async-start | bytes 3145728 | tf_op jit(solution)/shard_map/all_to_all | solution.py:302
  40.6 2.3 %tables.1 = (bf16[512,512]{1,0:T(8,128)(2,1)}, bf16[64,512]{1,0:T(8,128)(2,1)}, bf16[64,512]{1,0:T(8,128)(2,1)}, f32[8,512]{1,0:T(8,128)}) custom-call(s32[1]{0:T(128)} %bitcast.1.base_ref, s32[4,32]{1,0:T(4,128)} %neighbours_ref.1, f32[16,32]{1,0:T(8,128)} %metric_ref.1), custom_call_target="tpu_custom_call" | custom-call | tf_op jit(solution)/shard_map/tables/pallas_call | solution.py:296
  42.9 4.7 %first.1 = (f32[728,512]{1,0:T(8,128)}, f32[32,768]{1,0:T(8,128)}, f32[32,768]{1,0:T(8,128)}) custom-call(f32[720,512]{1,0:T(8,128)} %bitcast.5, f32[720,512]{1,0:T(8,128)} %get-tuple-element.17.tend_ref, f32[8,512]{1,0:T(8,128)} %get-tuple-element.18.mrow_ref, f32[256,256]{1,0:T(8,128)} %constant.21.clone.dx_ref, f32[256,256]{1,0:T(8,128)} %constant.22.clone.dy_ref, ...), custom_call_target="tpu_custom_call" | custom-call | tf_op jit(solution)/shard_map/first/pallas_call | solution.py:303
  47.7 1.1 collective-permute-start
  48.7 6.1 %collective-permute-start.1 = (f32[32,768]{1,0:T(8,128)}, f32[32,768]{1,0:T(8,128)S(1)}, u32[]{:S(2)}, u32[]{:S(2)}) collective-permute-start(f32[32,768]{1,0:T(8,128)} %get-tuple-element.23), channel_id=1, source_target_pairs={{0,127},{1,0},{2,1},{3,2},{4,3},{5,4},{6,5},{7,6},{8,7},{9,8},{10,... | collective-permute-start | bytes 294920 | tf_op jit(solution)/shard_map/ppermute | solution.py:286
  54.8 3.6 %sum.3.l_ref = f32[728,512]{1,0:T(8,128)} custom-call(f32[728,512]{1,0:T(8,128)} %get-tuple-element.20.m_ref, bf16[512,512]{1,0:T(8,128)(2,1)} %get-tuple-element.21.whole_ref), custom_call_target="tpu_custom_call" | custom-call | tf_op jit(solution)/shard_map/sum/pallas_call | solution.py:307
  58.4 7.7 %collective-permute-done.prev_ref = f32[32,768]{1,0:T(8,128)S(1)} collective-permute-done((f32[32,768]{1,0:T(8,128)}, f32[32,768]{1,0:T(8,128)S(1)}, u32[]{:S(2)}, u32[]{:S(2)}) %collective-permute-start) | collective-permute-done | bytes 98336 | tf_op jit(solution)/shard_map/ppermute | solution.py:286
  66.1 0.0 copy-start.6
  66.1 0.0 collective-permute-done.1.next_ref
  66.1 0.0 copy-start.7
  66.1 0.6 copy-done.6
  66.7 0.0 copy-done.7
  66.8 5.4 %next.2 = (f32[728,512]{1,0:T(8,128)}, f32[32,768]{1,0:T(8,128)}, f32[32,768]{1,0:T(8,128)}) custom-call(f32[728,512]{1,0:T(8,128)} %sum.3.l_ref, f32[32,768]{1,0:T(8,128)} %copy-done.6, f32[32,768]{1,0:T(8,128)} %copy-done.7, bf16[64,512]{1,0:T(8,128)(2,1)} %get-tuple-element.24.in_ref, f32[720,512]{1,0:T(8,128)} %get-tuple-element.17.tend_ref, ...), custom_call_target="tpu_custom_call" | custom-call | tf_op jit(solution)/shard_map/next/pallas_call | solution.py:309
  72.2 0.0 collective-permute-start.2
  72.2 7.2 %collective-permute-start.3 = (f32[32,768]{1,0:T(8,128)}, f32[32,768]{1,0:T(8,128)S(1)}, u32[]{:S(2)}, u32[]{:S(2)}) collective-permute-start(f32[32,768]{1,0:T(8,128)} %get-tuple-element.27), channel_id=1, source_target_pairs={{0,127},{1,0},{2,1},{3,2},{4,3},{5,4},{6,5},{7,6},{8,7},{9,8},{10,... | collective-permute-start | bytes 294920 | tf_op jit(solution)/shard_map/ppermute | solution.py:286
  79.3 3.6 %sum.4.l_ref = f32[728,512]{1,0:T(8,128)} custom-call(f32[728,512]{1,0:T(8,128)} %get-tuple-element.25.m_ref, bf16[512,512]{1,0:T(8,128)(2,1)} %get-tuple-element.21.whole_ref), custom_call_target="tpu_custom_call" | custom-call | tf_op jit(solution)/shard_map/sum/pallas_call | solution.py:307
  82.9 0.0 collective-permute-done.2.prev_ref
  82.9 0.0 copy-start.4
  82.9 0.0 collective-permute-done.3.next_ref
  82.9 0.6 copy-done.4
  83.5 0.0 copy-start.5
  83.5 0.6 copy-done.5
  84.2 5.4 %next.3 = (f32[728,512]{1,0:T(8,128)}, f32[32,768]{1,0:T(8,128)}, f32[32,768]{1,0:T(8,128)}) custom-call(f32[728,512]{1,0:T(8,128)} %sum.4.l_ref, f32[32,768]{1,0:T(8,128)} %copy-done.4, f32[32,768]{1,0:T(8,128)} %copy-done.5, bf16[64,512]{1,0:T(8,128)(2,1)} %get-tuple-element.24.in_ref, f32[720,512]{1,0:T(8,128)} %get-tuple-element.17.tend_ref, ...), custom_call_target="tpu_custom_call" | custom-call | tf_op jit(solution)/shard_map/next/pallas_call | solution.py:309
  89.5 0.0 collective-permute-start.4
  89.5 7.2 %collective-permute-start.5 = (f32[32,768]{1,0:T(8,128)}, f32[32,768]{1,0:T(8,128)S(1)}, u32[]{:S(2)}, u32[]{:S(2)}) collective-permute-start(f32[32,768]{1,0:T(8,128)} %get-tuple-element.30), channel_id=1, source_target_pairs={{0,127},{1,0},{2,1},{3,2},{4,3},{5,4},{6,5},{7,6},{8,7},{9,8},{10,... | collective-permute-start | bytes 294920 | tf_op jit(solution)/shard_map/ppermute | solution.py:286
  96.7 3.6 %sum.5.l_ref = f32[728,512]{1,0:T(8,128)} custom-call(f32[728,512]{1,0:T(8,128)} %get-tuple-element.28.m_ref, bf16[512,512]{1,0:T(8,128)(2,1)} %get-tuple-element.21.whole_ref), custom_call_target="tpu_custom_call" | custom-call | tf_op jit(solution)/shard_map/sum/pallas_call | solution.py:307
  100.3 0.0 collective-permute-done.4.prev_ref
  100.3 0.0 copy-start.2
  100.3 0.0 collective-permute-done.5.next_ref
  100.3 0.6 copy-done.2
  100.9 0.0 copy-start.3
  100.9 0.6 copy-done.3
  101.6 3.4 %finish.1 = f32[720,512]{1,0:T(8,128)} custom-call(f32[728,512]{1,0:T(8,128)} %sum.5.l_ref, f32[32,768]{1,0:T(8,128)} %copy-done.2, f32[32,768]{1,0:T(8,128)} %copy-done.3, bf16[64,512]{1,0:T(8,128)(2,1)} %get-tuple-element.24.in_ref), custom_call_target="tpu_custom_call" | custom-call | tf_op jit(solution)/shard_map/finish/pallas_call | solution.py:311
  105.0 0.0 all-to-all-done.arrived_ref
  105.0 0.0 copy-start.1
  105.0 1.2 %copy-done.1 = f32[128,4,768]{2,1,0:T(4,128)} copy-done((f32[128,4,768]{2,1,0:T(4,128)}, f32[128,4,768]{2,1,0:T(4,128)S(1)}, u32[]{:S(2)}) %copy-start.1) | copy-done | bytes 1572888
  106.2 3.7 %place.1 = f32[720,512]{1,0:T(8,128)} custom-call(f32[128,4,768]{2,1,0:T(4,128)} %copy-done.1), custom_call_target="tpu_custom_call" | custom-call | tf_op jit(solution)/shard_map/place/pallas_call | solution.py:312
Async XLA Ops:
  0.6 1.0 copy-start
  20.2 84.8 %all-to-all-start = ((f32[128,4,768]{2,1,0:T(4,128)}), f32[128,4,768]{2,1,0:T(4,128)S(1)}, u32[]{:S(2)}, u32[]{:S(2)}) async-start(f32[128,4,768]{2,1,0:T(4,128)} %get-tuple-element.31), calls=%async_computation | async-start | bytes 3145728 | tf_op jit(solution)/shard_map/all_to_all | solution.py:302
  47.7 18.5 %collective-permute-start = (f32[32,768]{1,0:T(8,128)}, f32[32,768]{1,0:T(8,128)S(1)}, u32[]{:S(2)}, u32[]{:S(2)}) collective-permute-start(f32[32,768]{1,0:T(8,128)} %get-tuple-element.22), channel_id=1, source_target_pairs={{0,1},{1,2},{2,3},{3,4},{4,5},{5,6},{6,7},{7,8},{8,9},{9,10},{10,1... | collective-permute-start | bytes 294920 | tf_op jit(solution)/shard_map/ppermute | solution.py:286
  48.7 17.4 %collective-permute-start.1 = (f32[32,768]{1,0:T(8,128)}, f32[32,768]{1,0:T(8,128)S(1)}, u32[]{:S(2)}, u32[]{:S(2)}) collective-permute-start(f32[32,768]{1,0:T(8,128)} %get-tuple-element.23), channel_id=1, source_target_pairs={{0,127},{1,0},{2,1},{3,2},{4,3},{5,4},{6,5},{7,6},{8,7},{9,8},{10,... | collective-permute-start | bytes 294920 | tf_op jit(solution)/shard_map/ppermute | solution.py:286
  66.1 0.6 copy-start.6
  66.1 0.7 copy-start.7
  72.2 10.7 %collective-permute-start.2 = (f32[32,768]{1,0:T(8,128)}, f32[32,768]{1,0:T(8,128)S(1)}, u32[]{:S(2)}, u32[]{:S(2)}) collective-permute-start(f32[32,768]{1,0:T(8,128)} %get-tuple-element.26), channel_id=1, source_target_pairs={{0,1},{1,2},{2,3},{3,4},{4,5},{5,6},{6,7},{7,8},{8,9},{9,10},{10,1... | collective-permute-start | bytes 294920 | tf_op jit(solution)/shard_map/ppermute | solution.py:286
  72.2 10.7 %collective-permute-start.3 = (f32[32,768]{1,0:T(8,128)}, f32[32,768]{1,0:T(8,128)S(1)}, u32[]{:S(2)}, u32[]{:S(2)}) collective-permute-start(f32[32,768]{1,0:T(8,128)} %get-tuple-element.27), channel_id=1, source_target_pairs={{0,127},{1,0},{2,1},{3,2},{4,3},{5,4},{6,5},{7,6},{8,7},{9,8},{10,... | collective-permute-start | bytes 294920 | tf_op jit(solution)/shard_map/ppermute | solution.py:286
  82.9 0.6 copy-start.4
  83.5 0.6 copy-start.5
  89.5 10.7 %collective-permute-start.4 = (f32[32,768]{1,0:T(8,128)}, f32[32,768]{1,0:T(8,128)S(1)}, u32[]{:S(2)}, u32[]{:S(2)}) collective-permute-start(f32[32,768]{1,0:T(8,128)} %get-tuple-element.29), channel_id=1, source_target_pairs={{0,1},{1,2},{2,3},{3,4},{4,5},{5,6},{6,7},{7,8},{8,9},{9,10},{10,1... | collective-permute-start | bytes 294920 | tf_op jit(solution)/shard_map/ppermute | solution.py:286
  89.5 10.7 %collective-permute-start.5 = (f32[32,768]{1,0:T(8,128)}, f32[32,768]{1,0:T(8,128)S(1)}, u32[]{:S(2)}, u32[]{:S(2)}) collective-permute-start(f32[32,768]{1,0:T(8,128)} %get-tuple-element.30), channel_id=1, source_target_pairs={{0,127},{1,0},{2,1},{3,2},{4,3},{5,4},{6,5},{7,6},{8,7},{9,8},{10,... | collective-permute-start | bytes 294920 | tf_op jit(solution)/shard_map/ppermute | solution.py:286
  100.3 0.6 copy-start.2
  100.9 0.6 copy-start.3
  105.0 1.2 %copy-start.1 = (f32[128,4,768]{2,1,0:T(4,128)}, f32[128,4,768]{2,1,0:T(4,128)S(1)}, u32[]{:S(2)}) copy-start(f32[128,4,768]{2,1,0:T(4,128)S(1)} %all-to-all-done.arrived_ref) | copy-start | bytes 4718596

commit v2 on v1

v2 whole, which is shorter than its diff:
```python
import jax
import jax.numpy as jnp
import numpy as np
from jax import lax
from jax.experimental import pallas as pl
from jax.experimental.pallas import tpu as pltpu
from jax.sharding import PartitionSpec as P


AXES = ("elem", "face")
F32 = jnp.float32
BF16 = jnp.bfloat16
HIGHEST = lax.Precision.HIGHEST
FIELDS, LEVELS, SUBSTEPS = 10, 72, 3
ROWS, COLS, MEMBERS, WIDE = 720, 512, 32, 768
TALL = ROWS + 8
PHYSICS_RATE, TIME_STEP = 0.1, 0.02
VM = pl.BlockSpec(memory_space=pltpu.VMEM)
HB = pl.BlockSpec(memory_space=pltpu.HBM)
SM = pl.BlockSpec(memory_space=pltpu.SMEM)
PARAMS = pltpu.CompilerParams(vmem_limit_bytes=30 << 20)


def gll_matrix():
    nodes = np.array([-1.0, -1.0 / np.sqrt(5.0), 1.0 / np.sqrt(5.0), 1.0])
    derivative = np.zeros((4, 4))
    for i in range(4):
        for j in range(4):
            others = [k for k in range(4) if k != j]
            if i == j:
                derivative[i, j] = sum(1.0 / (nodes[j] - nodes[k]) for k in others)
            else:
                top = np.prod([nodes[i] - nodes[k] for k in others if k != i])
                derivative[i, j] = top / np.prod([nodes[j] - nodes[k] for k in others])
    return derivative


def derivative_blocks():
    d = gll_matrix()
    across = np.kron(np.eye(4), d).astype(np.float32).T
    upward = np.kron(d, np.eye(4)).astype(np.float32).T
    return np.kron(np.eye(16), across).astype(np.float32), np.kron(np.eye(16), upward).astype(np.float32)


def split2(v):
    hi = v.astype(BF16)
    return hi, (v - hi.astype(F32)).astype(BF16)


def dot(a, b):
    return jnp.dot(a, b, preferred_element_type=F32)


def dot_nt(a, b):
    return lax.dot_general(a, b, (((1,), (1,)), ((), ())), preferred_element_type=F32)


def iota(shape, dim):
    return lax.broadcasted_iota(jnp.int32, shape, dim)


def expand_points(table):
    spread = jnp.where(iota((32, COLS), 1) // 16 == iota((32, COLS), 0), 1.0, 0.0)
    wide = jnp.dot(table, spread, precision=HIGHEST, preferred_element_type=F32)
    wide = jnp.where(iota((16, COLS), 1) % 16 == iota((16, COLS), 0), wide, 0.0)
    return jnp.sum(wide, axis=0, keepdims=True)


def as_column(row):
    return jnp.transpose(jnp.broadcast_to(row, (8, COLS)))[:, 0:1]


def rank_row(key_row):
    key_col = as_column(key_row)
    return jnp.sum(jnp.where(key_col < key_row, 1.0, 0.0), axis=0, keepdims=True)


def physics_kernel(me_ref, fcm_hbm, state_hbm, class_hbm, slots_hbm, mix_hbm, metric_hbm, nb_hbm, dx_hbm, dy_hbm,
                   send_hbm, tend_ref, m_ref, mine_a_ref, mine_b_ref, out_ref, in_ref, mrow_ref,
                   k32, kk, state_ref, class_ref, slot_ref, mix_ref, x0, yy, tt, rr, qa, qb, send_ref,
                   metric_ref, nb_ref, dx_ref, dy_ref, dxs, dys, fcm_ref, sems):
    me = me_ref[0]
    load_slots = pltpu.make_async_copy(
        slots_hbm.at[:, pl.ds(pl.multiple_of(me // 4 * 128, 128), 128)], slot_ref, sems.at[0])
    load_state = pltpu.make_async_copy(state_hbm, state_ref, sems.at[1])
    load_class = pltpu.make_async_copy(class_hbm, class_ref, sems.at[2])
    load_mix = pltpu.make_async_copy(mix_hbm, mix_ref, sems.at[3])
    load_fcm = pltpu.make_async_copy(fcm_hbm, fcm_ref, sems.at[4])
    load_metric = pltpu.make_async_copy(metric_hbm, metric_ref, sems.at[5])
    load_nb = pltpu.make_async_copy(nb_hbm, nb_ref, sems.at[6])
    load_dx = pltpu.make_async_copy(dx_hbm, dx_ref, sems.at[7])
    load_dy = pltpu.make_async_copy(dy_hbm, dy_ref, sems.at[8])
    load_fcm.start()
    load_mix.start()
    load_slots.start()
    load_class.start()
    load_state.start()
    load_nb.start()
    load_metric.start()
    load_dx.start()
    load_dy.start()
    rep = jnp.where(
        (iota((LEVELS, WIDE), 1) % LEVELS == iota((LEVELS, WIDE), 0)) & (iota((LEVELS, WIDE), 1) < ROWS), 1.0, 0.0
    ).astype(BF16)
    lane = iota((1, WIDE), 1)
    load_fcm.wait()
    load_mix.wait()
    for f in range(FIELDS):
        crow = jnp.zeros((1, WIDE), F32)
        for g in range(FIELDS):
            crow = jnp.where((lane >= LEVELS * g) & (lane < LEVELS * g + LEVELS), PHYSICS_RATE * fcm_ref[g, f], crow)
        mh, ml = split2(jnp.transpose(mix_ref[f]))
        k32[LEVELS * f:LEVELS * f + LEVELS, :] = (dot(mh, rep) + dot(ml, rep)) * crow
    k32[ROWS:WIDE, :] = jnp.zeros((WIDE - ROWS, WIDE), F32)
    hi, lo = split2(k32[...])
    kk[0:WIDE, :] = hi
    kk[WIDE:, :] = lo
    load_slots.wait()
    load_class.wait()
    part = me % 4
    own = slot_ref[:, 0:MEMBERS]
    for j in range(1, 4):
        own = jnp.where(part == j, slot_ref[:, MEMBERS * j:MEMBERS * j + MEMBERS], own)
    cls = expand_points(class_ref[...].astype(F32))
    slot = expand_points(own.astype(F32))
    col = iota((1, COLS), 1).astype(F32)
    crank = rank_row((4.0 - cls) * COLS + col)
    srank = rank_row(slot)
    place = slot - jnp.floor(slot * (1.0 / COLS)) * COLS
    perm = jnp.where(iota((COLS, COLS), 0).astype(F32) == crank, 1.0, 0.0).astype(BF16)
    extra = jnp.where(iota((128, COLS), 0) == 0, place, 0.0)
    eh, el = split2(extra)
    x0[:, ROWS:WIDE] = (dot_nt(perm, eh) + dot_nt(perm, el))[:, 0:WIDE - ROWS]
    rh, rl = split2(jnp.broadcast_to(srank, (16, COLS)))
    srank_sorted = (dot_nt(rh, perm) + dot_nt(rl, perm))[0:1, :]
    n1 = jnp.sum(jnp.where(cls > 1.5, 1, 0))
    n2 = jnp.sum(jnp.where(cls > 2.5, 1, 0))
    n3 = jnp.sum(jnp.where(cls > 3.5, 1, 0))
    load_state.wait()
    sh, sl = split2(state_ref[...])
    x0[:, 0:ROWS] = dot_nt(perm, sh) + dot_nt(perm, sl)
    xh, xl = split2(x0[...])
    xhh = jnp.concatenate([xh, xh], axis=1)
    for n in range(0, WIDE, 256):
        at = slice(n, n + 256)
        y = (dot(xl, kk[0:WIDE, at]) + dot(xhh, kk[:, at])) * (1.0 / PHYSICS_RATE)
        yy[:, at] = y
        t = jnp.tanh(y)
        tt[:, at] = t
        q = t.astype(BF16)
        rr[:, at] = t - q.astype(F32)
        qa[:, at] = q

    def step(rows, live, old, new, low):
        deep = 2 * WIDE if low else WIDE
        n, wd, at, br = 0, WIDE, slice(0, WIDE), 64
        acc = dot(old[0:rows, 0:deep], kk[0:deep, :])
        for b in range(0, rows, br):
            part = acc[b:b + br]
            rb = slice(b, b + br)
            y = yy[rb, at] + part
            yy[rb, at] = y
            t = jnp.tanh(y)
            if b + 64 >= rows:
                tt[rb, at] += jnp.where(iota((br, wd), 0) + b < live, t, 0.0)
            else:
                tt[rb, at] += t
            s = t + rr[rb, at]
            q = s.astype(BF16)
            rr[rb, at] = s - q.astype(F32)
            new[rb, at] = q
            if not low:
                new[rb, WIDE + n:WIDE + n + wd] = (old[rb, at].astype(F32) + q.astype(F32)).astype(BF16)

    def sweep(k, old, new, low):
        live = jnp.where(k < 4, COLS, jnp.where(k < 8, n1, jnp.where(k < 12, n2, jnp.where(k < 16, n3, 0))))
        which = (live + 63) // 64
        for i in range(8):
            @pl.when(which == i + 1)
            def _():
                step(64 * (i + 1), live, old, new, low)

    def two_sweeps(j, _):
        sweep(2 * j + 1, qa, qb, False)
        sweep(2 * j + 2, qb, qa, True)
        return 0

    lax.fori_loop(0, 8, two_sweeps, 0)
    q_send = jnp.where(iota((COLS, COLS), 0).astype(F32) == srank_sorted, 1.0, 0.0).astype(BF16)
    fh, fl = split2(x0[...] + PHYSICS_RATE * tt[...])
    out = dot(q_send, fh) + dot(q_send, fl)
    send_ref[...] = out.reshape(COLS // 4, 4, WIDE)
    store_send = pltpu.make_async_copy(send_ref, send_hbm, sems.at[9])
    store_send.start()
    th, tl = split2(jnp.transpose(tt[...])[0:ROWS, :] * (PHYSICS_RATE / SUBSTEPS))
    tend_ref[...] = dot(th, perm) + dot(tl, perm)
    load_nb.wait()
    load_metric.wait()
    tables(me * MEMBERS, nb_ref, metric_ref, out_ref, in_ref, mrow_ref)
    load_dx.wait()
    load_dy.wait()
    move(lambda at, n: state_ref[pl.ds(at, n), :], tend_ref, mrow_ref, dx_ref, dy_ref, out_ref,
         dxs, dys, m_ref, mine_a_ref, mine_b_ref)
    store_send.wait()


HALO = ((MEMBERS, WIDE), F32)
MOVED = ((TALL, COLS), F32)
GRID = ((ROWS, COLS), F32)


def physics_call(state2, cost_class, batch_slot, level_mix, fcm, me, metric, neighbours, dx, dy):
    work = [((WIDE, WIDE), F32), ((2 * WIDE, WIDE), BF16), GRID, ((16, MEMBERS), jnp.int32),
            ((16, 128), jnp.int32), ((FIELDS, LEVELS, LEVELS), F32)]
    work += [((COLS, WIDE), F32)] * 4 + [((COLS, WIDE), BF16), ((COLS, 2 * WIDE), BF16), ((COLS // 4, 4, WIDE), F32)]
    work += [((16, MEMBERS), F32), ((4, MEMBERS), jnp.int32), ((256, 256), F32), ((256, 256), F32), GRID, GRID]
    out = [((COLS // 4, 4, WIDE), F32), GRID, MOVED, HALO, HALO, ((2 * MEMBERS, COLS), BF16),
           ((2 * MEMBERS, COLS), BF16), ((8, COLS), F32)]
    shapes = tuple((pltpu.HBM if k < 1 else pltpu.VMEM)(s, t) for k, (s, t) in enumerate(out))
    return pl.pallas_call(
        physics_kernel, out_shape=shapes, in_specs=[SM] + [HB] * 9, out_specs=(HB,) + (VM,) * 7,
        scratch_shapes=[pltpu.VMEM(s, t) for s, t in work]
        + [pltpu.SMEM((FIELDS, FIELDS), F32), pltpu.SemaphoreType.DMA((10,))],
        compiler_params=PARAMS, name="physics",
    )(me, *in_hbm(fcm, state2, cost_class, batch_slot, level_mix, metric, neighbours, dx, dy))


def element_tables(neighbours_ref, base):
    local = neighbours_ref[...] - base
    outside = (local < 0) | (local >= MEMBERS)
    wide = jnp.concatenate([local.astype(F32), jnp.where(outside, 1.0, 0.0)], axis=0)
    spread = jnp.where(iota((MEMBERS, COLS), 1) // 16 == iota((MEMBERS, COLS), 0), 1.0, 0.0)
    by_column = jnp.dot(wide, spread, precision=HIGHEST, preferred_element_type=F32)
    return wide, by_column, spread


def east_west(by_column):
    col = iota((1, COLS), 1)
    ix, line = col % 4, (col % 16) // 4 * 4
    source = jnp.where(ix == 3, 16.0 * by_column[0:1] + line.astype(F32),
                       jnp.where(ix == 0, 16.0 * by_column[1:2] + (line + 3).astype(F32), -1.0))
    row = iota((COLS, COLS), 0)
    hit = (row.astype(F32) == source) | (row == iota((COLS, COLS), 1))
    return jnp.where(hit, 1.0, 0.0).astype(BF16)


def north_south(by_column):
    col = iota((1, COLS), 1)
    ix, iy = (col % 4).astype(F32), (col % 16) // 4
    north = jnp.where(by_column[6:7] > 0.5, -1.0, 16.0 * by_column[2:3] + ix)
    south = jnp.where(by_column[7:8] > 0.5, -1.0, 16.0 * by_column[3:4] + 12.0 + ix)
    source = jnp.where(iy == 3, north, jnp.where(iy == 0, south, -1.0))
    row = iota((COLS, COLS), 0)
    hit = (row.astype(F32) == source) | (row == iota((COLS, COLS), 1))
    return jnp.where(hit, 1.0, 0.0).astype(BF16)


def rank_among(key, member, spread):
    key8 = jnp.broadcast_to(jnp.where(member > 0.5, key, 1e9), (8, MEMBERS))
    key_col = jnp.transpose(key8)[:, 0:1]
    rank = jnp.sum(jnp.where(key_col < key, 1.0, 0.0), axis=0, keepdims=True)
    return jnp.dot(jnp.broadcast_to(rank, (8, MEMBERS)), spread, precision=HIGHEST,
                   preferred_element_type=F32)[0:1]


def halo_targets(wide, by_column, spread):
    col = iota((1, COLS), 1)
    ix, iy = (col % 4).astype(F32), (col % 16) // 4
    own = iota((1, MEMBERS), 1).astype(F32)
    up, down = by_column[6:7] > 0.5, by_column[7:8] > 0.5
    to_north = jnp.where((iy == 3) & up, 8.0 * ix + rank_among(own, wide[6:7], spread), -1.0)
    to_south = jnp.where((iy == 0) & down, 8.0 * ix + rank_among(own, wide[7:8], spread), -1.0)
    from_south = jnp.where((iy == 0) & down, 8.0 * ix + rank_among(wide[3:4], wide[7:8], spread), -1.0)
    from_north = jnp.where((iy == 3) & up, 8.0 * ix + rank_among(wide[2:3], wide[6:7], spread), -1.0)
    return to_north, to_south, from_south, from_north


def two_selections(first, second):
    row = iota((2 * MEMBERS, COLS), 0).astype(F32)
    hit = (row == first) | ((row - MEMBERS == second) & (second > -0.5))
    return jnp.where(hit, 1.0, 0.0).astype(BF16)


def whole_kernel(base_ref, neighbours_ref, whole_ref):
    base = base_ref[0]
    _, by_column, _ = element_tables(neighbours_ref, base)
    whole_ref[...] = dot(east_west(by_column), north_south(by_column)).astype(BF16)


def tables(base, neighbours_ref, metric_ref, out_ref, in_ref, mrow_ref):
    wide, by_column, spread = element_tables(neighbours_ref, base)
    to_north, to_south, from_south, from_north = halo_targets(wide, by_column, spread)
    odd = base // MEMBERS % 2 == 1
    sent = two_selections(jnp.where(odd, to_south, to_north), jnp.where(odd, to_north, to_south))
    out_ref[...] = dot_nt(sent, east_west(by_column)).astype(BF16)
    in_ref[...] = two_selections(jnp.where(odd, from_south, from_north), jnp.where(odd, from_north, from_south))
    mrow_ref[...] = jnp.broadcast_to(expand_points(metric_ref[...]), (8, COLS))


def move(read, tend_ref, mrow_ref, dx_ref, dy_ref, out_ref, dxs, dys, m_ref, north_ref, south_ref):
    vh, vl = split2(read(0, ROWS))
    for half in (0, 256):
        at = slice(half, half + 256)
        for d_ref, acc in ((dx_ref, dxs), (dy_ref, dys)):
            dh, dl = split2(d_ref[...])
            acc[:, at] = dot(vh[:, at], dh) + dot(vl[:, at], dh) + dot(vh[:, at], dl)
    metric = mrow_ref[0:1, :]
    u, v = read(0, LEVELS), read(LEVELS, LEVELS)
    for f in range(FIELDS):
        at = pl.ds(LEVELS * f, LEVELS)
        rate = u * dxs[at, :] + v * dys[at, :]
        m_ref[at, :] = metric * ((read(LEVELS * f, LEVELS) - TIME_STEP * rate) + tend_ref[at, :])
    m_ref[ROWS:TALL, :] = mrow_ref[...]
    mh, ml = split2(m_ref[...])
    halo = dot_nt(out_ref[...], mh) + dot_nt(out_ref[...], ml)
    north_ref[:, 0:TALL] = halo[0:MEMBERS]
    south_ref[:, 0:TALL] = halo[MEMBERS:]
    north_ref[:, TALL:WIDE] = jnp.zeros((MEMBERS, WIDE - TALL), F32)
    south_ref[:, TALL:WIDE] = jnp.zeros((MEMBERS, WIDE - TALL), F32)


def sum_kernel(m_ref, whole_ref, l_ref):
    mh, ml = split2(m_ref[...])
    l_ref[...] = dot(mh, whole_ref[...]) + dot(ml, whole_ref[...])


def finish(l_ref, prev_ref, next_ref, in_ref, c_ref, done=lambda at: None):
    halo = jnp.concatenate([prev_ref[...], next_ref[...]], axis=0)
    hh, hl = split2(jnp.transpose(halo)[0:TALL, :])
    mass = l_ref[ROWS:TALL, :] + dot(hh[ROWS:TALL], in_ref[...]) + dot(hl[ROWS:TALL], in_ref[...])
    inverse = 1.0 / mass[0:1, :]
    for at in CHUNKS:
        c_ref[at, :] = (l_ref[at, :] + dot(hh[at], in_ref[...]) + dot(hl[at], in_ref[...])) * inverse
        done(at)


CHUNKS = tuple(slice(a, a + 144) for a in range(0, ROWS, 144))


def storing(body, source, target, sems):
    copies = []

    def done(at):
        copies.append(pltpu.make_async_copy(source.at[at], target.at[at], sems.at[len(copies)]))
        copies[-1].start()

    body(done)
    for copy in copies:
        copy.wait()


def finish_kernel(l_ref, prev_ref, next_ref, in_ref, out_hbm, cur, sems):
    storing(lambda done: finish(l_ref, prev_ref, next_ref, in_ref, cur, done), cur, out_hbm, sems)


def next_kernel(l_ref, prev_ref, next_ref, in_ref, tend_ref, mrow_ref, dx_ref, dy_ref, out_ref,
                m_ref, north_ref, south_ref, cur, dxs, dys):
    finish(l_ref, prev_ref, next_ref, in_ref, cur)
    move(lambda at, n: cur[pl.ds(at, n), :], tend_ref, mrow_ref, dx_ref, dy_ref, out_ref,
         dxs, dys, m_ref, north_ref, south_ref)


def place_kernel(arrived_ref, out_hbm, cur, sems):
    rows = arrived_ref[...].reshape(COLS, WIDE)
    place_col = rows[:, ROWS:ROWS + 1]
    pick = jnp.where(iota((COLS, COLS), 1).astype(F32) == place_col, 1.0, 0.0).astype(BF16)
    hi, lo = split2(jnp.transpose(rows)[0:ROWS, :])

    def body(done):
        for at in CHUNKS:
            cur[at, :] = dot(hi[at], pick) + dot(lo[at], pick)
            done(at)

    storing(body, cur, out_hbm, sems)


def call(kernel, out, specs, scratch=(), semaphores=0, hbm_out=0):
    shapes = tuple((pltpu.HBM if k < hbm_out else pltpu.VMEM)(s, t) for k, (s, t) in enumerate(out))
    work = [pltpu.VMEM(s, t) for s, t in scratch]
    if semaphores:
        work.append(pltpu.SemaphoreType.DMA((semaphores,)))
    return pl.pallas_call(
        kernel, out_shape=shapes, in_specs=specs, out_specs=(HB,) * hbm_out + (VM,) * (len(out) - hbm_out),
        scratch_shapes=work, compiler_params=PARAMS)


def in_hbm(*arrays):
    return tuple(pltpu.with_memory_space_constraint(a, pltpu.HBM) for a in arrays)


def swapped(array, first):
    length = lax.axis_size(AXES)
    low = range(0 if first else 1, length, 2)
    pairs = [(i, (i + 1) % length) for i in low]
    return lax.ppermute(array, AXES, pairs + [(j, i) for i, j in pairs])


def step(state, metric, neighbours, cost_class, batch_slot, level_mix, field_coupling_matrix):
    me = lax.axis_index(AXES).astype(jnp.int32).reshape(1)
    base = me * MEMBERS
    state2 = state.reshape(ROWS, COLS)
    dx, dy = (jnp.asarray(a) for a in derivative_blocks())
    send, tend, m, mine_a, mine_b, out_rows, in_rows, mrow = physics_call(
        state2, cost_class, batch_slot, level_mix, field_coupling_matrix, me, metric, neighbours, dx, dy)
    (whole,) = call(whole_kernel, [((COLS, COLS), BF16)], [SM, VM])(base, neighbours)
    arrived = lax.all_to_all(send, AXES, split_axis=0, concat_axis=0, tiled=True)
    for substep in range(SUBSTEPS):
        theirs_b = swapped(mine_b, False)
        theirs_a = swapped(mine_a, True)
        (total,) = call(sum_kernel, [MOVED], [VM, VM])(m, whole)
        if substep < SUBSTEPS - 1:
            m, mine_a, mine_b = call(next_kernel, [MOVED, HALO, HALO], [VM] * 9, [GRID] * 3)(
                total, theirs_a, theirs_b, in_rows, tend, mrow, dx, dy, out_rows)
    (physics_state,) = call(place_kernel, [GRID], [VM], [GRID], len(CHUNKS), 1)(arrived)
    (state_out,) = call(finish_kernel, [GRID], [VM] * 4, [GRID], len(CHUNKS), 1)(
        total, theirs_a, theirs_b, in_rows)
    return state_out.reshape(state.shape), physics_state.reshape(state.shape)


def solution(mesh):
    split = P(None, AXES)
    whole = P(None, None, AXES)
    return jax.shard_map(
        step, mesh=mesh, in_specs=(whole, split, split, split, P(), P(), P()),
        out_specs=(whole, whole), check_vma=False)
```

time: 111 us -> 92.3 us (0.83)
  Pallas kernels: 53.5 us -> 29.5 us
  waiting for transfers between devices: 7.74 us -> 27.6 us
  starting transfers between devices: 42 us -> 31.6 us
  local copies, waits for them, and re-layouts: 5.99 us -> 2.51 us
    pallas_call x10 -> x9, Pallas kernels: 53.5 us -> 29.5 us  [the longest x1 17.7 us: physics_call(): pl.pallas_call(physics_kernel, out_shape=shapes, in_specs=[SM] + [HB] * 9...]
    ppermute x6, waiting for transfers between devices: 7.73 us -> 27.6 us  [swapped(): return lax.ppermute(array, AXES, pairs + [(j, i) for i, j in pairs])]
    ppermute x6, starting transfers between devices: 21.5 us -> 12.3 us  [swapped(): return lax.ppermute(array, AXES, pairs + [(j, i) for i, j in pairs])]
    unnamed x16 -> x10, local copies, waits for them, and re-layouts: 5.31 us -> 2.51 us
    all_to_all x1, starting transfers between devices: 20.4 us -> 19.3 us  [step(): lax.all_to_all(send, AXES, split_axis=0, concat_axis=0, tiled=True)]
  transfers between devices with their start and end apart: 7 -> 7, of which waited for: 1 -> 6; matrix products, arithmetic and copies ran while one was open for 0% -> 0% of each run, Pallas kernels for 29% -> 11%
where the time goes in v2:
time: 92.3 us; the launch traced here: 92.1 us
  starting transfers between devices  31.6 us (34%)
  Pallas kernels  29.5 us (32%)
  waiting for transfers between devices  27.6 us (30%)
  local copies, waits for them, and re-layouts  2.51 us (3%)
    ppermute x6, waiting for transfers between devices, swapped(): return lax.ppermute(array, AXES, pairs + [(j, i) for i, j in pairs])  27.6 us
    all_to_all x1, starting transfers between devices, step(): lax.all_to_all(send, AXES, split_axis=0, concat_axis=0, tiled=True)  19.3 us
    pallas_call x1, Pallas kernels, physics_call(): pl.pallas_call(physics_kernel, out_shape=shapes, in_specs=[SM] + [HB] * 9...  17.7 us
    ppermute x6, starting transfers between devices, swapped(): return lax.ppermute(array, AXES, pairs + [(j, i) for i, j in pairs])  12.3 us
    pallas_call x2, Pallas kernels, step(): call(next_kernel, [MOVED, HALO, HALO], [VM] * 9, [GRID] * 3)  4.86 us
    pallas_call x3, Pallas kernels, step(): total, = call(sum_kernel, [MOVED], [VM, VM])(m, whole)  2.86 us
    unnamed x10, local copies, waits for them, and re-layouts  2.51 us
    pallas_call x1, Pallas kernels, step(): call(place_kernel, [GRID], [VM], [GRID], len(CHUNKS), 1)(arrived)  1.95 us
  transfers between devices with their start and end apart: 7, of which 6 were waited for; matrix products, arithmetic and copies ran while one was open for 0% of the time, Pallas kernels for 11%

profile of v2, /device:TPU:0, one launch (start us, length us, event | category | flops | bytes accessed | tf_op | source)
XLA Modules:
  0.0 92.1 jit_solution(7834563422791578394)
XLA Ops:
  0.6 17.7 %physics.1 = (f32[128,4,768]{2,1,0:T(4,128)}, f32[720,512]{1,0:T(8,128)S(1)}, f32[728,512]{1,0:T(8,128)S(1)}, f32[32,768]{1,0:T(8,128)S(1)}, f32[32,768]{1,0:T(8...) custom-call(s32[1]{0:T(128)} %bitcast.me_ref, f32[10,10]{1,0:T(8,128)} %fcm_hbm.1, ...), custom_call_target="tpu_custom_call" | custom-call | tf_op jit(solution)/shard_map/physics/pallas_call | solution.py:220
  18.3 0.0 copy-start.2
  18.4 1.1 %copy-done.2 = f32[728,512]{1,0:T(8,128)} copy-done((f32[728,512]{1,0:T(8,128)}, f32[728,512]{1,0:T(8,128)S(1)}, u32[]{:S(2)}) %copy-start.2) | copy-done | bytes 1490968
  19.5 0.0 copy-start.4
  19.5 19.3 %all-to-all-start = ((f32[128,4,768]{2,1,0:T(4,128)}), f32[128,4,768]{2,1,0:T(4,128)S(1)}, u32[]{:S(2)}, u32[]{:S(2)}) async-start(f32[128,4,768]{2,1,0:T(4,128)} %get-tuple-element.29), calls=%async_computation | async-start | bytes 3145728 | tf_op jit(solution)/shard_map/all_to_all | solution.py:406
  38.8 1.2 %collective-permute-start = (f32[32,768]{1,0:T(8,128)S(1)}, f32[32,768]{1,0:T(8,128)S(1)}, u32[]{:S(2)}, u32[]{:S(2)}) collective-permute-start(f32[32,768]{1,0:T(8,128)S(1)} %get-tuple-element.17), channel_id=1, source_target_pairs={{0,1},{2,3},{4,5},{6,7},{8,9},{10,11},{12,13},{14,15},{16,17},{18,... | collective-permute-start | bytes 294920 | tf_op jit(solution)/shard_map/ppermute | solution.py:395
  39.9 6.3 %collective-permute-start.1 = (f32[32,768]{1,0:T(8,128)S(1)}, f32[32,768]{1,0:T(8,128)S(1)}, u32[]{:S(2)}, u32[]{:S(2)}) collective-permute-start(f32[32,768]{1,0:T(8,128)S(1)} %get-tuple-element.18), channel_id=1, source_target_pairs={{1,2},{3,4},{5,6},{7,8},{9,10},{11,12},{13,14},{15,16},{17,18},{19... | collective-permute-start | bytes 294920 | tf_op jit(solution)/shard_map/ppermute | solution.py:395
  46.2 0.0 copy-done.4
  46.2 0.6 shard_map.104.whole_ref
  46.9 0.0 copy-start.3
  46.9 1.4 %copy-done.3 = f32[728,512]{1,0:T(8,128)S(1)} copy-done((f32[728,512]{1,0:T(8,128)S(1)}, f32[728,512]{1,0:T(8,128)}, u32[]{:S(2)}) %copy-start.3) | copy-done | bytes 1490968
  48.2 0.0 copy-start
  48.2 0.0 copy-start.1
  48.2 0.9 %shard_map.105.l_ref = f32[728,512]{1,0:T(8,128)S(1)} custom-call(f32[728,512]{1,0:T(8,128)S(1)} %copy-done.3, bf16[512,512]{1,0:T(8,128)(2,1)S(1)} %shard_map.104.whole_ref), custom_call_target="tpu_custom_call" | custom-call | tf_op jit(solution)/shard_map/pallas_call | solution.py:410
  49.2 8.9 %collective-permute-done.prev_ref = f32[32,768]{1,0:T(8,128)S(1)} collective-permute-done((f32[32,768]{1,0:T(8,128)S(1)}, f32[32,768]{1,0:T(8,128)S(1)}, u32[]{:S(2)}, u32[]{:S(2)}) %collective-permute-start) | collective-permute-done | bytes 98336 | tf_op jit(solution)/shard_map/ppermute | solution.py:395
  58.0 6.3 %collective-permute-done.1.next_ref = f32[32,768]{1,0:T(8,128)S(1)} collective-permute-done((f32[32,768]{1,0:T(8,128)S(1)}, f32[32,768]{1,0:T(8,128)S(1)}, u32[]{:S(2)}, u32[]{:S(2)}) %collective-permute-start.1) | collective-permute-done | bytes 98336 | tf_op jit(solution)/shard_map/ppermute | solution.py:395
  64.3 0.0 copy-done
  64.3 0.0 copy-done.1
  64.3 2.4 %shard_map.106 = (f32[728,512]{1,0:T(8,128)S(1)}, f32[32,768]{1,0:T(8,128)S(1)}, f32[32,768]{1,0:T(8,128)S(1)}) custom-call(f32[728,512]{1,0:T(8,128)S(1)} %shard_map.105.l_ref, f32[32,768]{1,0:T(8,128)S(1)} %collective-permute-done.prev_ref, f32[32,768]{1,0:T(8,128)S(1)} %collective-permute-done.1.next_ref, bf16[64,512]{1,0:T(8,128)(2,1)S(1)} %get-tuple-element.19.in_ref, ...), custom_call_target="tpu_custom_call" | custom-call | tf_op jit(solution)/shard_map/pallas_call | solution.py:412
  66.8 0.1 collective-permute-start.2
  66.8 2.4 %collective-permute-start.3 = (f32[32,768]{1,0:T(8,128)S(1)}, f32[32,768]{1,0:T(8,128)S(1)}, u32[]{:S(2)}, u32[]{:S(2)}) collective-permute-start(f32[32,768]{1,0:T(8,128)S(1)} %get-tuple-element.25), channel_id=1, source_target_pairs={{1,2},{3,4},{5,6},{7,8},{9,10},{11,12},{13,14},{15,16},{17,18},{19... | collective-permute-start | bytes 294920 | tf_op jit(solution)/shard_map/ppermute | solution.py:395
  69.2 1.0 %shard_map.107.l_ref = f32[728,512]{1,0:T(8,128)S(1)} custom-call(f32[728,512]{1,0:T(8,128)S(1)} %get-tuple-element.23.m_ref, bf16[512,512]{1,0:T(8,128)(2,1)S(1)} %shard_map.104.whole_ref), custom_call_target="tpu_custom_call" | custom-call | tf_op jit(solution)/shard_map/pallas_call | solution.py:410
  70.2 1.3 %collective-permute-done.2.prev_ref = f32[32,768]{1,0:T(8,128)S(1)} collective-permute-done((f32[32,768]{1,0:T(8,128)S(1)}, f32[32,768]{1,0:T(8,128)S(1)}, u32[]{:S(2)}, u32[]{:S(2)}) %collective-permute-start.2) | collective-permute-done | bytes 98336 | tf_op jit(solution)/shard_map/ppermute | solution.py:395
  71.4 4.9 %collective-permute-done.3.next_ref = f32[32,768]{1,0:T(8,128)S(1)} collective-permute-done((f32[32,768]{1,0:T(8,128)S(1)}, f32[32,768]{1,0:T(8,128)S(1)}, u32[]{:S(2)}, u32[]{:S(2)}) %collective-permute-start.3) | collective-permute-done | bytes 98336 | tf_op jit(solution)/shard_map/ppermute | solution.py:395
  76.4 2.4 %shard_map.108 = (f32[728,512]{1,0:T(8,128)S(1)}, f32[32,768]{1,0:T(8,128)S(1)}, f32[32,768]{1,0:T(8,128)S(1)}) custom-call(f32[728,512]{1,0:T(8,128)S(1)} %shard_map.107.l_ref, f32[32,768]{1,0:T(8,128)S(1)} %collective-permute-done.2.prev_ref, f32[32,768]{1,0:T(8,128)S(1)} %collective-permute-done.3.next_ref, bf16[64,512]{1,0:T(8,128)(2,1)S(1)} %get-tuple-element.19.in_ref, ...), custom_call_target="tpu_custom_call" | custom-call | tf_op jit(solution)/shard_map/pallas_call | solution.py:412
  78.8 0.1 collective-permute-start.4
  78.9 2.4 %collective-permute-start.5 = (f32[32,768]{1,0:T(8,128)S(1)}, f32[32,768]{1,0:T(8,128)S(1)}, u32[]{:S(2)}, u32[]{:S(2)}) collective-permute-start(f32[32,768]{1,0:T(8,128)S(1)} %get-tuple-element.28), channel_id=1, source_target_pairs={{1,2},{3,4},{5,6},{7,8},{9,10},{11,12},{13,14},{15,16},{17,18},{19... | collective-permute-start | bytes 294920 | tf_op jit(solution)/shard_map/ppermute | solution.py:395
  81.3 1.0 %shard_map.109.l_ref = f32[728,512]{1,0:T(8,128)S(1)} custom-call(f32[728,512]{1,0:T(8,128)S(1)} %get-tuple-element.26.m_ref, bf16[512,512]{1,0:T(8,128)(2,1)S(1)} %shard_map.104.whole_ref), custom_call_target="tpu_custom_call" | custom-call | tf_op jit(solution)/shard_map/pallas_call | solution.py:410
  82.2 1.3 %collective-permute-done.4.prev_ref = f32[32,768]{1,0:T(8,128)S(1)} collective-permute-done((f32[32,768]{1,0:T(8,128)S(1)}, f32[32,768]{1,0:T(8,128)S(1)}, u32[]{:S(2)}, u32[]{:S(2)}) %collective-permute-start.4) | collective-permute-done | bytes 98336 | tf_op jit(solution)/shard_map/ppermute | solution.py:395
  83.5 4.9 %collective-permute-done.5.next_ref = f32[32,768]{1,0:T(8,128)S(1)} collective-permute-done((f32[32,768]{1,0:T(8,128)S(1)}, f32[32,768]{1,0:T(8,128)S(1)}, u32[]{:S(2)}, u32[]{:S(2)}) %collective-permute-start.5) | collective-permute-done | bytes 98336 | tf_op jit(solution)/shard_map/ppermute | solution.py:395
  88.5 1.5 %shard_map.110 = f32[720,512]{1,0:T(8,128)} custom-call(f32[728,512]{1,0:T(8,128)S(1)} %shard_map.109.l_ref, f32[32,768]{1,0:T(8,128)S(1)} %collective-permute-done.4.prev_ref, f32[32,768]{1,0:T(8,128)S(1)} %collective-permute-done.5.next_ref, bf16[64,512]{1,0:T(8,128)(2,1)S(1)} %get-tuple-element.19.in_ref), custom_call_target="tpu_custom_call" | custom-call | tf_op jit(solution)/shard_map/pallas_call | solution.py:415
  90.0 0.0 all-to-all-done.arrived_ref
  90.0 1.9 %shard_map.111 = f32[720,512]{1,0:T(8,128)} custom-call(f32[128,4,768]{2,1,0:T(4,128)S(1)} %all-to-all-done.arrived_ref), custom_call_target="tpu_custom_call" | custom-call | tf_op jit(solution)/shard_map/pallas_call | solution.py:414
Async XLA Ops:
  18.3 1.1 %copy-start.2 = (f32[728,512]{1,0:T(8,128)}, f32[728,512]{1,0:T(8,128)S(1)}, u32[]{:S(2)}) copy-start(f32[728,512]{1,0:T(8,128)S(1)} %get-tuple-element.16.m_ref) | copy-start | bytes 4472836
  19.5 26.7 %copy-start.4 = (s32[4,32]{1,0:T(4,128)S(1)}, s32[4,32]{1,0:T(4,128)}, u32[]{:S(2)}) copy-start(s32[4,32]{1,0:T(4,128)} %neighbours_ref.1) | copy-start | bytes 1540
  19.5 70.5 %all-to-all-start = ((f32[128,4,768]{2,1,0:T(4,128)}), f32[128,4,768]{2,1,0:T(4,128)S(1)}, u32[]{:S(2)}, u32[]{:S(2)}) async-start(f32[128,4,768]{2,1,0:T(4,128)} %get-tuple-element.29), calls=%async_computation | async-start | bytes 3145728 | tf_op jit(solution)/shard_map/all_to_all | solution.py:406
  38.8 19.3 %collective-permute-start = (f32[32,768]{1,0:T(8,128)S(1)}, f32[32,768]{1,0:T(8,128)S(1)}, u32[]{:S(2)}, u32[]{:S(2)}) collective-permute-start(f32[32,768]{1,0:T(8,128)S(1)} %get-tuple-element.17), channel_id=1, source_target_pairs={{0,1},{2,3},{4,5},{6,7},{8,9},{10,11},{12,13},{14,15},{16,17},{18,... | collective-permute-start | bytes 294920 | tf_op jit(solution)/shard_map/ppermute | solution.py:395
  39.9 24.4 %collective-permute-start.1 = (f32[32,768]{1,0:T(8,128)S(1)}, f32[32,768]{1,0:T(8,128)S(1)}, u32[]{:S(2)}, u32[]{:S(2)}) collective-permute-start(f32[32,768]{1,0:T(8,128)S(1)} %get-tuple-element.18), channel_id=1, source_target_pairs={{1,2},{3,4},{5,6},{7,8},{9,10},{11,12},{13,14},{15,16},{17,18},{19... | collective-permute-start | bytes 294920 | tf_op jit(solution)/shard_map/ppermute | solution.py:395
  46.9 1.4 %copy-start.3 = (f32[728,512]{1,0:T(8,128)S(1)}, f32[728,512]{1,0:T(8,128)}, u32[]{:S(2)}) copy-start(f32[728,512]{1,0:T(8,128)} %copy-done.2) | copy-start | bytes 4472836
  48.2 16.1 %copy-start = (f32[256,256]{1,0:T(8,128)S(1)}, f32[256,256]{1,0:T(8,128)}, u32[]{:S(2)}) copy-start(f32[256,256]{1,0:T(8,128)} %constant.18.clone.dy_hbm.dy_ref) | copy-start | bytes 786436
  48.2 16.1 %copy-start.1 = (f32[256,256]{1,0:T(8,128)S(1)}, f32[256,256]{1,0:T(8,128)}, u32[]{:S(2)}) copy-start(f32[256,256]{1,0:T(8,128)} %constant.17.clone.dx_hbm.dx_ref) | copy-start | bytes 786436
  66.8 4.7 %collective-permute-start.2 = (f32[32,768]{1,0:T(8,128)S(1)}, f32[32,768]{1,0:T(8,128)S(1)}, u32[]{:S(2)}, u32[]{:S(2)}) collective-permute-start(f32[32,768]{1,0:T(8,128)S(1)} %get-tuple-element.24), channel_id=1, source_target_pairs={{0,1},{2,3},{4,5},{6,7},{8,9},{10,11},{12,13},{14,15},{16,17},{18,... | collective-permute-start | bytes 294920 | tf_op jit(solution)/shard_map/ppermute | solution.py:395
  66.8 9.6 %collective-permute-start.3 = (f32[32,768]{1,0:T(8,128)S(1)}, f32[32,768]{1,0:T(8,128)S(1)}, u32[]{:S(2)}, u32[]{:S(2)}) collective-permute-start(f32[32,768]{1,0:T(8,128)S(1)} %get-tuple-element.25), channel_id=1, source_target_pairs={{1,2},{3,4},{5,6},{7,8},{9,10},{11,12},{13,14},{15,16},{17,18},{19... | collective-permute-start | bytes 294920 | tf_op jit(solution)/shard_map/ppermute | solution.py:395
  78.8 4.7 %collective-permute-start.4 = (f32[32,768]{1,0:T(8,128)S(1)}, f32[32,768]{1,0:T(8,128)S(1)}, u32[]{:S(2)}, u32[]{:S(2)}) collective-permute-start(f32[32,768]{1,0:T(8,128)S(1)} %get-tuple-element.27), channel_id=1, source_target_pairs={{0,1},{2,3},{4,5},{6,7},{8,9},{10,11},{12,13},{14,15},{16,17},{18,... | collective-permute-start | bytes 294920 | tf_op jit(solution)/shard_map/ppermute | solution.py:395
  78.9 9.6 %collective-permute-start.5 = (f32[32,768]{1,0:T(8,128)S(1)}, f32[32,768]{1,0:T(8,128)S(1)}, u32[]{:S(2)}, u32[]{:S(2)}) collective-permute-start(f32[32,768]{1,0:T(8,128)S(1)} %get-tuple-element.28), channel_id=1, source_target_pairs={{1,2},{3,4},{5,6},{7,8},{9,10},{11,12},{13,14},{15,16},{17,18},{19... | collective-permute-start | bytes 294920 | tf_op jit(solution)/shard_map/ppermute | solution.py:395

commit v3 on v2

--- a/solution.py
+++ b/solution.py
@@ -75,30 +75,81 @@
     return jnp.sum(jnp.where(key_col < key_row, 1.0, 0.0), axis=0, keepdims=True)
 
 
-def physics_kernel(me_ref, fcm_hbm, state_hbm, class_hbm, slots_hbm, mix_hbm, metric_hbm, nb_hbm, dx_hbm, dy_hbm,
-                   send_hbm, tend_ref, m_ref, mine_a_ref, mine_b_ref, out_ref, in_ref, mrow_ref,
-                   k32, kk, state_ref, class_ref, slot_ref, mix_ref, x0, yy, tt, rr, qa, qb, send_ref,
-                   metric_ref, nb_ref, dx_ref, dy_ref, dxs, dys, fcm_ref, sems):
+HALF = COLS // 2
+SIZES = (32, 96, 128, 160, HALF)
+
+
+def all_started(*copies):
+    for copy in copies:
+        copy.start()
+    return copies
+
+
+def copies(pairs, sems):
+    return all_started(*(pltpu.make_async_copy(a, b, sems.at[k]) for k, (a, b) in enumerate(pairs)))
+
+
+def sweeps(x_ref, kk, yy, tt, rr, qa, qb, cls, lanes):
+    n1, n2, n3 = (jnp.sum(jnp.where(lanes & (cls > j + 0.5), 1, 0)) for j in (1, 2, 3))
+    xh, xl = split2(x_ref[...])
+    xhh = jnp.concatenate([xh, xh], axis=1)
+    y = (dot(xl, kk[0:WIDE, :]) + dot(xhh, kk[...])) * (1.0 / PHYSICS_RATE)
+    yy[...] = y
+    t = jnp.tanh(y)
+    tt[...] = t
+    q = t.astype(BF16)
+    rr[...] = t - q.astype(F32)
+    qa[...] = q
+
+    def step(rows, live, old, new, low):
+        deep = 2 * WIDE if low else WIDE
+        acc = dot(old[0:rows, 0:deep], kk[0:deep, :])
+        for b in range(0, rows, 32):
+            rb = slice(b, b + 32)
+            y = yy[rb, :] + acc[rb]
+            yy[rb, :] = y
+            t = jnp.tanh(y)
+            if b + 32 > max((0,) + tuple(n for n in SIZES if n < rows)):
+                tt[rb, :] += jnp.where(iota((32, WIDE), 0) + b < live, t, 0.0)
+            else:
+                tt[rb, :] += t
+            s = t + rr[rb, :]
+            q = s.astype(BF16)
+            rr[rb, :] = s - q.astype(F32)
+            new[rb, 0:WIDE] = q
+            if not low:
+                new[rb, WIDE:] = (old[rb, :].astype(F32) + q.astype(F32)).astype(BF16)
+
+    def sweep(k, old, new, low):
+        live = jnp.where(k < 4, HALF, jnp.where(k < 8, n1, jnp.where(k < 12, n2, jnp.where(k < 16, n3, 0))))
+        for below, rows in zip((0,) + SIZES, SIZES):
+            @pl.when((live > below) & (live <= rows))
+            def _():
+                step(rows, live, old, new, low)
+
+    def two_sweeps(j, _):
+        sweep(2 * j + 1, qa, qb, False)
+        sweep(2 * j + 2, qb, qa, True)
+        return 0
+
+    lax.fori_loop(0, 8, two_sweeps, 0)
+
+
+def sent(x, ranks):
+    pick = jnp.where(iota((HALF, HALF), 0).astype(F32) == ranks, 1.0, 0.0).astype(BF16)
+    hi, lo = split2(x)
+    return (dot(pick, hi) + dot(pick, lo)).reshape(HALF // 2, 2, WIDE)
+
+
+def part1_kernel(me_ref, fcm_hbm, state_hbm, class_hbm, slots_hbm, mix_hbm,
+                 send_hbm, x2_hbm, kk_hbm, perm_hbm, t1_hbm, info_hbm,
+                 k32, kk, state_ref, class_ref, slot_ref, mix_ref, x0, yy, tt, rr, qa, qb, send_ref, pp, info,
+                 fcm_ref, sems, out_sems):
     me = me_ref[0]
-    load_slots = pltpu.make_async_copy(
-        slots_hbm.at[:, pl.ds(pl.multiple_of(me // 4 * 128, 128), 128)], slot_ref, sems.at[0])
-    load_state = pltpu.make_async_copy(state_hbm, state_ref, sems.at[1])
-    load_class = pltpu.make_async_copy(class_hbm, class_ref, sems.at[2])
-    load_mix = pltpu.make_async_copy(mix_hbm, mix_ref, sems.at[3])
-    load_fcm = pltpu.make_async_copy(fcm_hbm, fcm_ref, sems.at[4])
-    load_metric = pltpu.make_async_copy(metric_hbm, metric_ref, sems.at[5])
-    load_nb = pltpu.make_async_copy(nb_hbm, nb_ref, sems.at[6])
-    load_dx = pltpu.make_async_copy(dx_hbm, dx_ref, sems.at[7])
-    load_dy = pltpu.make_async_copy(dy_hbm, dy_ref, sems.at[8])
-    load_fcm.start()
-    load_mix.start()
-    load_slots.start()
-    load_class.start()
-    load_state.start()
-    load_nb.start()
-    load_metric.start()
-    load_dx.start()
-    load_dy.start()
+    load_fcm, load_mix, load_slots, load_class, load_state = copies(
+        ((fcm_hbm, fcm_ref), (mix_hbm, mix_ref),
+         (slots_hbm.at[:, pl.ds(pl.multiple_of(me // 4 * 128, 128), 128)], slot_ref),
+         (class_hbm, class_ref), (state_hbm, state_ref)), sems)
     rep = jnp.where(
         (iota((LEVELS, WIDE), 1) % LEVELS == iota((LEVELS, WIDE), 0)) & (iota((LEVELS, WIDE), 1) < ROWS), 1.0, 0.0
     ).astype(BF16)
@@ -115,6 +166,8 @@
     hi, lo = split2(k32[...])
     kk[0:WIDE, :] = hi
     kk[WIDE:, :] = lo
+    store_kk = pltpu.make_async_copy(kk, kk_hbm, out_sems.at[0])
+    store_kk.start()
     load_slots.wait()
     load_class.wait()
     part = me % 4
@@ -124,81 +177,59 @@
     cls = expand_points(class_ref[...].astype(F32))
     slot = expand_points(own.astype(F32))
     col = iota((1, COLS), 1).astype(F32)
-    crank = rank_row((4.0 - cls) * COLS + col)
     srank = rank_row(slot)
+    batch = jnp.floor(srank * 0.25)
+    within = srank - 4.0 * batch
+    late = within < 1.5
+    hrank = 2.0 * batch + jnp.where(late, within, within - 2.0)
+    crank = rank_row(jnp.where(late, 4.0 * COLS, 0.0) + (4.0 - cls) * COLS + col)
     place = slot - jnp.floor(slot * (1.0 / COLS)) * COLS
     perm = jnp.where(iota((COLS, COLS), 0).astype(F32) == crank, 1.0, 0.0).astype(BF16)
+    pp[...] = perm
+    store_perm = pltpu.make_async_copy(pp, perm_hbm, out_sems.at[1])
+    store_perm.start()
+    row16 = iota((16, COLS), 0)
+    notes = jnp.where(row16 == 0, hrank, jnp.where(row16 == 1, cls, 0.0)).astype(BF16)
+    info[...] = dot_nt(notes, perm)[0:8, :]
+    store_info = pltpu.make_async_copy(info, info_hbm, out_sems.at[2])
+    store_info.start()
     extra = jnp.where(iota((128, COLS), 0) == 0, place, 0.0)
     eh, el = split2(extra)
     x0[:, ROWS:WIDE] = (dot_nt(perm, eh) + dot_nt(perm, el))[:, 0:WIDE - ROWS]
-    rh, rl = split2(jnp.broadcast_to(srank, (16, COLS)))
-    srank_sorted = (dot_nt(rh, perm) + dot_nt(rl, perm))[0:1, :]
-    n1 = jnp.sum(jnp.where(cls > 1.5, 1, 0))
-    n2 = jnp.sum(jnp.where(cls > 2.5, 1, 0))
-    n3 = jnp.sum(jnp.where(cls > 3.5, 1, 0))
     load_state.wait()
     sh, sl = split2(state_ref[...])
     x0[:, 0:ROWS] = dot_nt(perm, sh) + dot_nt(perm, sl)
-    xh, xl = split2(x0[...])
-    xhh = jnp.concatenate([xh, xh], axis=1)
-    for n in range(0, WIDE, 256):
-        at = slice(n, n + 256)
-        y = (dot(xl, kk[0:WIDE, at]) + dot(xhh, kk[:, at])) * (1.0 / PHYSICS_RATE)
-        yy[:, at] = y
-        t = jnp.tanh(y)
-        tt[:, at] = t
-        q = t.astype(BF16)
-        rr[:, at] = t - q.astype(F32)
-        qa[:, at] = q
-
-    def step(rows, live, old, new, low):
-        deep = 2 * WIDE if low else WIDE
-        n, wd, at, br = 0, WIDE, slice(0, WIDE), 64
-        acc = dot(old[0:rows, 0:deep], kk[0:deep, :])
-        for b in range(0, rows, br):
-            part = acc[b:b + br]
-            rb = slice(b, b + br)
-            y = yy[rb, at] + part
-            yy[rb, at] = y
-            t = jnp.tanh(y)
-            if b + 64 >= rows:
-                tt[rb, at] += jnp.where(iota((br, wd), 0) + b < live, t, 0.0)
-            else:
-                tt[rb, at] += t
-            s = t + rr[rb, at]
-            q = s.astype(BF16)
-            rr[rb, at] = s - q.astype(F32)
-            new[rb, at] = q
-            if not low:
-                new[rb, WIDE + n:WIDE + n + wd] = (old[rb, at].astype(F32) + q.astype(F32)).astype(BF16)
-
-    def sweep(k, old, new, low):
-        live = jnp.where(k < 4, COLS, jnp.where(k < 8, n1, jnp.where(k < 12, n2, jnp.where(k < 16, n3, 0))))
-        which = (live + 63) // 64
-        for i in range(8):
-            @pl.when(which == i + 1)
-            def _():
-                step(64 * (i + 1), live, old, new, low)
-
-    def two_sweeps(j, _):
-        sweep(2 * j + 1, qa, qb, False)
-        sweep(2 * j + 2, qb, qa, True)
-        return 0
-
-    lax.fori_loop(0, 8, two_sweeps, 0)
-    q_send = jnp.where(iota((COLS, COLS), 0).astype(F32) == srank_sorted, 1.0, 0.0).astype(BF16)
-    fh, fl = split2(x0[...] + PHYSICS_RATE * tt[...])
-    out = dot(q_send, fh) + dot(q_send, fl)
-    send_ref[...] = out.reshape(COLS // 4, 4, WIDE)
-    store_send = pltpu.make_async_copy(send_ref, send_hbm, sems.at[9])
+    store_x2 = pltpu.make_async_copy(x0.at[HALF:COLS], x2_hbm, out_sems.at[3])
+    store_x2.start()
+    sweeps(x0.at[0:HALF], kk, yy, tt, rr, qa, qb, info[1:2, :], iota((1, COLS), 1) < HALF)
+    store_t1 = pltpu.make_async_copy(tt, t1_hbm, out_sems.at[4])
+    store_t1.start()
+    send_ref[...] = sent(x0[0:HALF, :] + PHYSICS_RATE * tt[...], info[0:1, 0:HALF])
+    pltpu.sync_copy(send_ref, send_hbm)
+    for store in (store_kk, store_perm, store_info, store_x2, store_t1):
+        store.wait()
+
+
+def part2_kernel(me_ref, x2_hbm, kk_hbm, perm_hbm, t1_hbm, info_hbm, state_hbm, metric_hbm, nb_hbm, dx_hbm, dy_hbm,
+                 send_hbm, tend_ref, m_ref, mine_a_ref, mine_b_ref, out_ref, in_ref, mrow_ref,
+                 x2, kk, pp, t1, info, state_ref, metric_ref, nb_ref, dx_ref, dy_ref,
+                 yy, tt, rr, qa, qb, send_ref, dxs, dys, sems):
+    me = me_ref[0]
+    loads = copies(((info_hbm, info), (x2_hbm, x2), (kk_hbm, kk), (perm_hbm, pp), (t1_hbm, t1), (state_hbm, state_ref),
+                    (metric_hbm, metric_ref), (nb_hbm, nb_ref), (dx_hbm, dx_ref), (dy_hbm, dy_ref)), sems)
+    for load in loads[0:3]:
+        load.wait()
+    sweeps(x2, kk, yy, tt, rr, qa, qb, info[1:2, :], iota((1, COLS), 1) >= HALF)
+    send_ref[...] = sent(x2[...] + PHYSICS_RATE * tt[...], info[0:1, HALF:COLS])
+    store_send = pltpu.make_async_copy(send_ref, send_hbm, sems.at[10])
     store_send.start()
-    th, tl = split2(jnp.transpose(tt[...])[0:ROWS, :] * (PHYSICS_RATE / SUBSTEPS))
-    tend_ref[...] = dot(th, perm) + dot(tl, perm)
-    load_nb.wait()
-    load_metric.wait()
+    for load in loads[3:]:
+        load.wait()
+    ah, al = split2(jnp.transpose(t1[...])[0:ROWS, :] * (PHYSICS_RATE / SUBSTEPS))
+    bh, bl = split2(jnp.transpose(tt[...])[0:ROWS, :] * (PHYSICS_RATE / SUBSTEPS))
+    first, second = pp[0:HALF, :], pp[HALF:COLS, :]
+    tend_ref[...] = (dot(ah, first) + dot(al, first)) + (dot(bh, second) + dot(bl, second))
     tables(me * MEMBERS, nb_ref, metric_ref, out_ref, in_ref, mrow_ref)
-    load_dx.wait()
-    load_dy.wait()
     move(lambda at, n: state_ref[pl.ds(at, n), :], tend_ref, mrow_ref, dx_ref, dy_ref, out_ref,
          dxs, dys, m_ref, mine_a_ref, mine_b_ref)
     store_send.wait()
@@ -207,22 +238,12 @@
 HALO = ((MEMBERS, WIDE), F32)
 MOVED = ((TALL, COLS), F32)
 GRID = ((ROWS, COLS), F32)
-
-
-def physics_call(state2, cost_class, batch_slot, level_mix, fcm, me, metric, neighbours, dx, dy):
-    work = [((WIDE, WIDE), F32), ((2 * WIDE, WIDE), BF16), GRID, ((16, MEMBERS), jnp.int32),
-            ((16, 128), jnp.int32), ((FIELDS, LEVELS, LEVELS), F32)]
-    work += [((COLS, WIDE), F32)] * 4 + [((COLS, WIDE), BF16), ((COLS, 2 * WIDE), BF16), ((COLS // 4, 4, WIDE), F32)]
-    work += [((16, MEMBERS), F32), ((4, MEMBERS), jnp.int32), ((256, 256), F32), ((256, 256), F32), GRID, GRID]
-    out = [((COLS // 4, 4, WIDE), F32), GRID, MOVED, HALO, HALO, ((2 * MEMBERS, COLS), BF16),
-           ((2 * MEMBERS, COLS), BF16), ((8, COLS), F32)]
-    shapes = tuple((pltpu.HBM if k < 1 else pltpu.VMEM)(s, t) for k, (s, t) in enumerate(out))
-    return pl.pallas_call(
-        physics_kernel, out_shape=shapes, in_specs=[SM] + [HB] * 9, out_specs=(HB,) + (VM,) * 7,
-        scratch_shapes=[pltpu.VMEM(s, t) for s, t in work]
-        + [pltpu.SMEM((FIELDS, FIELDS), F32), pltpu.SemaphoreType.DMA((10,))],
-        compiler_params=PARAMS, name="physics",
-    )(me, *in_hbm(fcm, state2, cost_class, batch_slot, level_mix, metric, neighbours, dx, dy))
+SEND = ((HALF // 2, 2, WIDE), F32)
+HALF_X = ((HALF, WIDE), F32)
+OPERATOR = ((2 * WIDE, WIDE), BF16)
+PERM = ((COLS, COLS), BF16)
+INFO = ((8, COLS), F32)
+SWEEP = [HALF_X, HALF_X, HALF_X, ((HALF, WIDE), BF16), ((HALF, 2 * WIDE), BF16), SEND]
 
 
 def element_tables(neighbours_ref, base):
@@ -360,8 +381,8 @@
          dxs, dys, m_ref, north_ref, south_ref)
 
 
-def place_kernel(arrived_ref, out_hbm, cur, sems):
-    rows = arrived_ref[...].reshape(COLS, WIDE)
+def place_kernel(first_ref, second_ref, out_hbm, cur, sems):
+    rows = jnp.concatenate([first_ref[...].reshape(HALF, WIDE), second_ref[...].reshape(HALF, WIDE)], axis=0)
     place_col = rows[:, ROWS:ROWS + 1]
     pick = jnp.where(iota((COLS, COLS), 1).astype(F32) == place_col, 1.0, 0.0).astype(BF16)
     hi, lo = split2(jnp.transpose(rows)[0:ROWS, :])
@@ -374,11 +395,10 @@
     storing(body, cur, out_hbm, sems)
 
 
-def call(kernel, out, specs, scratch=(), semaphores=0, hbm_out=0):
+def call(kernel, out, specs, scratch=(), semaphores=(), hbm_out=0, smem=()):
     shapes = tuple((pltpu.HBM if k < hbm_out else pltpu.VMEM)(s, t) for k, (s, t) in enumerate(out))
-    work = [pltpu.VMEM(s, t) for s, t in scratch]
-    if semaphores:
-        work.append(pltpu.SemaphoreType.DMA((semaphores,)))
+    work = [pltpu.VMEM(s, t) for s, t in scratch] + [pltpu.SMEM(s, t) for s, t in smem]
+    work += [pltpu.SemaphoreType.DMA((n,)) for n in semaphores]
     return pl.pallas_call(
         kernel, out_shape=shapes, in_specs=specs, out_specs=(HB,) * hbm_out + (VM,) * (len(out) - hbm_out),
         scratch_shapes=work, compiler_params=PARAMS)
@@ -400,10 +420,23 @@
     base = me * MEMBERS
     state2 = state.reshape(ROWS, COLS)
     dx, dy = (jnp.asarray(a) for a in derivative_blocks())
-    send, tend, m, mine_a, mine_b, out_rows, in_rows, mrow = physics_call(
-        state2, cost_class, batch_slot, level_mix, field_coupling_matrix, me, metric, neighbours, dx, dy)
+    send1, *kept = call(
+        part1_kernel, [SEND, HALF_X, OPERATOR, PERM, HALF_X, INFO], [SM] + [HB] * 5,
+        [((WIDE, WIDE), F32), OPERATOR, GRID, ((16, MEMBERS), jnp.int32), ((16, 128), jnp.int32),
+         ((FIELDS, LEVELS, LEVELS), F32), ((COLS, WIDE), F32)] + SWEEP + [PERM, INFO],
+        [5, 5], 6, [((FIELDS, FIELDS), F32)],
+    )(me, *in_hbm(field_coupling_matrix, state2, cost_class, batch_slot, level_mix))
+    arrived1 = lax.all_to_all(send1, AXES, split_axis=0, concat_axis=0, tiled=True)
+    send2, tend, m, mine_a, mine_b, out_rows, in_rows, mrow = call(
+        part2_kernel,
+        [SEND, GRID, MOVED, HALO, HALO, ((2 * MEMBERS, COLS), BF16), ((2 * MEMBERS, COLS), BF16), INFO],
+        [SM] + [HB] * 10,
+        [HALF_X, OPERATOR, PERM, HALF_X, INFO, GRID, ((16, MEMBERS), F32), ((4, MEMBERS), jnp.int32),
+         ((256, 256), F32), ((256, 256), F32)] + SWEEP + [GRID, GRID],
+        [11], 1,
+    )(me, *in_hbm(*kept, state2, metric, neighbours, dx, dy))
     (whole,) = call(whole_kernel, [((COLS, COLS), BF16)], [SM, VM])(base, neighbours)
-    arrived = lax.all_to_all(send, AXES, split_axis=0, concat_axis=0, tiled=True)
+    arrived2 = lax.all_to_all(send2, AXES, split_axis=0, concat_axis=0, tiled=True)
     for substep in range(SUBSTEPS):
         theirs_b = swapped(mine_b, False)
         theirs_a = swapped(mine_a, True)
@@ -411,8 +444,8 @@
         if substep < SUBSTEPS - 1:
             m, mine_a, mine_b = call(next_kernel, [MOVED, HALO, HALO], [VM] * 9, [GRID] * 3)(
                 total, theirs_a, theirs_b, in_rows, tend, mrow, dx, dy, out_rows)
-    (physics_state,) = call(place_kernel, [GRID], [VM], [GRID], len(CHUNKS), 1)(arrived)
-    (state_out,) = call(finish_kernel, [GRID], [VM] * 4, [GRID], len(CHUNKS), 1)(
+    (physics_state,) = call(place_kernel, [GRID], [VM, VM], [GRID], [len(CHUNKS)], 1)(arrived1, arrived2)
+    (state_out,) = call(finish_kernel, [GRID], [VM] * 4, [GRID], [len(CHUNKS)], 1)(
         total, theirs_a, theirs_b, in_rows)
     return state_out.reshape(state.shape), physics_state.reshape(state.shape)
 

time: 92.3 us -> 108 us (1.17)
  blocking collectives: 0 us -> 36.4 us
  starting transfers between devices: 31.6 us -> 17.1 us
  waiting for transfers between devices: 27.6 us -> 19.2 us
  Pallas kernels: 29.5 us -> 31.9 us
    all_to_all x0 -> x1, blocking collectives: none -> 36.4 us  [step(): lax.all_to_all(send2, AXES, split_axis=0, concat_axis=0, tiled=True)]
    all_to_all x1, starting transfers between devices: 19.3 us -> 4.83 us  [step(): lax.all_to_all(send1, AXES, split_axis=0, concat_axis=0, tiled=True)]
    ppermute x6, waiting for transfers between devices: 27.6 us -> 19.2 us  [swapped(): return lax.ppermute(array, AXES, pairs + [(j, i) for i, j in pairs])]
    pallas_call x3 -> x4, Pallas kernels: 21.1 us -> 23.5 us  [the longest x1 10.3 us: step(): call(part1_kernel, [SEND, HALF_X, OPERATOR, PERM, HALF_X, INFO], [SM] + [...]
  transfers between devices with their start and end apart: 7 -> 7, of which waited for: 6 -> 6; matrix products, arithmetic and copies ran while one was open for 0% -> 0% of each run, Pallas kernels for 11% -> 9%
where the time goes in v3:
time: 108 us
  blocking collectives  36.4 us (34%)
  Pallas kernels  31.9 us (30%)
  waiting for transfers between devices  19.2 us (18%)
  starting transfers between devices  17.1 us (16%)
  local copies, waits for them, and re-layouts  2.5 us (2%)
    all_to_all x1, blocking collectives, step(): lax.all_to_all(send2, AXES, split_axis=0, concat_axis=0, tiled=True)  36.4 us
    ppermute x6, waiting for transfers between devices, swapped(): return lax.ppermute(array, AXES, pairs + [(j, i) for i, j in pairs])  19.2 us
    ppermute x6, starting transfers between devices, swapped(): return lax.ppermute(array, AXES, pairs + [(j, i) for i, j in pairs])  12.3 us
    pallas_call x1, Pallas kernels, step(): call(part1_kernel, [SEND, HALF_X, OPERATOR, PERM, HALF_X, INFO], [SM] + [...  10.3 us
    pallas_call x1, Pallas kernels, step(): call(part2_kernel, [SEND, GRID, MOVED, HALO, HALO, ((2 * MEMBERS, COLS),...  9.86 us
    pallas_call x2, Pallas kernels, step(): call(next_kernel, [MOVED, HALO, HALO], [VM] * 9, [GRID] * 3)  4.86 us
    all_to_all x1, starting transfers between devices, step(): lax.all_to_all(send1, AXES, split_axis=0, concat_axis=0, tiled=True)  4.83 us
    pallas_call x3, Pallas kernels, step(): total, = call(sum_kernel, [MOVED], [VM, VM])(m, whole)  2.87 us
  transfers between devices with their start and end apart: 7, of which 6 were waited for; matrix products, arithmetic and copies ran while one was open for 0% of the time, Pallas kernels for 9%

profile of v3, /device:TPU:0, one launch (start us, length us, event | category | flops | bytes accessed | tf_op | source)
XLA Modules:
  0.0 108.0 jit_solution(17165892048036436065)
XLA Ops:
  0.6 10.3 %shard_map.104 = (f32[128,2,768]{2,1,0:T(2,128)}, f32[256,768]{1,0:T(8,128)}, bf16[1536,768]{1,0:T(8,128)(2,1)}, bf16[512,512]{1,0:T(8,128)(2,1)}, f32[256,768]{1,0:T(8,128)}, /*index=5*/f32[8,512]{1,0:T(8,128)}) custom-call(s32[1]{0:T(128)} %bitcast.me_ref, f32[10,10]{1,0:T(8,128)} %fcm_hbm.1, f32[720,512]{1,0:T(8,128)} %bitcast.4, s32[16,32]{1,0:T(8,128)} %class_hbm.1, ...), custom_call_target="tpu_custom_call" | custom-call | tf_op jit(solution)/shard_map/pallas_call | solution.py:423
  10.9 9.9 %shard_map.105 = (f32[128,2,768]{2,1,0:T(2,128)}, f32[720,512]{1,0:T(8,128)S(1)}, f32[728,512]{1,0:T(8,128)S(1)}, f32[32,768]{1,0:T(8,128)S(1)}, f32[32,768]{1,0...) custom-call(s32[1]{0:T(128)} %bitcast.me_ref, ...), custom_call_target="tpu_custom_call" | custom-call | tf_op jit(solution)/shard_map/pallas_call | solution.py:430
  20.8 0.0 copy-start.2
  20.8 1.1 %copy-done.2 = f32[728,512]{1,0:T(8,128)} copy-done((f32[728,512]{1,0:T(8,128)}, f32[728,512]{1,0:T(8,128)S(1)}, u32[]{:S(2)}) %copy-start.2) | copy-done | bytes 1490968
  21.9 0.0 copy-start.4
  21.9 36.4 %all_to_all.10.second_ref = f32[128,2,768]{2,1,0:T(2,128)S(1)} all-to-all(f32[128,2,768]{2,1,0:T(2,128)} %get-tuple-element.41), channel_id=1, replica_groups=mesh['elem'=32,'face'=4] {'elem','face'}, dimensions={0} | all-to-all | bytes 1572864 | tf_op jit(solution)/shard_map/all_to_all | solution.py:439
  58.3 4.8 %all-to-all-start = ((f32[128,2,768]{2,1,0:T(2,128)}), f32[128,2,768]{2,1,0:T(2,128)S(1)}, u32[]{:S(2)}, u32[]{:S(2)}) async-start(f32[128,2,768]{2,1,0:T(2,128)} %get-tuple-element.40), calls=%async_computation | async-start | bytes 1572864 | tf_op jit(solution)/shard_map/all_to_all | solution.py:429
  63.2 1.2 %collective-permute-start = (f32[32,768]{1,0:T(8,128)S(1)}, f32[32,768]{1,0:T(8,128)S(1)}, u32[]{:S(2)}, u32[]{:S(2)}) collective-permute-start(f32[32,768]{1,0:T(8,128)S(1)} %get-tuple-element.28), channel_id=1, source_target_pairs={{0,1},{2,3},{4,5},{6,7},{8,9},{10,11},{12,13},{14,15},{16,17},{18,... | collective-permute-start | bytes 294920 | tf_op jit(solution)/shard_map/ppermute | solution.py:415
  64.3 6.3 %collective-permute-start.1 = (f32[32,768]{1,0:T(8,128)S(1)}, f32[32,768]{1,0:T(8,128)S(1)}, u32[]{:S(2)}, u32[]{:S(2)}) collective-permute-start(f32[32,768]{1,0:T(8,128)S(1)} %get-tuple-element.29), channel_id=1, source_target_pairs={{1,2},{3,4},{5,6},{7,8},{9,10},{11,12},{13,14},{15,16},{17,18},{19... | collective-permute-start | bytes 294920 | tf_op jit(solution)/shard_map/ppermute | solution.py:415
  70.6 0.0 copy-done.4
  70.6 0.6 shard_map.106.whole_ref
  71.2 0.0 copy-start.3
  71.2 1.4 %copy-done.3 = f32[728,512]{1,0:T(8,128)S(1)} copy-done((f32[728,512]{1,0:T(8,128)S(1)}, f32[728,512]{1,0:T(8,128)}, u32[]{:S(2)}) %copy-start.3) | copy-done | bytes 1490968
  72.6 0.0 copy-start
  72.6 0.0 copy-start.1
  72.6 1.0 shard_map.107.l_ref
  73.6 0.2 collective-permute-done.prev_ref
  73.8 6.5 %collective-permute-done.1.next_ref = f32[32,768]{1,0:T(8,128)S(1)} collective-permute-done((f32[32,768]{1,0:T(8,128)S(1)}, f32[32,768]{1,0:T(8,128)S(1)}, u32[]{:S(2)}, u32[]{:S(2)}) %collective-permute-start.1) | collective-permute-done | bytes 98336 | tf_op jit(solution)/shard_map/ppermute | solution.py:415
  80.2 0.0 copy-done
  80.2 0.0 copy-done.1
  80.2 2.4 %shard_map.108 = (f32[728,512]{1,0:T(8,128)S(1)}, f32[32,768]{1,0:T(8,128)S(1)}, f32[32,768]{1,0:T(8,128)S(1)}) custom-call(f32[728,512]{1,0:T(8,128)S(1)} %shard_map.107.l_ref, f32[32,768]{1,0:T(8,128)S(1)} %collective-permute-done.prev_ref, f32[32,768]{1,0:T(8,128)S(1)} %collective-permute-done.1.next_ref, bf16[64,512]{1,0:T(8,128)(2,1)S(1)} %get-tuple-element.30.in_ref, ...), custom_call_target="tpu_custom_call" | custom-call | tf_op jit(solution)/shard_map/pallas_call | solution.py:445
  82.7 0.1 collective-permute-start.2
  82.8 2.3 %collective-permute-start.3 = (f32[32,768]{1,0:T(8,128)S(1)}, f32[32,768]{1,0:T(8,128)S(1)}, u32[]{:S(2)}, u32[]{:S(2)}) collective-permute-start(f32[32,768]{1,0:T(8,128)S(1)} %get-tuple-element.36), channel_id=1, source_target_pairs={{1,2},{3,4},{5,6},{7,8},{9,10},{11,12},{13,14},{15,16},{17,18},{19... | collective-permute-start | bytes 294920 | tf_op jit(solution)/shard_map/ppermute | solution.py:415
  85.1 1.0 shard_map.109.l_ref
  86.1 1.3 %collective-permute-done.2.prev_ref = f32[32,768]{1,0:T(8,128)S(1)} collective-permute-done((f32[32,768]{1,0:T(8,128)S(1)}, f32[32,768]{1,0:T(8,128)S(1)}, u32[]{:S(2)}, u32[]{:S(2)}) %collective-permute-start.2) | collective-permute-done | bytes 98336 | tf_op jit(solution)/shard_map/ppermute | solution.py:415
  87.4 4.9 %collective-permute-done.3.next_ref = f32[32,768]{1,0:T(8,128)S(1)} collective-permute-done((f32[32,768]{1,0:T(8,128)S(1)}, f32[32,768]{1,0:T(8,128)S(1)}, u32[]{:S(2)}, u32[]{:S(2)}) %collective-permute-start.3) | collective-permute-done | bytes 98336 | tf_op jit(solution)/shard_map/ppermute | solution.py:415
  92.3 2.4 %shard_map.110 = (f32[728,512]{1,0:T(8,128)S(1)}, f32[32,768]{1,0:T(8,128)S(1)}, f32[32,768]{1,0:T(8,128)S(1)}) custom-call(f32[728,512]{1,0:T(8,128)S(1)} %shard_map.109.l_ref, f32[32,768]{1,0:T(8,128)S(1)} %collective-permute-done.2.prev_ref, f32[32,768]{1,0:T(8,128)S(1)} %collective-permute-done.3.next_ref, bf16[64,512]{1,0:T(8,128)(2,1)S(1)} %get-tuple-element.30.in_ref, ...), custom_call_target="tpu_custom_call" | custom-call | tf_op jit(solution)/shard_map/pallas_call | solution.py:445
  94.8 0.1 collective-permute-start.4
  94.9 2.3 %collective-permute-start.5 = (f32[32,768]{1,0:T(8,128)S(1)}, f32[32,768]{1,0:T(8,128)S(1)}, u32[]{:S(2)}, u32[]{:S(2)}) collective-permute-start(f32[32,768]{1,0:T(8,128)S(1)} %get-tuple-element.39), channel_id=1, source_target_pairs={{1,2},{3,4},{5,6},{7,8},{9,10},{11,12},{13,14},{15,16},{17,18},{19... | collective-permute-start | bytes 294920 | tf_op jit(solution)/shard_map/ppermute | solution.py:415
  97.2 1.0 shard_map.111.l_ref
  98.2 1.3 %collective-permute-done.4.prev_ref = f32[32,768]{1,0:T(8,128)S(1)} collective-permute-done((f32[32,768]{1,0:T(8,128)S(1)}, f32[32,768]{1,0:T(8,128)S(1)}, u32[]{:S(2)}, u32[]{:S(2)}) %collective-permute-start.4) | collective-permute-done | bytes 98336 | tf_op jit(solution)/shard_map/ppermute | solution.py:415
  99.5 4.9 %collective-permute-done.5.next_ref = f32[32,768]{1,0:T(8,128)S(1)} collective-permute-done((f32[32,768]{1,0:T(8,128)S(1)}, f32[32,768]{1,0:T(8,128)S(1)}, u32[]{:S(2)}, u32[]{:S(2)}) %collective-permute-start.5) | collective-permute-done | bytes 98336 | tf_op jit(solution)/shard_map/ppermute | solution.py:415
  104.4 1.5 %shard_map.112 = f32[720,512]{1,0:T(8,128)} custom-call(f32[728,512]{1,0:T(8,128)S(1)} %shard_map.111.l_ref, f32[32,768]{1,0:T(8,128)S(1)} %collective-permute-done.4.prev_ref, f32[32,768]{1,0:T(8,128)S(1)} %collective-permute-done.5.next_ref, bf16[64,512]{1,0:T(8,128)(2,1)S(1)} %get-tuple-element.30.in_ref), custom_call_target="tpu_custom_call" | custom-call | tf_op jit(solution)/shard_map/pallas_call | solution.py:448
  105.9 0.0 all-to-all-done.first_ref
  105.9 1.9 %shard_map.113 = f32[720,512]{1,0:T(8,128)} custom-call(f32[128,2,768]{2,1,0:T(2,128)S(1)} %all-to-all-done.first_ref, f32[128,2,768]{2,1,0:T(2,128)S(1)} %all_to_all.10.second_ref), custom_call_target="tpu_custom_call" | custom-call | tf_op jit(solution)/shard_map/pallas_call | solution.py:447
Async XLA Ops:
  20.8 1.1 %copy-start.2 = (f32[728,512]{1,0:T(8,128)}, f32[728,512]{1,0:T(8,128)S(1)}, u32[]{:S(2)}) copy-start(f32[728,512]{1,0:T(8,128)S(1)} %get-tuple-element.27.m_ref) | copy-start | bytes 4472836
  21.9 48.7 %copy-start.4 = (s32[4,32]{1,0:T(4,128)S(1)}, s32[4,32]{1,0:T(4,128)}, u32[]{:S(2)}) copy-start(s32[4,32]{1,0:T(4,128)} %neighbours_ref.1) | copy-start | bytes 1540
  58.3 47.6 %all-to-all-start = ((f32[128,2,768]{2,1,0:T(2,128)}), f32[128,2,768]{2,1,0:T(2,128)S(1)}, u32[]{:S(2)}, u32[]{:S(2)}) async-start(f32[128,2,768]{2,1,0:T(2,128)} %get-tuple-element.40), calls=%async_computation | async-start | bytes 1572864 | tf_op jit(solution)/shard_map/all_to_all | solution.py:429
  63.2 10.6 %collective-permute-start = (f32[32,768]{1,0:T(8,128)S(1)}, f32[32,768]{1,0:T(8,128)S(1)}, u32[]{:S(2)}, u32[]{:S(2)}) collective-permute-start(f32[32,768]{1,0:T(8,128)S(1)} %get-tuple-element.28), channel_id=1, source_target_pairs={{0,1},{2,3},{4,5},{6,7},{8,9},{10,11},{12,13},{14,15},{16,17},{18,... | collective-permute-start | bytes 294920 | tf_op jit(solution)/shard_map/ppermute | solution.py:415
  64.3 15.9 %collective-permute-start.1 = (f32[32,768]{1,0:T(8,128)S(1)}, f32[32,768]{1,0:T(8,128)S(1)}, u32[]{:S(2)}, u32[]{:S(2)}) collective-permute-start(f32[32,768]{1,0:T(8,128)S(1)} %get-tuple-element.29), channel_id=1, source_target_pairs={{1,2},{3,4},{5,6},{7,8},{9,10},{11,12},{13,14},{15,16},{17,18},{19... | collective-permute-start | bytes 294920 | tf_op jit(solution)/shard_map/ppermute | solution.py:415
  71.2 1.4 %copy-start.3 = (f32[728,512]{1,0:T(8,128)S(1)}, f32[728,512]{1,0:T(8,128)}, u32[]{:S(2)}) copy-start(f32[728,512]{1,0:T(8,128)} %copy-done.2) | copy-start | bytes 4472836
  72.6 7.6 %copy-start = (f32[256,256]{1,0:T(8,128)S(1)}, f32[256,256]{1,0:T(8,128)}, u32[]{:S(2)}) copy-start(f32[256,256]{1,0:T(8,128)} %constant.17.clone.dx_hbm.dx_ref) | copy-start | bytes 786436
  72.6 7.6 %copy-start.1 = (f32[256,256]{1,0:T(8,128)S(1)}, f32[256,256]{1,0:T(8,128)}, u32[]{:S(2)}) copy-start(f32[256,256]{1,0:T(8,128)} %constant.18.clone.dy_hbm.dy_ref) | copy-start | bytes 786436
  82.7 4.7 %collective-permute-start.2 = (f32[32,768]{1,0:T(8,128)S(1)}, f32[32,768]{1,0:T(8,128)S(1)}, u32[]{:S(2)}, u32[]{:S(2)}) collective-permute-start(f32[32,768]{1,0:T(8,128)S(1)} %get-tuple-element.35), channel_id=1, source_target_pairs={{0,1},{2,3},{4,5},{6,7},{8,9},{10,11},{12,13},{14,15},{16,17},{18,... | collective-permute-start | bytes 294920 | tf_op jit(solution)/shard_map/ppermute | solution.py:415
  82.8 9.6 %collective-permute-start.3 = (f32[32,768]{1,0:T(8,128)S(1)}, f32[32,768]{1,0:T(8,128)S(1)}, u32[]{:S(2)}, u32[]{:S(2)}) collective-permute-start(f32[32,768]{1,0:T(8,128)S(1)} %get-tuple-element.36), channel_id=1, source_target_pairs={{1,2},{3,4},{5,6},{7,8},{9,10},{11,12},{13,14},{15,16},{17,18},{19... | collective-permute-start | bytes 294920 | tf_op jit(solution)/shard_map/ppermute | solution.py:415
  94.8 4.7 %collective-permute-start.4 = (f32[32,768]{1,0:T(8,128)S(1)}, f32[32,768]{1,0:T(8,128)S(1)}, u32[]{:S(2)}, u32[]{:S(2)}) collective-permute-start(f32[32,768]{1,0:T(8,128)S(1)} %get-tuple-element.38), channel_id=1, source_target_pairs={{0,1},{2,3},{4,5},{6,7},{8,9},{10,11},{12,13},{14,15},{16,17},{18,... | collective-permute-start | bytes 294920 | tf_op jit(solution)/shard_map/ppermute | solution.py:415
  94.9 9.6 %collective-permute-start.5 = (f32[32,768]{1,0:T(8,128)S(1)}, f32[32,768]{1,0:T(8,128)S(1)}, u32[]{:S(2)}, u32[]{:S(2)}) collective-permute-start(f32[32,768]{1,0:T(8,128)S(1)} %get-tuple-element.39), channel_id=1, source_target_pairs={{1,2},{3,4},{5,6},{7,8},{9,10},{11,12},{13,14},{15,16},{17,18},{19... | collective-permute-start | bytes 294920 | tf_op jit(solution)/shard_map/ppermute | solution.py:415

commit v4 on v3

--- a/solution.py
+++ b/solution.py
@@ -1,3 +1,5 @@
+from functools import partial
+
 import jax
 import jax.numpy as jnp
 import numpy as np
@@ -75,8 +77,8 @@
     return jnp.sum(jnp.where(key_col < key_row, 1.0, 0.0), axis=0, keepdims=True)
 
 
-HALF = COLS // 2
-SIZES = (32, 96, 128, 160, HALF)
+LOCAL_SIZES = (160, 288, 416, COLS)
+PIECES = ((0, 128, (64, 128)), (128, 320, (192,)), (320, 512, (192,)))
 
 
 def all_started(*copies):
@@ -89,8 +91,8 @@
     return all_started(*(pltpu.make_async_copy(a, b, sems.at[k]) for k, (a, b) in enumerate(pairs)))
 
 
-def sweeps(x_ref, kk, yy, tt, rr, qa, qb, cls, lanes):
-    n1, n2, n3 = (jnp.sum(jnp.where(lanes & (cls > j + 0.5), 1, 0)) for j in (1, 2, 3))
+def sweeps(x_ref, kk, yy, tt, rr, qa, qb, counts, sizes):
+    n1, n2, n3 = counts
     xh, xl = split2(x_ref[...])
     xhh = jnp.concatenate([xh, xh], axis=1)
     y = (dot(xl, kk[0:WIDE, :]) + dot(xhh, kk[...])) * (1.0 / PHYSICS_RATE)
@@ -109,7 +111,7 @@
             y = yy[rb, :] + acc[rb]
             yy[rb, :] = y
             t = jnp.tanh(y)
-            if b + 32 > max((0,) + tuple(n for n in SIZES if n < rows)):
+            if b + 32 > max((0,) + tuple(n for n in sizes if n < rows)):
                 tt[rb, :] += jnp.where(iota((32, WIDE), 0) + b < live, t, 0.0)
             else:
                 tt[rb, :] += t
@@ -121,8 +123,8 @@
                 new[rb, WIDE:] = (old[rb, :].astype(F32) + q.astype(F32)).astype(BF16)
 
     def sweep(k, old, new, low):
-        live = jnp.where(k < 4, HALF, jnp.where(k < 8, n1, jnp.where(k < 12, n2, jnp.where(k < 16, n3, 0))))
-        for below, rows in zip((0,) + SIZES, SIZES):
+        live = jnp.where(k < 4, sizes[-1], jnp.where(k < 8, n1, jnp.where(k < 12, n2, jnp.where(k < 16, n3, 0))))
+        for below, rows in zip((0,) + sizes, sizes):
             @pl.when((live > below) & (live <= rows))
             def _():
                 step(rows, live, old, new, low)
@@ -135,27 +137,40 @@
     lax.fori_loop(0, 8, two_sweeps, 0)
 
 
-def sent(x, ranks):
-    pick = jnp.where(iota((HALF, HALF), 0).astype(F32) == ranks, 1.0, 0.0).astype(BF16)
-    hi, lo = split2(x)
-    return (dot(pick, hi) + dot(pick, lo)).reshape(HALF // 2, 2, WIDE)
-
-
-def part1_kernel(me_ref, fcm_hbm, state_hbm, class_hbm, slots_hbm, mix_hbm,
-                 send_hbm, x2_hbm, kk_hbm, perm_hbm, t1_hbm, info_hbm,
-                 k32, kk, state_ref, class_ref, slot_ref, mix_ref, x0, yy, tt, rr, qa, qb, send_ref, pp, info,
-                 fcm_ref, sems, out_sems):
+def sender_kernel(me_ref, state_hbm, class_hbm, slots_hbm, send_hbm, state_ref, class_ref, slot_ref, send_ref, sems):
     me = me_ref[0]
-    load_fcm, load_mix, load_slots, load_class, load_state = copies(
-        ((fcm_hbm, fcm_ref), (mix_hbm, mix_ref),
-         (slots_hbm.at[:, pl.ds(pl.multiple_of(me // 4 * 128, 128), 128)], slot_ref),
+    load_slots, load_class, load_state = copies(
+        ((slots_hbm.at[:, pl.ds(pl.multiple_of(me // 4 * 128, 128), 128)], slot_ref),
          (class_hbm, class_ref), (state_hbm, state_ref)), sems)
+    load_slots.wait()
+    load_class.wait()
+    part = me % 4
+    own = slot_ref[:, 0:MEMBERS]
+    for j in range(1, 4):
+        own = jnp.where(part == j, slot_ref[:, MEMBERS * j:MEMBERS * j + MEMBERS], own)
+    cls = expand_points(class_ref[...].astype(F32))
+    slot = expand_points(own.astype(F32))
+    place = slot - jnp.floor(slot * (1.0 / COLS)) * COLS
+    perm = jnp.where(iota((COLS, COLS), 0).astype(F32) == rank_row(slot), 1.0, 0.0).astype(BF16)
+    row = iota((128, COLS), 0)
+    eh, el = split2(jnp.where(row == 0, place, jnp.where(row == 1, cls, 0.0)))
+    tail = dot_nt(perm, eh) + dot_nt(perm, el)
+    load_state.wait()
+    sh, sl = split2(state_ref[...])
+    body = dot_nt(perm, sh) + dot_nt(perm, sl)
+    send_ref[...] = jnp.concatenate([body, tail[:, 0:WIDE - ROWS]], axis=1).reshape(COLS // 4, 4, WIDE)
+    pltpu.sync_copy(send_ref, send_hbm)
+
+
+def physics_kernel(fcm_hbm, mix_hbm, class_hbm, state_hbm, kk_hbm, perm_hbm, tt,
+                   mix_ref, class_ref, state_ref, k32, x0, yy, rr, qa, qb, pp, kk, fcm_ref, sems):
+    loads = copies(((fcm_hbm, fcm_ref), (mix_hbm, mix_ref), (class_hbm, class_ref), (state_hbm, state_ref)), sems)
     rep = jnp.where(
         (iota((LEVELS, WIDE), 1) % LEVELS == iota((LEVELS, WIDE), 0)) & (iota((LEVELS, WIDE), 1) < ROWS), 1.0, 0.0
     ).astype(BF16)
     lane = iota((1, WIDE), 1)
-    load_fcm.wait()
-    load_mix.wait()
+    for load in loads[0:3]:
+        load.wait()
     for f in range(FIELDS):
         crow = jnp.zeros((1, WIDE), F32)
         for g in range(FIELDS):
@@ -166,84 +181,86 @@
     hi, lo = split2(k32[...])
     kk[0:WIDE, :] = hi
     kk[WIDE:, :] = lo
-    store_kk = pltpu.make_async_copy(kk, kk_hbm, out_sems.at[0])
+    store_kk = pltpu.make_async_copy(kk, kk_hbm, sems.at[4])
     store_kk.start()
-    load_slots.wait()
-    load_class.wait()
-    part = me % 4
-    own = slot_ref[:, 0:MEMBERS]
-    for j in range(1, 4):
-        own = jnp.where(part == j, slot_ref[:, MEMBERS * j:MEMBERS * j + MEMBERS], own)
     cls = expand_points(class_ref[...].astype(F32))
-    slot = expand_points(own.astype(F32))
-    col = iota((1, COLS), 1).astype(F32)
-    srank = rank_row(slot)
-    batch = jnp.floor(srank * 0.25)
-    within = srank - 4.0 * batch
-    late = within < 1.5
-    hrank = 2.0 * batch + jnp.where(late, within, within - 2.0)
-    crank = rank_row(jnp.where(late, 4.0 * COLS, 0.0) + (4.0 - cls) * COLS + col)
-    place = slot - jnp.floor(slot * (1.0 / COLS)) * COLS
+    crank = rank_row((4.0 - cls) * COLS + iota((1, COLS), 1).astype(F32))
     perm = jnp.where(iota((COLS, COLS), 0).astype(F32) == crank, 1.0, 0.0).astype(BF16)
     pp[...] = perm
-    store_perm = pltpu.make_async_copy(pp, perm_hbm, out_sems.at[1])
+    store_perm = pltpu.make_async_copy(pp, perm_hbm, sems.at[5])
     store_perm.start()
-    row16 = iota((16, COLS), 0)
-    notes = jnp.where(row16 == 0, hrank, jnp.where(row16 == 1, cls, 0.0)).astype(BF16)
-    info[...] = dot_nt(notes, perm)[0:8, :]
-    store_info = pltpu.make_async_copy(info, info_hbm, out_sems.at[2])
-    store_info.start()
-    extra = jnp.where(iota((128, COLS), 0) == 0, place, 0.0)
-    eh, el = split2(extra)
-    x0[:, ROWS:WIDE] = (dot_nt(perm, eh) + dot_nt(perm, el))[:, 0:WIDE - ROWS]
-    load_state.wait()
+    for load in loads[3:]:
+        load.wait()
     sh, sl = split2(state_ref[...])
     x0[:, 0:ROWS] = dot_nt(perm, sh) + dot_nt(perm, sl)
-    store_x2 = pltpu.make_async_copy(x0.at[HALF:COLS], x2_hbm, out_sems.at[3])
-    store_x2.start()
-    sweeps(x0.at[0:HALF], kk, yy, tt, rr, qa, qb, info[1:2, :], iota((1, COLS), 1) < HALF)
-    store_t1 = pltpu.make_async_copy(tt, t1_hbm, out_sems.at[4])
-    store_t1.start()
-    send_ref[...] = sent(x0[0:HALF, :] + PHYSICS_RATE * tt[...], info[0:1, 0:HALF])
-    pltpu.sync_copy(send_ref, send_hbm)
-    for store in (store_kk, store_perm, store_info, store_x2, store_t1):
-        store.wait()
-
-
-def part2_kernel(me_ref, x2_hbm, kk_hbm, perm_hbm, t1_hbm, info_hbm, state_hbm, metric_hbm, nb_hbm, dx_hbm, dy_hbm,
-                 send_hbm, tend_ref, m_ref, mine_a_ref, mine_b_ref, out_ref, in_ref, mrow_ref,
-                 x2, kk, pp, t1, info, state_ref, metric_ref, nb_ref, dx_ref, dy_ref,
-                 yy, tt, rr, qa, qb, send_ref, dxs, dys, sems):
+    x0[:, ROWS:WIDE] = jnp.zeros((COLS, WIDE - ROWS), F32)
+    counts = tuple(jnp.sum(jnp.where(cls > j + 0.5, 1, 0)) for j in (1, 2, 3))
+    sweeps(x0, kk, yy, tt, rr, qa, qb, counts, LOCAL_SIZES)
+    store_kk.wait()
+    store_perm.wait()
+
+
+def start_kernel(me_ref, arrived_ref, tt, perm_hbm, nb_hbm, metric_hbm, dx_hbm, dy_hbm, state_hbm,
+                 tend_ref, m_ref, mine_a_ref, mine_b_ref, out_ref, in_ref, mrow_ref,
+                 pp, nb_ref, metric_ref, dx_ref, dy_ref, state_ref, dxs, dys, sems):
     me = me_ref[0]
-    loads = copies(((info_hbm, info), (x2_hbm, x2), (kk_hbm, kk), (perm_hbm, pp), (t1_hbm, t1), (state_hbm, state_ref),
-                    (metric_hbm, metric_ref), (nb_hbm, nb_ref), (dx_hbm, dx_ref), (dy_hbm, dy_ref)), sems)
+    loads = copies(((perm_hbm, pp), (nb_hbm, nb_ref), (metric_hbm, metric_ref), (dx_hbm, dx_ref), (dy_hbm, dy_ref),
+                    (state_hbm, state_ref)), sems)
+    th, tl = split2(jnp.transpose(tt[...])[0:ROWS, :] * (PHYSICS_RATE / SUBSTEPS))
     for load in loads[0:3]:
         load.wait()
-    sweeps(x2, kk, yy, tt, rr, qa, qb, info[1:2, :], iota((1, COLS), 1) >= HALF)
-    send_ref[...] = sent(x2[...] + PHYSICS_RATE * tt[...], info[0:1, HALF:COLS])
-    store_send = pltpu.make_async_copy(send_ref, send_hbm, sems.at[10])
-    store_send.start()
+    tend_ref[...] = dot(th, pp[...]) + dot(tl, pp[...])
+    tables(me * MEMBERS, nb_ref, metric_ref, out_ref, in_ref, mrow_ref)
     for load in loads[3:]:
         load.wait()
-    ah, al = split2(jnp.transpose(t1[...])[0:ROWS, :] * (PHYSICS_RATE / SUBSTEPS))
-    bh, bl = split2(jnp.transpose(tt[...])[0:ROWS, :] * (PHYSICS_RATE / SUBSTEPS))
-    first, second = pp[0:HALF, :], pp[HALF:COLS, :]
-    tend_ref[...] = (dot(ah, first) + dot(al, first)) + (dot(bh, second) + dot(bl, second))
-    tables(me * MEMBERS, nb_ref, metric_ref, out_ref, in_ref, mrow_ref)
     move(lambda at, n: state_ref[pl.ds(at, n), :], tend_ref, mrow_ref, dx_ref, dy_ref, out_ref,
          dxs, dys, m_ref, mine_a_ref, mine_b_ref)
-    store_send.wait()
+
+
+def piece(arrived_ref, kk, low, high, sizes, work):
+    xs, yy, tt, rr, qa, qb = work
+    rows = arrived_ref[...].reshape(COLS, WIDE)
+    place_row = jnp.transpose(rows[:, WIDE - 128:WIDE])[ROWS - (WIDE - 128):ROWS - (WIDE - 128) + 1, :]
+    pick = jnp.where((iota((high - low, COLS), 0) + low).astype(F32) == place_row, 1.0, 0.0).astype(BF16)
+    hi, lo = split2(rows)
+    xs[...] = dot(pick, hi) + dot(pick, lo)
+    cls = xs[:, ROWS + 1:ROWS + 2]
+    counts = tuple(jnp.sum(jnp.where(cls > j + 0.5, 1, 0)) for j in (1, 2, 3))
+    sweeps(xs, kk, yy, tt, rr, qa, qb, counts, sizes)
+    return xs[...] + PHYSICS_RATE * tt[...]
+
+
+def piece_kernel(arrived_ref, kk, out_ref, *work, low, high, sizes):
+    out_ref[...] = piece(arrived_ref, kk, low, high, sizes, work)
+
+
+def last_kernel(arrived_ref, kk, first_ref, second_ref, out_hbm, cur, *work, low, high, sizes):
+    sems = work[-1]
+    last = piece(arrived_ref, kk, low, high, sizes, work[:-1])
+    turned = jnp.transpose(jnp.concatenate([first_ref[...], second_ref[...], last], axis=0))
+
+    def body(done):
+        for at in CHUNKS:
+            cur[at, :] = turned[at]
+            done(at)
+
+    storing(body, cur, out_hbm, sems)
+
+
+def sweep_work(rows):
+    tall = ((rows, WIDE), F32)
+    return [tall] * 4 + [((rows, WIDE), BF16), ((rows, 2 * WIDE), BF16)]
 
 
 HALO = ((MEMBERS, WIDE), F32)
 MOVED = ((TALL, COLS), F32)
 GRID = ((ROWS, COLS), F32)
-SEND = ((HALF // 2, 2, WIDE), F32)
-HALF_X = ((HALF, WIDE), F32)
+SEND = ((COLS // 4, 4, WIDE), F32)
 OPERATOR = ((2 * WIDE, WIDE), BF16)
 PERM = ((COLS, COLS), BF16)
 INFO = ((8, COLS), F32)
-SWEEP = [HALF_X, HALF_X, HALF_X, ((HALF, WIDE), BF16), ((HALF, 2 * WIDE), BF16), SEND]
+SELECT = ((2 * MEMBERS, COLS), BF16)
+TABLE = ((16, MEMBERS), jnp.int32)
 
 
 def element_tables(neighbours_ref, base):
@@ -381,20 +398,6 @@
          dxs, dys, m_ref, north_ref, south_ref)
 
 
-def place_kernel(first_ref, second_ref, out_hbm, cur, sems):
-    rows = jnp.concatenate([first_ref[...].reshape(HALF, WIDE), second_ref[...].reshape(HALF, WIDE)], axis=0)
-    place_col = rows[:, ROWS:ROWS + 1]
-    pick = jnp.where(iota((COLS, COLS), 1).astype(F32) == place_col, 1.0, 0.0).astype(BF16)
-    hi, lo = split2(jnp.transpose(rows)[0:ROWS, :])
-
-    def body(done):
-        for at in CHUNKS:
-            cur[at, :] = dot(hi[at], pick) + dot(lo[at], pick)
-            done(at)
-
-    storing(body, cur, out_hbm, sems)
-
-
 def call(kernel, out, specs, scratch=(), semaphores=(), hbm_out=0, smem=()):
     shapes = tuple((pltpu.HBM if k < hbm_out else pltpu.VMEM)(s, t) for k, (s, t) in enumerate(out))
     work = [pltpu.VMEM(s, t) for s, t in scratch] + [pltpu.SMEM(s, t) for s, t in smem]
@@ -420,31 +423,41 @@
     base = me * MEMBERS
     state2 = state.reshape(ROWS, COLS)
     dx, dy = (jnp.asarray(a) for a in derivative_blocks())
-    send1, *kept = call(
-        part1_kernel, [SEND, HALF_X, OPERATOR, PERM, HALF_X, INFO], [SM] + [HB] * 5,
-        [((WIDE, WIDE), F32), OPERATOR, GRID, ((16, MEMBERS), jnp.int32), ((16, 128), jnp.int32),
-         ((FIELDS, LEVELS, LEVELS), F32), ((COLS, WIDE), F32)] + SWEEP + [PERM, INFO],
-        [5, 5], 6, [((FIELDS, FIELDS), F32)],
-    )(me, *in_hbm(field_coupling_matrix, state2, cost_class, batch_slot, level_mix))
-    arrived1 = lax.all_to_all(send1, AXES, split_axis=0, concat_axis=0, tiled=True)
-    send2, tend, m, mine_a, mine_b, out_rows, in_rows, mrow = call(
-        part2_kernel,
-        [SEND, GRID, MOVED, HALO, HALO, ((2 * MEMBERS, COLS), BF16), ((2 * MEMBERS, COLS), BF16), INFO],
-        [SM] + [HB] * 10,
-        [HALF_X, OPERATOR, PERM, HALF_X, INFO, GRID, ((16, MEMBERS), F32), ((4, MEMBERS), jnp.int32),
-         ((256, 256), F32), ((256, 256), F32)] + SWEEP + [GRID, GRID],
-        [11], 1,
-    )(me, *in_hbm(*kept, state2, metric, neighbours, dx, dy))
+    (send,) = call(
+        sender_kernel, [SEND], [SM] + [HB] * 3, [GRID, TABLE, ((16, 128), jnp.int32), SEND], [3], 1,
+    )(me, *in_hbm(state2, cost_class, batch_slot))
+    arrived = lax.all_to_all(send, AXES, split_axis=0, concat_axis=0, tiled=True)
+    kk, perm, sums = call(
+        physics_kernel, [OPERATOR, PERM, ((COLS, WIDE), F32)], [HB] * 4,
+        [((FIELDS, LEVELS, LEVELS), F32), TABLE, GRID, ((WIDE, WIDE), F32)] + sweep_work(COLS)[1:]
+        + [PERM, OPERATOR],
+        [6], 2, [((FIELDS, FIELDS), F32)],
+    )(*in_hbm(field_coupling_matrix, level_mix, cost_class, state2))
+    tend, m, mine_a, mine_b, out_rows, in_rows, mrow = call(
+        start_kernel, [GRID, MOVED, HALO, HALO, SELECT, SELECT, INFO], [SM, VM, VM] + [HB] * 6,
+        [PERM, ((4, MEMBERS), jnp.int32), ((16, MEMBERS), F32), ((256, 256), F32), ((256, 256), F32), GRID, GRID,
+         GRID],
+        [6],
+    )(me, arrived, sums, *in_hbm(perm, neighbours, metric, dx, dy, state2))
     (whole,) = call(whole_kernel, [((COLS, COLS), BF16)], [SM, VM])(base, neighbours)
-    arrived2 = lax.all_to_all(send2, AXES, split_axis=0, concat_axis=0, tiled=True)
+    done = []
     for substep in range(SUBSTEPS):
         theirs_b = swapped(mine_b, False)
         theirs_a = swapped(mine_a, True)
         (total,) = call(sum_kernel, [MOVED], [VM, VM])(m, whole)
+        low, high, sizes = PIECES[substep]
+        form = dict(low=low, high=high, sizes=sizes)
+        if substep < SUBSTEPS - 1:
+            done += call(
+                partial(piece_kernel, **form), [((high - low, WIDE), F32)], [VM, VM],
+                sweep_work(high - low))(arrived, kk)
+        else:
+            (physics_state,) = call(
+                partial(last_kernel, **form), [GRID], [VM] * 4, [GRID] + sweep_work(high - low),
+                [len(CHUNKS)], 1)(arrived, kk, *done)
         if substep < SUBSTEPS - 1:
             m, mine_a, mine_b = call(next_kernel, [MOVED, HALO, HALO], [VM] * 9, [GRID] * 3)(
                 total, theirs_a, theirs_b, in_rows, tend, mrow, dx, dy, out_rows)
-    (physics_state,) = call(place_kernel, [GRID], [VM, VM], [GRID], [len(CHUNKS)], 1)(arrived1, arrived2)
     (state_out,) = call(finish_kernel, [GRID], [VM] * 4, [GRID], [len(CHUNKS)], 1)(
         total, theirs_a, theirs_b, in_rows)
     return state_out.reshape(state.shape), physics_state.reshape(state.shape)

time: 108 us -> 91.5 us (0.85)
  blocking collectives: 36.4 us -> 0 us
  Pallas kernels: 31.9 us -> 46.7 us
  waiting for transfers between devices: 19.2 us -> 27.7 us
  local copies, waits for them, and re-layouts: 2.5 us -> 0.02 us
  starting transfers between devices: 17.1 us -> 15.8 us
    all_to_all x1 -> x0, blocking collectives: 36.4 us -> none  [step(): lax.all_to_all(send2, AXES, split_axis=0, concat_axis=0, tiled=True)]
    pallas_call x3 -> x6, Pallas kernels: 22 us -> 36.8 us  [the longest x2 12.1 us: step(): call(partial(piece_kernel, **form), [((high - low, WIDE), F32)], [VM, VM]...]
    all_to_all x1, waiting for transfers between devices: 0.01 us -> 13.7 us  [step(): lax.all_to_all(send, AXES, split_axis=0, concat_axis=0, tiled=True)]
    ppermute x6, starting transfers between devices: 12.3 us -> 4.65 us  [swapped(): return lax.ppermute(array, AXES, pairs + [(j, i) for i, j in pairs])]
    all_to_all x1, starting transfers between devices: 4.83 us -> 11.2 us  [step(): lax.all_to_all(send, AXES, split_axis=0, concat_axis=0, tiled=True)]
    ppermute x6, waiting for transfers between devices: 19.2 us -> 14.1 us  [swapped(): return lax.ppermute(array, AXES, pairs + [(j, i) for i, j in pairs])]
    unnamed x10 -> x8, local copies, waits for them, and re-layouts: 2.5 us -> 0.02 us
  transfers between devices with their start and end apart: 7 -> 7, of which waited for: 6 -> 5; matrix products, arithmetic and copies ran while one was open for 0% -> 0% of each run, Pallas kernels for 9% -> 34%
where the time goes in v4:
time: 91.5 us; the launch traced here: 91.2 us
  Pallas kernels  46.7 us (51%)
  waiting for transfers between devices  27.7 us (30%)
  starting transfers between devices  15.8 us (17%)
  between operations  0.97 us (1%)
    ppermute x6, waiting for transfers between devices, swapped(): return lax.ppermute(array, AXES, pairs + [(j, i) for i, j in pairs])  14.1 us
    all_to_all x1, waiting for transfers between devices, step(): lax.all_to_all(send, AXES, split_axis=0, concat_axis=0, tiled=True)  13.7 us
    pallas_call x2, Pallas kernels, step(): call(partial(piece_kernel, **form), [((high - low, WIDE), F32)], [VM, VM]...  12.1 us
    all_to_all x1, starting transfers between devices, step(): lax.all_to_all(send, AXES, split_axis=0, concat_axis=0, tiled=True)  11.2 us
    pallas_call x1, Pallas kernels, step(): call(physics_kernel, [OPERATOR, PERM, ((COLS, WIDE), F32)], [HB] * 4, [((...  10.5 us
    pallas_call x1, Pallas kernels, step(): call(partial(last_kernel, **form), [GRID], [VM] * 4, [GRID] + sweep_work(...  5.1 us
    pallas_call x2, Pallas kernels, step(): call(next_kernel, [MOVED, HALO, HALO], [VM] * 9, [GRID] * 3)  4.86 us
    ppermute x6, starting transfers between devices, swapped(): return lax.ppermute(array, AXES, pairs + [(j, i) for i, j in pairs])  4.65 us
  transfers between devices with their start and end apart: 7, of which 5 were waited for; matrix products, arithmetic and copies ran while one was open for 0% of the time, Pallas kernels for 34%

profile of v4, /device:TPU:0, one launch (start us, length us, event | category | flops | bytes accessed | tf_op | source)
XLA Modules:
  0.0 91.2 jit_solution(4867989351477092322)
XLA Ops:
  0.6 4.6 %shard_map.104 = f32[128,4,768]{2,1,0:T(4,128)} custom-call(s32[1]{0:T(128)} %bitcast.me_ref, f32[720,512]{1,0:T(8,128)} %bitcast.4, s32[16,32]{1,0:T(8,128)} %class_hbm.3, s32[16,4096]{1,0:T(8,128)} %slots_hbm.1), custom_call_target="tpu_custom_call" | custom-call | tf_op jit(solution)/shard_map/pallas_call | solution.py:426
  5.2 11.2 %all-to-all-start = ((f32[128,4,768]{2,1,0:T(4,128)}), f32[128,4,768]{2,1,0:T(4,128)S(1)}, u32[]{:S(2)}, u32[]{:S(2)}) async-start(f32[128,4,768]{2,1,0:T(4,128)} %shard_map.104), calls=%async_computation | async-start | bytes 3145728 | tf_op jit(solution)/shard_map/all_to_all | solution.py:429
  16.4 10.5 %shard_map.105 = (bf16[1536,768]{1,0:T(8,128)(2,1)}, bf16[512,512]{1,0:T(8,128)(2,1)}, f32[512,768]{1,0:T(8,128)S(1)}) custom-call(f32[10,10]{1,0:T(8,128)} %fcm_hbm.1, f32[10,72,72]{2,1,0:T(8,128)} %mix_hbm.1, s32[16,32]{1,0:T(8,128)} %class_hbm.3, f32[720,512]{1,0:T(8,128)} %bitcast.5), custom_call_target="tpu_custom_call" | custom-call | tf_op jit(solution)/shard_map/pallas_call | solution.py:430
  26.9 13.7 %all-to-all-done.arrived_ref = f32[128,4,768]{2,1,0:T(4,128)S(1)} async-done(((f32[128,4,768]{2,1,0:T(4,128)}), f32[128,4,768]{2,1,0:T(4,128)S(1)}, u32[]{:S(2)}, u32[]{:S(2)}) %all-to-all-start) | async-done | bytes 1572896 | tf_op jit(solution)/shard_map/all_to_all | solution.py:429
  40.6 0.0 copy-start.3
  40.6 4.6 %shard_map.106 = (f32[720,512]{1,0:T(8,128)S(1)}, f32[728,512]{1,0:T(8,128)S(1)}, f32[32,768]{1,0:T(8,128)S(1)}, f32[32,768]{1,0:T(8,128)S(1)}, bf16[64,512]{1,0...) custom-call(s32[1]{0:T(128)} %bitcast.me_ref, f32[128,4,768]{2,1,0:T(4,128)S(1)} %all-to-all-done.arrived_ref, ...), custom_call_target="tpu_custom_call" | custom-call | tf_op jit(solution)/shard_map/pallas_call | solution.py:436
  45.2 0.9 %collective-permute-start = (f32[32,768]{1,0:T(8,128)S(1)}, f32[32,768]{1,0:T(8,128)S(1)}, u32[]{:S(2)}, u32[]{:S(2)}) collective-permute-start(f32[32,768]{1,0:T(8,128)S(1)} %get-tuple-element.21), channel_id=1, source_target_pairs={{0,1},{2,3},{4,5},{6,7},{8,9},{10,11},{12,13},{14,15},{16,17},{18,... | collective-permute-start | bytes 294920 | tf_op jit(solution)/shard_map/ppermute | solution.py:418
  46.1 1.1 %collective-permute-start.1 = (f32[32,768]{1,0:T(8,128)S(1)}, f32[32,768]{1,0:T(8,128)S(1)}, u32[]{:S(2)}, u32[]{:S(2)}) collective-permute-start(f32[32,768]{1,0:T(8,128)S(1)} %get-tuple-element.22), channel_id=1, source_target_pairs={{1,2},{3,4},{5,6},{7,8},{9,10},{11,12},{13,14},{15,16},{17,18},{19... | collective-permute-start | bytes 294920 | tf_op jit(solution)/shard_map/ppermute | solution.py:418
  47.2 0.0 copy-done.3
  47.2 0.6 shard_map.107.whole_ref
  47.9 0.0 copy-start.1
  47.9 0.0 copy-start.2
  47.9 1.0 %shard_map.108.l_ref = f32[728,512]{1,0:T(8,128)S(1)} custom-call(f32[728,512]{1,0:T(8,128)S(1)} %get-tuple-element.20.m_ref, bf16[512,512]{1,0:T(8,128)(2,1)S(1)} %shard_map.107.whole_ref), custom_call_target="tpu_custom_call" | custom-call | tf_op jit(solution)/shard_map/pallas_call | solution.py:447
  48.8 1.3 %collective-permute-done.prev_ref = f32[32,768]{1,0:T(8,128)S(1)} collective-permute-done((f32[32,768]{1,0:T(8,128)S(1)}, f32[32,768]{1,0:T(8,128)S(1)}, u32[]{:S(2)}, u32[]{:S(2)}) %collective-permute-start) | collective-permute-done | bytes 98336 | tf_op jit(solution)/shard_map/ppermute | solution.py:418
  50.1 5.4 %collective-permute-done.1.next_ref = f32[32,768]{1,0:T(8,128)S(1)} collective-permute-done((f32[32,768]{1,0:T(8,128)S(1)}, f32[32,768]{1,0:T(8,128)S(1)}, u32[]{:S(2)}, u32[]{:S(2)}) %collective-permute-start.1) | collective-permute-done | bytes 98336 | tf_op jit(solution)/shard_map/ppermute | solution.py:418
  55.5 0.0 copy-done.1
  55.5 0.0 copy-done.2
  55.5 2.4 %shard_map.109 = (f32[728,512]{1,0:T(8,128)S(1)}, f32[32,768]{1,0:T(8,128)S(1)}, f32[32,768]{1,0:T(8,128)S(1)}) custom-call(f32[728,512]{1,0:T(8,128)S(1)} %shard_map.108.l_ref, f32[32,768]{1,0:T(8,128)S(1)} %collective-permute-done.prev_ref, f32[32,768]{1,0:T(8,128)S(1)} %collective-permute-done.1.next_ref, bf16[64,512]{1,0:T(8,128)(2,1)S(1)} %get-tuple-element.23.in_ref, ...), custom_call_target="tpu_custom_call" | custom-call | tf_op jit(solution)/shard_map/pallas_call | solution.py:459
  58.0 0.1 collective-permute-start.2
  58.1 1.2 %collective-permute-start.3 = (f32[32,768]{1,0:T(8,128)S(1)}, f32[32,768]{1,0:T(8,128)S(1)}, u32[]{:S(2)}, u32[]{:S(2)}) collective-permute-start(f32[32,768]{1,0:T(8,128)S(1)} %get-tuple-element.29), channel_id=1, source_target_pairs={{1,2},{3,4},{5,6},{7,8},{9,10},{11,12},{13,14},{15,16},{17,18},{19... | collective-permute-start | bytes 294920 | tf_op jit(solution)/shard_map/ppermute | solution.py:418
  59.3 1.0 %shard_map.110.l_ref = f32[728,512]{1,0:T(8,128)S(1)} custom-call(f32[728,512]{1,0:T(8,128)S(1)} %get-tuple-element.27.m_ref, bf16[512,512]{1,0:T(8,128)(2,1)S(1)} %shard_map.107.whole_ref), custom_call_target="tpu_custom_call" | custom-call | tf_op jit(solution)/shard_map/pallas_call | solution.py:447
  60.3 0.0 copy-start
  60.3 2.4 %collective-permute-done.2.prev_ref = f32[32,768]{1,0:T(8,128)S(1)} collective-permute-done((f32[32,768]{1,0:T(8,128)S(1)}, f32[32,768]{1,0:T(8,128)S(1)}, u32[]{:S(2)}, u32[]{:S(2)}) %collective-permute-start.2) | collective-permute-done | bytes 98336 | tf_op jit(solution)/shard_map/ppermute | solution.py:418
  62.7 4.9 %collective-permute-done.3.next_ref = f32[32,768]{1,0:T(8,128)S(1)} collective-permute-done((f32[32,768]{1,0:T(8,128)S(1)}, f32[32,768]{1,0:T(8,128)S(1)}, u32[]{:S(2)}, u32[]{:S(2)}) %collective-permute-start.3) | collective-permute-done | bytes 98336 | tf_op jit(solution)/shard_map/ppermute | solution.py:418
  67.6 2.4 %shard_map.111 = (f32[728,512]{1,0:T(8,128)S(1)}, f32[32,768]{1,0:T(8,128)S(1)}, f32[32,768]{1,0:T(8,128)S(1)}) custom-call(f32[728,512]{1,0:T(8,128)S(1)} %shard_map.110.l_ref, f32[32,768]{1,0:T(8,128)S(1)} %collective-permute-done.2.prev_ref, f32[32,768]{1,0:T(8,128)S(1)} %collective-permute-done.3.next_ref, bf16[64,512]{1,0:T(8,128)(2,1)S(1)} %get-tuple-element.23.in_ref, ...), custom_call_target="tpu_custom_call" | custom-call | tf_op jit(solution)/shard_map/pallas_call | solution.py:459
  70.1 0.1 collective-permute-start.4
  70.2 1.2 %collective-permute-start.5 = (f32[32,768]{1,0:T(8,128)S(1)}, f32[32,768]{1,0:T(8,128)S(1)}, u32[]{:S(2)}, u32[]{:S(2)}) collective-permute-start(f32[32,768]{1,0:T(8,128)S(1)} %get-tuple-element.32), channel_id=1, source_target_pairs={{1,2},{3,4},{5,6},{7,8},{9,10},{11,12},{13,14},{15,16},{17,18},{19... | collective-permute-start | bytes 294920 | tf_op jit(solution)/shard_map/ppermute | solution.py:418
  71.4 0.0 copy-done
  71.4 8.5 %shard_map.114.first_ref = f32[128,768]{1,0:T(8,128)S(1)} custom-call(f32[128,4,768]{2,1,0:T(4,128)S(1)} %all-to-all-done.arrived_ref, bf16[1536,768]{1,0:T(8,128)(2,1)S(1)} %copy-done), custom_call_target="tpu_custom_call" | custom-call | tf_op jit(solution)/shard_map/pallas_call | solution.py:451
  79.8 3.6 %shard_map.115.second_ref = f32[192,768]{1,0:T(8,128)S(1)} custom-call(f32[128,4,768]{2,1,0:T(4,128)S(1)} %all-to-all-done.arrived_ref, bf16[1536,768]{1,0:T(8,128)(2,1)S(1)} %copy-done), custom_call_target="tpu_custom_call" | custom-call | tf_op jit(solution)/shard_map/pallas_call | solution.py:451
  83.5 5.1 %shard_map.116 = f32[720,512]{1,0:T(8,128)} custom-call(f32[128,4,768]{2,1,0:T(4,128)S(1)} %all-to-all-done.arrived_ref, bf16[1536,768]{1,0:T(8,128)(2,1)S(1)} %copy-done, f32[128,768]{1,0:T(8,128)S(1)} %shard_map.114.first_ref, f32[192,768]{1,0:T(8,128)S(1)} %shard_map.115.second_ref), custom_call_target="tpu_custom_call" | custom-call | tf_op jit(solution)/shard_map/pallas_call | solution.py:455
  88.6 1.0 %shard_map.112.l_ref = f32[728,512]{1,0:T(8,128)S(1)} custom-call(f32[728,512]{1,0:T(8,128)S(1)} %get-tuple-element.30.m_ref, bf16[512,512]{1,0:T(8,128)(2,1)S(1)} %shard_map.107.whole_ref), custom_call_target="tpu_custom_call" | custom-call | tf_op jit(solution)/shard_map/pallas_call | solution.py:447
  89.5 0.0 collective-permute-done.4.prev_ref
  89.6 0.0 collective-permute-done.5.next_ref
  89.6 1.5 %shard_map.113 = f32[720,512]{1,0:T(8,128)} custom-call(f32[728,512]{1,0:T(8,128)S(1)} %shard_map.112.l_ref, f32[32,768]{1,0:T(8,128)S(1)} %collective-permute-done.4.prev_ref, f32[32,768]{1,0:T(8,128)S(1)} %collective-permute-done.5.next_ref, bf16[64,512]{1,0:T(8,128)(2,1)S(1)} %get-tuple-element.23.in_ref), custom_call_target="tpu_custom_call" | custom-call | tf_op jit(solution)/shard_map/pallas_call | solution.py:461
Async XLA Ops:
  5.2 35.3 %all-to-all-start = ((f32[128,4,768]{2,1,0:T(4,128)}), f32[128,4,768]{2,1,0:T(4,128)S(1)}, u32[]{:S(2)}, u32[]{:S(2)}) async-start(f32[128,4,768]{2,1,0:T(4,128)} %shard_map.104), calls=%async_computation | async-start | bytes 3145728 | tf_op jit(solution)/shard_map/all_to_all | solution.py:429
  40.6 6.6 %copy-start.3 = (s32[4,32]{1,0:T(4,128)S(1)}, s32[4,32]{1,0:T(4,128)}, u32[]{:S(2)}) copy-start(s32[4,32]{1,0:T(4,128)} %neighbours_ref.1) | copy-start | bytes 1540
  45.2 4.9 %collective-permute-start = (f32[32,768]{1,0:T(8,128)S(1)}, f32[32,768]{1,0:T(8,128)S(1)}, u32[]{:S(2)}, u32[]{:S(2)}) collective-permute-start(f32[32,768]{1,0:T(8,128)S(1)} %get-tuple-element.21), channel_id=1, source_target_pairs={{0,1},{2,3},{4,5},{6,7},{8,9},{10,11},{12,13},{14,15},{16,17},{18,... | collective-permute-start | bytes 294920 | tf_op jit(solution)/shard_map/ppermute | solution.py:418
  46.1 9.5 %collective-permute-start.1 = (f32[32,768]{1,0:T(8,128)S(1)}, f32[32,768]{1,0:T(8,128)S(1)}, u32[]{:S(2)}, u32[]{:S(2)}) collective-permute-start(f32[32,768]{1,0:T(8,128)S(1)} %get-tuple-element.22), channel_id=1, source_target_pairs={{1,2},{3,4},{5,6},{7,8},{9,10},{11,12},{13,14},{15,16},{17,18},{19... | collective-permute-start | bytes 294920 | tf_op jit(solution)/shard_map/ppermute | solution.py:418
  47.9 7.7 %copy-start.1 = (f32[256,256]{1,0:T(8,128)S(1)}, f32[256,256]{1,0:T(8,128)}, u32[]{:S(2)}) copy-start(f32[256,256]{1,0:T(8,128)} %constant.18.clone.dy_hbm.dy_ref) | copy-start | bytes 786436
  47.9 7.7 %copy-start.2 = (f32[256,256]{1,0:T(8,128)S(1)}, f32[256,256]{1,0:T(8,128)}, u32[]{:S(2)}) copy-start(f32[256,256]{1,0:T(8,128)} %constant.17.clone.dx_hbm.dx_ref) | copy-start | bytes 786436
  58.0 4.7 %collective-permute-start.2 = (f32[32,768]{1,0:T(8,128)S(1)}, f32[32,768]{1,0:T(8,128)S(1)}, u32[]{:S(2)}, u32[]{:S(2)}) collective-permute-start(f32[32,768]{1,0:T(8,128)S(1)} %get-tuple-element.28), channel_id=1, source_target_pairs={{0,1},{2,3},{4,5},{6,7},{8,9},{10,11},{12,13},{14,15},{16,17},{18,... | collective-permute-start | bytes 294920 | tf_op jit(solution)/shard_map/ppermute | solution.py:418
  58.1 9.6 %collective-permute-start.3 = (f32[32,768]{1,0:T(8,128)S(1)}, f32[32,768]{1,0:T(8,128)S(1)}, u32[]{:S(2)}, u32[]{:S(2)}) collective-permute-start(f32[32,768]{1,0:T(8,128)S(1)} %get-tuple-element.29), channel_id=1, source_target_pairs={{1,2},{3,4},{5,6},{7,8},{9,10},{11,12},{13,14},{15,16},{17,18},{19... | collective-permute-start | bytes 294920 | tf_op jit(solution)/shard_map/ppermute | solution.py:418
  60.3 11.1 %copy-start = (bf16[1536,768]{1,0:T(8,128)(2,1)S(1)}, bf16[1536,768]{1,0:T(8,128)(2,1)}, u32[]{:S(2)}) copy-start(bf16[1536,768]{1,0:T(8,128)(2,1)} %get-tuple-element.33.kk) | copy-start | bytes 7077892
  70.1 19.5 %collective-permute-start.4 = (f32[32,768]{1,0:T(8,128)S(1)}, f32[32,768]{1,0:T(8,128)S(1)}, u32[]{:S(2)}, u32[]{:S(2)}) collective-permute-start(f32[32,768]{1,0:T(8,128)S(1)} %get-tuple-element.31), channel_id=1, source_target_pairs={{0,1},{2,3},{4,5},{6,7},{8,9},{10,11},{12,13},{14,15},{16,17},{18,... | collective-permute-start | bytes 294920 | tf_op jit(solution)/shard_map/ppermute | solution.py:418
  70.2 19.4 %collective-permute-start.5 = (f32[32,768]{1,0:T(8,128)S(1)}, f32[32,768]{1,0:T(8,128)S(1)}, u32[]{:S(2)}, u32[]{:S(2)}) collective-permute-start(f32[32,768]{1,0:T(8,128)S(1)} %get-tuple-element.32), channel_id=1, source_target_pairs={{1,2},{3,4},{5,6},{7,8},{9,10},{11,12},{13,14},{15,16},{17,18},{19... | collective-permute-start | bytes 294920 | tf_op jit(solution)/shard_map/ppermute | solution.py:418

commit v5 on v2

--- a/solution.py
+++ b/solution.py
@@ -40,6 +40,9 @@
     across = np.kron(np.eye(4), d).astype(np.float32).T
     upward = np.kron(d, np.eye(4)).astype(np.float32).T
     return np.kron(np.eye(16), across).astype(np.float32), np.kron(np.eye(16), upward).astype(np.float32)
+
+
+SIZES = (160, 288, 416, COLS)
 
 
 def split2(v):
@@ -153,32 +156,29 @@
 
     def step(rows, live, old, new, low):
         deep = 2 * WIDE if low else WIDE
-        n, wd, at, br = 0, WIDE, slice(0, WIDE), 64
         acc = dot(old[0:rows, 0:deep], kk[0:deep, :])
-        for b in range(0, rows, br):
-            part = acc[b:b + br]
-            rb = slice(b, b + br)
-            y = yy[rb, at] + part
-            yy[rb, at] = y
+        for b in range(0, rows, 32):
+            rb = slice(b, b + 32)
+            y = yy[rb, :] + acc[rb]
+            yy[rb, :] = y
             t = jnp.tanh(y)
-            if b + 64 >= rows:
-                tt[rb, at] += jnp.where(iota((br, wd), 0) + b < live, t, 0.0)
+            if b + 32 > max((0,) + tuple(n for n in SIZES if n < rows)):
+                tt[rb, :] += jnp.where(iota((32, WIDE), 0) + b < live, t, 0.0)
             else:
-                tt[rb, at] += t
-            s = t + rr[rb, at]
+                tt[rb, :] += t
+            s = t + rr[rb, :]
             q = s.astype(BF16)
-            rr[rb, at] = s - q.astype(F32)
-            new[rb, at] = q
+            rr[rb, :] = s - q.astype(F32)
+            new[rb, 0:WIDE] = q
             if not low:
-                new[rb, WIDE + n:WIDE + n + wd] = (old[rb, at].astype(F32) + q.astype(F32)).astype(BF16)
+                new[rb, WIDE:] = (old[rb, 0:WIDE].astype(F32) + q.astype(F32)).astype(BF16)
 
     def sweep(k, old, new, low):
         live = jnp.where(k < 4, COLS, jnp.where(k < 8, n1, jnp.where(k < 12, n2, jnp.where(k < 16, n3, 0))))
-        which = (live + 63) // 64
-        for i in range(8):
-            @pl.when(which == i + 1)
+        for below, rows in zip((0,) + SIZES, SIZES):
+            @pl.when((live > below) & (live <= rows))
             def _():
-                step(64 * (i + 1), live, old, new, low)
+                step(rows, live, old, new, low)
 
     def two_sweeps(j, _):
         sweep(2 * j + 1, qa, qb, False)
@@ -360,7 +360,8 @@
          dxs, dys, m_ref, north_ref, south_ref)
 
 
-def place_kernel(arrived_ref, out_hbm, cur, sems):
+def place_kernel(arrived_hbm, out_hbm, arrived_ref, cur, sems):
+    pltpu.sync_copy(arrived_hbm, arrived_ref)
     rows = arrived_ref[...].reshape(COLS, WIDE)
     place_col = rows[:, ROWS:ROWS + 1]
     pick = jnp.where(iota((COLS, COLS), 1).astype(F32) == place_col, 1.0, 0.0).astype(BF16)
@@ -411,7 +412,8 @@
         if substep < SUBSTEPS - 1:
             m, mine_a, mine_b = call(next_kernel, [MOVED, HALO, HALO], [VM] * 9, [GRID] * 3)(
                 total, theirs_a, theirs_b, in_rows, tend, mrow, dx, dy, out_rows)
-    (physics_state,) = call(place_kernel, [GRID], [VM], [GRID], len(CHUNKS), 1)(arrived)
+    (physics_state,) = call(place_kernel, [GRID], [HB], [((COLS // 4, 4, WIDE), F32), GRID], len(CHUNKS), 1)(
+        *in_hbm(arrived))
     (state_out,) = call(finish_kernel, [GRID], [VM] * 4, [GRID], len(CHUNKS), 1)(
         total, theirs_a, theirs_b, in_rows)
     return state_out.reshape(state.shape), physics_state.reshape(state.shape)

time: 92.3 us -> 91.3 us (0.989)
  local copies, waits for them, and re-layouts: 2.51 us -> 0.02 us
  waiting for transfers between devices: 27.6 us -> 28.6 us
    unnamed x10 -> x6, local copies, waits for them, and re-layouts: 2.51 us -> 0.02 us
    pallas_call x1, Pallas kernels: 1.95 us -> 3.36 us  [step(): call(place_kernel, [GRID], [HB], [((COLS // 4, 4, WIDE), F32), GRID], len...]
    ppermute x6, waiting for transfers between devices: 27.6 us -> 28.6 us  [swapped(): return lax.ppermute(array, AXES, pairs + [(j, i) for i, j in pairs])]
where the time goes in v5:
time: 91.3 us; the launch traced here: 91 us
  starting transfers between devices  31.2 us (34%)
  Pallas kernels  30.3 us (33%)
  waiting for transfers between devices  28.6 us (31%)
  between operations  0.93 us (1%)
    ppermute x6, waiting for transfers between devices, swapped(): return lax.ppermute(array, AXES, pairs + [(j, i) for i, j in pairs])  28.6 us
    all_to_all x1, starting transfers between devices, step(): lax.all_to_all(send, AXES, split_axis=0, concat_axis=0, tiled=True)  19 us
    pallas_call x1, Pallas kernels, physics_call(): pl.pallas_call(physics_kernel, out_shape=shapes, in_specs=[SM] + [HB] * 9...  17.1 us
    ppermute x6, starting transfers between devices, swapped(): return lax.ppermute(array, AXES, pairs + [(j, i) for i, j in pairs])  12.2 us
    pallas_call x2, Pallas kernels, step(): call(next_kernel, [MOVED, HALO, HALO], [VM] * 9, [GRID] * 3)  4.86 us
    pallas_call x1, Pallas kernels, step(): call(place_kernel, [GRID], [HB], [((COLS // 4, 4, WIDE), F32), GRID], len...  3.36 us
    pallas_call x3, Pallas kernels, step(): total, = call(sum_kernel, [MOVED], [VM, VM])(m, whole)  2.87 us
  transfers between devices with their start and end apart: 7, of which 6 were waited for; matrix products, arithmetic and copies ran while one was open for 0% of the time, Pallas kernels for 11%

profile of v5, /device:TPU:0, one launch (start us, length us, event | category | flops | bytes accessed | tf_op | source)
XLA Modules:
  0.0 91.0 jit_solution(2500084745992338647)
XLA Ops:
  0.6 17.1 %physics.1 = (f32[128,4,768]{2,1,0:T(4,128)}, f32[720,512]{1,0:T(8,128)S(1)}, f32[728,512]{1,0:T(8,128)S(1)}, f32[32,768]{1,0:T(8,128)S(1)}, f32[32,768]{1,0:T(8...) custom-call(s32[1]{0:T(128)} %bitcast.me_ref, f32[10,10]{1,0:T(8,128)} %fcm_hbm.1, ...), custom_call_target="tpu_custom_call" | custom-call | tf_op jit(solution)/shard_map/physics/pallas_call | solution.py:220
  17.8 0.0 copy-start.2
  17.8 19.0 %all-to-all-start = ((f32[128,4,768]{2,1,0:T(4,128)}), f32[128,4,768]{2,1,0:T(4,128)}, u32[]{:S(2)}, u32[]{:S(2)}) async-start(f32[128,4,768]{2,1,0:T(4,128)} %get-tuple-element.29), calls=%async_computation | async-start | bytes 3145728 | tf_op jit(solution)/shard_map/all_to_all | solution.py:407
  36.8 1.1 %collective-permute-start = (f32[32,768]{1,0:T(8,128)S(1)}, f32[32,768]{1,0:T(8,128)S(1)}, u32[]{:S(2)}, u32[]{:S(2)}) collective-permute-start(f32[32,768]{1,0:T(8,128)S(1)} %get-tuple-element.17), channel_id=1, source_target_pairs={{0,1},{2,3},{4,5},{6,7},{8,9},{10,11},{12,13},{14,15},{16,17},{18,... | collective-permute-start | bytes 294920 | tf_op jit(solution)/shard_map/ppermute | solution.py:396
  37.9 6.3 %collective-permute-start.1 = (f32[32,768]{1,0:T(8,128)S(1)}, f32[32,768]{1,0:T(8,128)S(1)}, u32[]{:S(2)}, u32[]{:S(2)}) collective-permute-start(f32[32,768]{1,0:T(8,128)S(1)} %get-tuple-element.18), channel_id=1, source_target_pairs={{1,2},{3,4},{5,6},{7,8},{9,10},{11,12},{13,14},{15,16},{17,18},{19... | collective-permute-start | bytes 294920 | tf_op jit(solution)/shard_map/ppermute | solution.py:396
  44.1 0.0 copy-done.2
  44.2 0.6 shard_map.104.whole_ref
  44.8 0.0 copy-start
  44.8 0.0 copy-start.1
  44.8 1.0 %shard_map.105.l_ref = f32[728,512]{1,0:T(8,128)S(1)} custom-call(f32[728,512]{1,0:T(8,128)S(1)} %get-tuple-element.16.m_ref, bf16[512,512]{1,0:T(8,128)(2,1)S(1)} %shard_map.104.whole_ref), custom_call_target="tpu_custom_call" | custom-call | tf_op jit(solution)/shard_map/pallas_call | solution.py:411
  45.8 10.4 %collective-permute-done.prev_ref = f32[32,768]{1,0:T(8,128)S(1)} collective-permute-done((f32[32,768]{1,0:T(8,128)S(1)}, f32[32,768]{1,0:T(8,128)S(1)}, u32[]{:S(2)}, u32[]{:S(2)}) %collective-permute-start) | collective-permute-done | bytes 98336 | tf_op jit(solution)/shard_map/ppermute | solution.py:396
  56.2 5.6 %collective-permute-done.1.next_ref = f32[32,768]{1,0:T(8,128)S(1)} collective-permute-done((f32[32,768]{1,0:T(8,128)S(1)}, f32[32,768]{1,0:T(8,128)S(1)}, u32[]{:S(2)}, u32[]{:S(2)}) %collective-permute-start.1) | collective-permute-done | bytes 98336 | tf_op jit(solution)/shard_map/ppermute | solution.py:396
  61.8 0.0 copy-done
  61.8 0.0 copy-done.1
  61.8 2.4 %shard_map.106 = (f32[728,512]{1,0:T(8,128)S(1)}, f32[32,768]{1,0:T(8,128)S(1)}, f32[32,768]{1,0:T(8,128)S(1)}) custom-call(f32[728,512]{1,0:T(8,128)S(1)} %shard_map.105.l_ref, f32[32,768]{1,0:T(8,128)S(1)} %collective-permute-done.prev_ref, f32[32,768]{1,0:T(8,128)S(1)} %collective-permute-done.1.next_ref, bf16[64,512]{1,0:T(8,128)(2,1)S(1)} %get-tuple-element.19.in_ref, ...), custom_call_target="tpu_custom_call" | custom-call | tf_op jit(solution)/shard_map/pallas_call | solution.py:413
  64.3 0.1 collective-permute-start.2
  64.4 2.3 %collective-permute-start.3 = (f32[32,768]{1,0:T(8,128)S(1)}, f32[32,768]{1,0:T(8,128)S(1)}, u32[]{:S(2)}, u32[]{:S(2)}) collective-permute-start(f32[32,768]{1,0:T(8,128)S(1)} %get-tuple-element.25), channel_id=1, source_target_pairs={{1,2},{3,4},{5,6},{7,8},{9,10},{11,12},{13,14},{15,16},{17,18},{19... | collective-permute-start | bytes 294920 | tf_op jit(solution)/shard_map/ppermute | solution.py:396
  66.7 1.0 %shard_map.107.l_ref = f32[728,512]{1,0:T(8,128)S(1)} custom-call(f32[728,512]{1,0:T(8,128)S(1)} %get-tuple-element.23.m_ref, bf16[512,512]{1,0:T(8,128)(2,1)S(1)} %shard_map.104.whole_ref), custom_call_target="tpu_custom_call" | custom-call | tf_op jit(solution)/shard_map/pallas_call | solution.py:411
  67.7 1.3 %collective-permute-done.2.prev_ref = f32[32,768]{1,0:T(8,128)S(1)} collective-permute-done((f32[32,768]{1,0:T(8,128)S(1)}, f32[32,768]{1,0:T(8,128)S(1)}, u32[]{:S(2)}, u32[]{:S(2)}) %collective-permute-start.2) | collective-permute-done | bytes 98336 | tf_op jit(solution)/shard_map/ppermute | solution.py:396
  69.0 4.9 %collective-permute-done.3.next_ref = f32[32,768]{1,0:T(8,128)S(1)} collective-permute-done((f32[32,768]{1,0:T(8,128)S(1)}, f32[32,768]{1,0:T(8,128)S(1)}, u32[]{:S(2)}, u32[]{:S(2)}) %collective-permute-start.3) | collective-permute-done | bytes 98336 | tf_op jit(solution)/shard_map/ppermute | solution.py:396
  73.9 2.4 %shard_map.108 = (f32[728,512]{1,0:T(8,128)S(1)}, f32[32,768]{1,0:T(8,128)S(1)}, f32[32,768]{1,0:T(8,128)S(1)}) custom-call(f32[728,512]{1,0:T(8,128)S(1)} %shard_map.107.l_ref, f32[32,768]{1,0:T(8,128)S(1)} %collective-permute-done.2.prev_ref, f32[32,768]{1,0:T(8,128)S(1)} %collective-permute-done.3.next_ref, bf16[64,512]{1,0:T(8,128)(2,1)S(1)} %get-tuple-element.19.in_ref, ...), custom_call_target="tpu_custom_call" | custom-call | tf_op jit(solution)/shard_map/pallas_call | solution.py:413
  76.4 0.1 collective-permute-start.4
  76.5 2.3 %collective-permute-start.5 = (f32[32,768]{1,0:T(8,128)S(1)}, f32[32,768]{1,0:T(8,128)S(1)}, u32[]{:S(2)}, u32[]{:S(2)}) collective-permute-start(f32[32,768]{1,0:T(8,128)S(1)} %get-tuple-element.28), channel_id=1, source_target_pairs={{1,2},{3,4},{5,6},{7,8},{9,10},{11,12},{13,14},{15,16},{17,18},{19... | collective-permute-start | bytes 294920 | tf_op jit(solution)/shard_map/ppermute | solution.py:396
  78.8 1.0 %shard_map.109.l_ref = f32[728,512]{1,0:T(8,128)S(1)} custom-call(f32[728,512]{1,0:T(8,128)S(1)} %get-tuple-element.26.m_ref, bf16[512,512]{1,0:T(8,128)(2,1)S(1)} %shard_map.104.whole_ref), custom_call_target="tpu_custom_call" | custom-call | tf_op jit(solution)/shard_map/pallas_call | solution.py:411
  79.8 1.3 %collective-permute-done.4.prev_ref = f32[32,768]{1,0:T(8,128)S(1)} collective-permute-done((f32[32,768]{1,0:T(8,128)S(1)}, f32[32,768]{1,0:T(8,128)S(1)}, u32[]{:S(2)}, u32[]{:S(2)}) %collective-permute-start.4) | collective-permute-done | bytes 98336 | tf_op jit(solution)/shard_map/ppermute | solution.py:396
  81.1 4.9 %collective-permute-done.5.next_ref = f32[32,768]{1,0:T(8,128)S(1)} collective-permute-done((f32[32,768]{1,0:T(8,128)S(1)}, f32[32,768]{1,0:T(8,128)S(1)}, u32[]{:S(2)}, u32[]{:S(2)}) %collective-permute-start.5) | collective-permute-done | bytes 98336 | tf_op jit(solution)/shard_map/ppermute | solution.py:396
  86.0 1.5 %shard_map.110 = f32[720,512]{1,0:T(8,128)} custom-call(f32[728,512]{1,0:T(8,128)S(1)} %shard_map.109.l_ref, f32[32,768]{1,0:T(8,128)S(1)} %collective-permute-done.4.prev_ref, f32[32,768]{1,0:T(8,128)S(1)} %collective-permute-done.5.next_ref, bf16[64,512]{1,0:T(8,128)(2,1)S(1)} %get-tuple-element.19.in_ref), custom_call_target="tpu_custom_call" | custom-call | tf_op jit(solution)/shard_map/pallas_call | solution.py:417
  87.5 0.0 all-to-all-done.arrived_hbm
  87.5 3.4 %shard_map.111 = f32[720,512]{1,0:T(8,128)} custom-call(f32[128,4,768]{2,1,0:T(4,128)} %all-to-all-done.arrived_hbm), custom_call_target="tpu_custom_call" | custom-call | tf_op jit(solution)/shard_map/pallas_call | solution.py:415
Async XLA Ops:
  17.8 26.4 %copy-start.2 = (s32[4,32]{1,0:T(4,128)S(1)}, s32[4,32]{1,0:T(4,128)}, u32[]{:S(2)}) copy-start(s32[4,32]{1,0:T(4,128)} %neighbours_ref.1) | copy-start | bytes 1540
  17.8 69.7 %all-to-all-start = ((f32[128,4,768]{2,1,0:T(4,128)}), f32[128,4,768]{2,1,0:T(4,128)}, u32[]{:S(2)}, u32[]{:S(2)}) async-start(f32[128,4,768]{2,1,0:T(4,128)} %get-tuple-element.29), calls=%async_computation | async-start | bytes 3145728 | tf_op jit(solution)/shard_map/all_to_all | solution.py:407
  36.8 19.4 %collective-permute-start = (f32[32,768]{1,0:T(8,128)S(1)}, f32[32,768]{1,0:T(8,128)S(1)}, u32[]{:S(2)}, u32[]{:S(2)}) collective-permute-start(f32[32,768]{1,0:T(8,128)S(1)} %get-tuple-element.17), channel_id=1, source_target_pairs={{0,1},{2,3},{4,5},{6,7},{8,9},{10,11},{12,13},{14,15},{16,17},{18,... | collective-permute-start | bytes 294920 | tf_op jit(solution)/shard_map/ppermute | solution.py:396
  37.9 24.0 %collective-permute-start.1 = (f32[32,768]{1,0:T(8,128)S(1)}, f32[32,768]{1,0:T(8,128)S(1)}, u32[]{:S(2)}, u32[]{:S(2)}) collective-permute-start(f32[32,768]{1,0:T(8,128)S(1)} %get-tuple-element.18), channel_id=1, source_target_pairs={{1,2},{3,4},{5,6},{7,8},{9,10},{11,12},{13,14},{15,16},{17,18},{19... | collective-permute-start | bytes 294920 | tf_op jit(solution)/shard_map/ppermute | solution.py:396
  44.8 17.0 %copy-start = (f32[256,256]{1,0:T(8,128)S(1)}, f32[256,256]{1,0:T(8,128)}, u32[]{:S(2)}) copy-start(f32[256,256]{1,0:T(8,128)} %constant.18.clone.dy_hbm.dy_ref) | copy-start | bytes 786436
  44.8 17.0 %copy-start.1 = (f32[256,256]{1,0:T(8,128)S(1)}, f32[256,256]{1,0:T(8,128)}, u32[]{:S(2)}) copy-start(f32[256,256]{1,0:T(8,128)} %constant.17.clone.dx_hbm.dx_ref) | copy-start | bytes 786436
  64.3 4.7 %collective-permute-start.2 = (f32[32,768]{1,0:T(8,128)S(1)}, f32[32,768]{1,0:T(8,128)S(1)}, u32[]{:S(2)}, u32[]{:S(2)}) collective-permute-start(f32[32,768]{1,0:T(8,128)S(1)} %get-tuple-element.24), channel_id=1, source_target_pairs={{0,1},{2,3},{4,5},{6,7},{8,9},{10,11},{12,13},{14,15},{16,17},{18,... | collective-permute-start | bytes 294920 | tf_op jit(solution)/shard_map/ppermute | solution.py:396
  64.4 9.6 %collective-permute-start.3 = (f32[32,768]{1,0:T(8,128)S(1)}, f32[32,768]{1,0:T(8,128)S(1)}, u32[]{:S(2)}, u32[]{:S(2)}) collective-permute-start(f32[32,768]{1,0:T(8,128)S(1)} %get-tuple-element.25), channel_id=1, source_target_pairs={{1,2},{3,4},{5,6},{7,8},{9,10},{11,12},{13,14},{15,16},{17,18},{19... | collective-permute-start | bytes 294920 | tf_op jit(solution)/shard_map/ppermute | solution.py:396
  76.4 4.7 %collective-permute-start.4 = (f32[32,768]{1,0:T(8,128)S(1)}, f32[32,768]{1,0:T(8,128)S(1)}, u32[]{:S(2)}, u32[]{:S(2)}) collective-permute-start(f32[32,768]{1,0:T(8,128)S(1)} %get-tuple-element.27), channel_id=1, source_target_pairs={{0,1},{2,3},{4,5},{6,7},{8,9},{10,11},{12,13},{14,15},{16,17},{18,... | collective-permute-start | bytes 294920 | tf_op jit(solution)/shard_map/ppermute | solution.py:396
  76.5 9.6 %collective-permute-start.5 = (f32[32,768]{1,0:T(8,128)S(1)}, f32[32,768]{1,0:T(8,128)S(1)}, u32[]{:S(2)}, u32[]{:S(2)}) collective-permute-start(f32[32,768]{1,0:T(8,128)S(1)} %get-tuple-element.28), channel_id=1, source_target_pairs={{1,2},{3,4},{5,6},{7,8},{9,10},{11,12},{13,14},{15,16},{17,18},{19... | collective-permute-start | bytes 294920 | tf_op jit(solution)/shard_map/ppermute | solution.py:396

commit v6 on v5

--- a/solution.py
+++ b/solution.py
@@ -102,12 +102,13 @@
     load_metric.start()
     load_dx.start()
     load_dy.start()
+    for load in (load_fcm, load_mix, load_slots, load_class, load_nb, load_metric, load_dx, load_dy, load_state):
+        load.wait()
+    tables(me * MEMBERS, nb_ref, metric_ref, out_ref, in_ref, mrow_ref)
     rep = jnp.where(
         (iota((LEVELS, WIDE), 1) % LEVELS == iota((LEVELS, WIDE), 0)) & (iota((LEVELS, WIDE), 1) < ROWS), 1.0, 0.0
     ).astype(BF16)
     lane = iota((1, WIDE), 1)
-    load_fcm.wait()
-    load_mix.wait()
     for f in range(FIELDS):
         crow = jnp.zeros((1, WIDE), F32)
         for g in range(FIELDS):
@@ -118,8 +119,6 @@
     hi, lo = split2(k32[...])
     kk[0:WIDE, :] = hi
     kk[WIDE:, :] = lo
-    load_slots.wait()
-    load_class.wait()
     part = me % 4
     own = slot_ref[:, 0:MEMBERS]
     for j in range(1, 4):
@@ -139,9 +138,9 @@
     n1 = jnp.sum(jnp.where(cls > 1.5, 1, 0))
     n2 = jnp.sum(jnp.where(cls > 2.5, 1, 0))
     n3 = jnp.sum(jnp.where(cls > 3.5, 1, 0))
-    load_state.wait()
     sh, sl = split2(state_ref[...])
     x0[:, 0:ROWS] = dot_nt(perm, sh) + dot_nt(perm, sl)
+    rates(state_ref[...], dx_ref, dy_ref, dxs, dys)
     xh, xl = split2(x0[...])
     xhh = jnp.concatenate([xh, xh], axis=1)
     for n in range(0, WIDE, 256):
@@ -194,13 +193,7 @@
     store_send.start()
     th, tl = split2(jnp.transpose(tt[...])[0:ROWS, :] * (PHYSICS_RATE / SUBSTEPS))
     tend_ref[...] = dot(th, perm) + dot(tl, perm)
-    load_nb.wait()
-    load_metric.wait()
-    tables(me * MEMBERS, nb_ref, metric_ref, out_ref, in_ref, mrow_ref)
-    load_dx.wait()
-    load_dy.wait()
-    move(lambda at, n: state_ref[pl.ds(at, n), :], tend_ref, mrow_ref, dx_ref, dy_ref, out_ref,
-         dxs, dys, m_ref, mine_a_ref, mine_b_ref)
+    move(lambda at, n: state_ref[pl.ds(at, n), :], tend_ref, mrow_ref, out_ref, dxs, dys, m_ref, mine_a_ref, mine_b_ref)
     store_send.wait()
 
 
@@ -297,13 +290,16 @@
     mrow_ref[...] = jnp.broadcast_to(expand_points(metric_ref[...]), (8, COLS))
 
 
-def move(read, tend_ref, mrow_ref, dx_ref, dy_ref, out_ref, dxs, dys, m_ref, north_ref, south_ref):
-    vh, vl = split2(read(0, ROWS))
+def rates(value, dx_ref, dy_ref, dxs, dys):
+    vh, vl = split2(value)
     for half in (0, 256):
         at = slice(half, half + 256)
         for d_ref, acc in ((dx_ref, dxs), (dy_ref, dys)):
             dh, dl = split2(d_ref[...])
             acc[:, at] = dot(vh[:, at], dh) + dot(vl[:, at], dh) + dot(vh[:, at], dl)
+
+
+def move(read, tend_ref, mrow_ref, out_ref, dxs, dys, m_ref, mine_a_ref, mine_b_ref):
     metric = mrow_ref[0:1, :]
     u, v = read(0, LEVELS), read(LEVELS, LEVELS)
     for f in range(FIELDS):
@@ -313,10 +309,10 @@
     m_ref[ROWS:TALL, :] = mrow_ref[...]
     mh, ml = split2(m_ref[...])
     halo = dot_nt(out_ref[...], mh) + dot_nt(out_ref[...], ml)
-    north_ref[:, 0:TALL] = halo[0:MEMBERS]
-    south_ref[:, 0:TALL] = halo[MEMBERS:]
-    north_ref[:, TALL:WIDE] = jnp.zeros((MEMBERS, WIDE - TALL), F32)
-    south_ref[:, TALL:WIDE] = jnp.zeros((MEMBERS, WIDE - TALL), F32)
+    mine_a_ref[:, 0:TALL] = halo[0:MEMBERS]
+    mine_b_ref[:, 0:TALL] = halo[MEMBERS:]
+    mine_a_ref[:, TALL:WIDE] = jnp.zeros((MEMBERS, WIDE - TALL), F32)
+    mine_b_ref[:, TALL:WIDE] = jnp.zeros((MEMBERS, WIDE - TALL), F32)
 
 
 def sum_kernel(m_ref, whole_ref, l_ref):
@@ -354,10 +350,10 @@
 
 
 def next_kernel(l_ref, prev_ref, next_ref, in_ref, tend_ref, mrow_ref, dx_ref, dy_ref, out_ref,
-                m_ref, north_ref, south_ref, cur, dxs, dys):
+                m_ref, mine_a_ref, mine_b_ref, cur, dxs, dys):
     finish(l_ref, prev_ref, next_ref, in_ref, cur)
-    move(lambda at, n: cur[pl.ds(at, n), :], tend_ref, mrow_ref, dx_ref, dy_ref, out_ref,
-         dxs, dys, m_ref, north_ref, south_ref)
+    rates(cur[...], dx_ref, dy_ref, dxs, dys)
+    move(lambda at, n: cur[pl.ds(at, n), :], tend_ref, mrow_ref, out_ref, dxs, dys, m_ref, mine_a_ref, mine_b_ref)
 
 
 def place_kernel(arrived_hbm, out_hbm, arrived_ref, cur, sems):

time: 91.3 us -> 89.7 us (0.982)
  Pallas kernels: 30.3 us -> 28.7 us
    pallas_call x1, Pallas kernels: 17.1 us -> 15.5 us  [physics_call(): pl.pallas_call(physics_kernel, out_shape=shapes, in_specs=[SM] + [HB] * 9...]
where the time goes in v6:
time: 89.7 us; the launch traced here: 89.5 us
  starting transfers between devices  31.2 us (35%)
  Pallas kernels  28.7 us (32%)
  waiting for transfers between devices  28.6 us (32%)
  between operations  0.93 us (1%)
    ppermute x6, waiting for transfers between devices, swapped(): return lax.ppermute(array, AXES, pairs + [(j, i) for i, j in pairs])  28.6 us
    all_to_all x1, starting transfers between devices, step(): lax.all_to_all(send, AXES, split_axis=0, concat_axis=0, tiled=True)  19 us
    pallas_call x1, Pallas kernels, physics_call(): pl.pallas_call(physics_kernel, out_shape=shapes, in_specs=[SM] + [HB] * 9...  15.5 us
    ppermute x6, starting transfers between devices, swapped(): return lax.ppermute(array, AXES, pairs + [(j, i) for i, j in pairs])  12.2 us
    pallas_call x2, Pallas kernels, step(): call(next_kernel, [MOVED, HALO, HALO], [VM] * 9, [GRID] * 3)  4.86 us
    pallas_call x1, Pallas kernels, step(): call(place_kernel, [GRID], [HB], [((COLS // 4, 4, WIDE), F32), GRID], len...  3.36 us
    pallas_call x3, Pallas kernels, step(): total, = call(sum_kernel, [MOVED], [VM, VM])(m, whole)  2.87 us
  transfers between devices with their start and end apart: 7, of which 6 were waited for; matrix products, arithmetic and copies ran while one was open for 0% of the time, Pallas kernels for 11%

profile of v6, /device:TPU:0, one launch (start us, length us, event | category | flops | bytes accessed | tf_op | source)
XLA Modules:
  0.0 89.5 jit_solution(9065807542685811338)
XLA Ops:
  0.6 15.5 %physics.1 = (f32[128,4,768]{2,1,0:T(4,128)}, f32[720,512]{1,0:T(8,128)S(1)}, f32[728,512]{1,0:T(8,128)S(1)}, f32[32,768]{1,0:T(8,128)S(1)}, f32[32,768]{1,0:T(8...) custom-call(s32[1]{0:T(128)} %bitcast.me_ref, f32[10,10]{1,0:T(8,128)} %fcm_hbm.1, ...), custom_call_target="tpu_custom_call" | custom-call | tf_op jit(solution)/shard_map/physics/pallas_call | solution.py:213
  16.2 0.0 copy-start.2
  16.2 19.0 %all-to-all-start = ((f32[128,4,768]{2,1,0:T(4,128)}), f32[128,4,768]{2,1,0:T(4,128)}, u32[]{:S(2)}, u32[]{:S(2)}) async-start(f32[128,4,768]{2,1,0:T(4,128)} %get-tuple-element.29), calls=%async_computation | async-start | bytes 3145728 | tf_op jit(solution)/shard_map/all_to_all | solution.py:403
  35.2 1.1 %collective-permute-start = (f32[32,768]{1,0:T(8,128)S(1)}, f32[32,768]{1,0:T(8,128)S(1)}, u32[]{:S(2)}, u32[]{:S(2)}) collective-permute-start(f32[32,768]{1,0:T(8,128)S(1)} %get-tuple-element.17), channel_id=1, source_target_pairs={{0,1},{2,3},{4,5},{6,7},{8,9},{10,11},{12,13},{14,15},{16,17},{18,... | collective-permute-start | bytes 294920 | tf_op jit(solution)/shard_map/ppermute | solution.py:392
  36.3 6.3 %collective-permute-start.1 = (f32[32,768]{1,0:T(8,128)S(1)}, f32[32,768]{1,0:T(8,128)S(1)}, u32[]{:S(2)}, u32[]{:S(2)}) collective-permute-start(f32[32,768]{1,0:T(8,128)S(1)} %get-tuple-element.18), channel_id=1, source_target_pairs={{1,2},{3,4},{5,6},{7,8},{9,10},{11,12},{13,14},{15,16},{17,18},{19... | collective-permute-start | bytes 294920 | tf_op jit(solution)/shard_map/ppermute | solution.py:392
  42.6 0.0 copy-done.2
  42.6 0.6 shard_map.104.whole_ref
  43.2 0.0 copy-start
  43.2 0.0 copy-start.1
  43.2 1.0 %shard_map.105.l_ref = f32[728,512]{1,0:T(8,128)S(1)} custom-call(f32[728,512]{1,0:T(8,128)S(1)} %get-tuple-element.16.m_ref, bf16[512,512]{1,0:T(8,128)(2,1)S(1)} %shard_map.104.whole_ref), custom_call_target="tpu_custom_call" | custom-call | tf_op jit(solution)/shard_map/pallas_call | solution.py:407
  44.2 10.4 %collective-permute-done.prev_ref = f32[32,768]{1,0:T(8,128)S(1)} collective-permute-done((f32[32,768]{1,0:T(8,128)S(1)}, f32[32,768]{1,0:T(8,128)S(1)}, u32[]{:S(2)}, u32[]{:S(2)}) %collective-permute-start) | collective-permute-done | bytes 98336 | tf_op jit(solution)/shard_map/ppermute | solution.py:392
  54.6 5.6 %collective-permute-done.1.next_ref = f32[32,768]{1,0:T(8,128)S(1)} collective-permute-done((f32[32,768]{1,0:T(8,128)S(1)}, f32[32,768]{1,0:T(8,128)S(1)}, u32[]{:S(2)}, u32[]{:S(2)}) %collective-permute-start.1) | collective-permute-done | bytes 98336 | tf_op jit(solution)/shard_map/ppermute | solution.py:392
  60.3 0.0 copy-done
  60.3 0.0 copy-done.1
  60.3 2.4 %shard_map.106 = (f32[728,512]{1,0:T(8,128)S(1)}, f32[32,768]{1,0:T(8,128)S(1)}, f32[32,768]{1,0:T(8,128)S(1)}) custom-call(f32[728,512]{1,0:T(8,128)S(1)} %shard_map.105.l_ref, f32[32,768]{1,0:T(8,128)S(1)} %collective-permute-done.prev_ref, f32[32,768]{1,0:T(8,128)S(1)} %collective-permute-done.1.next_ref, bf16[64,512]{1,0:T(8,128)(2,1)S(1)} %get-tuple-element.19.in_ref, ...), custom_call_target="tpu_custom_call" | custom-call | tf_op jit(solution)/shard_map/pallas_call | solution.py:409
  62.7 0.1 collective-permute-start.2
  62.8 2.3 %collective-permute-start.3 = (f32[32,768]{1,0:T(8,128)S(1)}, f32[32,768]{1,0:T(8,128)S(1)}, u32[]{:S(2)}, u32[]{:S(2)}) collective-permute-start(f32[32,768]{1,0:T(8,128)S(1)} %get-tuple-element.25), channel_id=1, source_target_pairs={{1,2},{3,4},{5,6},{7,8},{9,10},{11,12},{13,14},{15,16},{17,18},{19... | collective-permute-start | bytes 294920 | tf_op jit(solution)/shard_map/ppermute | solution.py:392
  65.1 1.0 %shard_map.107.l_ref = f32[728,512]{1,0:T(8,128)S(1)} custom-call(f32[728,512]{1,0:T(8,128)S(1)} %get-tuple-element.23.m_ref, bf16[512,512]{1,0:T(8,128)(2,1)S(1)} %shard_map.104.whole_ref), custom_call_target="tpu_custom_call" | custom-call | tf_op jit(solution)/shard_map/pallas_call | solution.py:407
  66.1 1.3 %collective-permute-done.2.prev_ref = f32[32,768]{1,0:T(8,128)S(1)} collective-permute-done((f32[32,768]{1,0:T(8,128)S(1)}, f32[32,768]{1,0:T(8,128)S(1)}, u32[]{:S(2)}, u32[]{:S(2)}) %collective-permute-start.2) | collective-permute-done | bytes 98336 | tf_op jit(solution)/shard_map/ppermute | solution.py:392
  67.4 4.9 %collective-permute-done.3.next_ref = f32[32,768]{1,0:T(8,128)S(1)} collective-permute-done((f32[32,768]{1,0:T(8,128)S(1)}, f32[32,768]{1,0:T(8,128)S(1)}, u32[]{:S(2)}, u32[]{:S(2)}) %collective-permute-start.3) | collective-permute-done | bytes 98336 | tf_op jit(solution)/shard_map/ppermute | solution.py:392
  72.4 2.4 %shard_map.108 = (f32[728,512]{1,0:T(8,128)S(1)}, f32[32,768]{1,0:T(8,128)S(1)}, f32[32,768]{1,0:T(8,128)S(1)}) custom-call(f32[728,512]{1,0:T(8,128)S(1)} %shard_map.107.l_ref, f32[32,768]{1,0:T(8,128)S(1)} %collective-permute-done.2.prev_ref, f32[32,768]{1,0:T(8,128)S(1)} %collective-permute-done.3.next_ref, bf16[64,512]{1,0:T(8,128)(2,1)S(1)} %get-tuple-element.19.in_ref, ...), custom_call_target="tpu_custom_call" | custom-call | tf_op jit(solution)/shard_map/pallas_call | solution.py:409
  74.8 0.1 collective-permute-start.4
  74.9 2.3 %collective-permute-start.5 = (f32[32,768]{1,0:T(8,128)S(1)}, f32[32,768]{1,0:T(8,128)S(1)}, u32[]{:S(2)}, u32[]{:S(2)}) collective-permute-start(f32[32,768]{1,0:T(8,128)S(1)} %get-tuple-element.28), channel_id=1, source_target_pairs={{1,2},{3,4},{5,6},{7,8},{9,10},{11,12},{13,14},{15,16},{17,18},{19... | collective-permute-start | bytes 294920 | tf_op jit(solution)/shard_map/ppermute | solution.py:392
  77.2 1.0 %shard_map.109.l_ref = f32[728,512]{1,0:T(8,128)S(1)} custom-call(f32[728,512]{1,0:T(8,128)S(1)} %get-tuple-element.26.m_ref, bf16[512,512]{1,0:T(8,128)(2,1)S(1)} %shard_map.104.whole_ref), custom_call_target="tpu_custom_call" | custom-call | tf_op jit(solution)/shard_map/pallas_call | solution.py:407
  78.2 1.3 %collective-permute-done.4.prev_ref = f32[32,768]{1,0:T(8,128)S(1)} collective-permute-done((f32[32,768]{1,0:T(8,128)S(1)}, f32[32,768]{1,0:T(8,128)S(1)}, u32[]{:S(2)}, u32[]{:S(2)}) %collective-permute-start.4) | collective-permute-done | bytes 98336 | tf_op jit(solution)/shard_map/ppermute | solution.py:392
  79.5 4.9 %collective-permute-done.5.next_ref = f32[32,768]{1,0:T(8,128)S(1)} collective-permute-done((f32[32,768]{1,0:T(8,128)S(1)}, f32[32,768]{1,0:T(8,128)S(1)}, u32[]{:S(2)}, u32[]{:S(2)}) %collective-permute-start.5) | collective-permute-done | bytes 98336 | tf_op jit(solution)/shard_map/ppermute | solution.py:392
  84.4 1.5 %shard_map.110 = f32[720,512]{1,0:T(8,128)} custom-call(f32[728,512]{1,0:T(8,128)S(1)} %shard_map.109.l_ref, f32[32,768]{1,0:T(8,128)S(1)} %collective-permute-done.4.prev_ref, f32[32,768]{1,0:T(8,128)S(1)} %collective-permute-done.5.next_ref, bf16[64,512]{1,0:T(8,128)(2,1)S(1)} %get-tuple-element.19.in_ref), custom_call_target="tpu_custom_call" | custom-call | tf_op jit(solution)/shard_map/pallas_call | solution.py:413
  85.9 0.0 all-to-all-done.arrived_hbm
  85.9 3.4 %shard_map.111 = f32[720,512]{1,0:T(8,128)} custom-call(f32[128,4,768]{2,1,0:T(4,128)} %all-to-all-done.arrived_hbm), custom_call_target="tpu_custom_call" | custom-call | tf_op jit(solution)/shard_map/pallas_call | solution.py:411
Async XLA Ops:
  16.2 26.4 %copy-start.2 = (s32[4,32]{1,0:T(4,128)S(1)}, s32[4,32]{1,0:T(4,128)}, u32[]{:S(2)}) copy-start(s32[4,32]{1,0:T(4,128)} %neighbours_ref.1) | copy-start | bytes 1540
  16.2 69.7 %all-to-all-start = ((f32[128,4,768]{2,1,0:T(4,128)}), f32[128,4,768]{2,1,0:T(4,128)}, u32[]{:S(2)}, u32[]{:S(2)}) async-start(f32[128,4,768]{2,1,0:T(4,128)} %get-tuple-element.29), calls=%async_computation | async-start | bytes 3145728 | tf_op jit(solution)/shard_map/all_to_all | solution.py:403
  35.2 19.4 %collective-permute-start = (f32[32,768]{1,0:T(8,128)S(1)}, f32[32,768]{1,0:T(8,128)S(1)}, u32[]{:S(2)}, u32[]{:S(2)}) collective-permute-start(f32[32,768]{1,0:T(8,128)S(1)} %get-tuple-element.17), channel_id=1, source_target_pairs={{0,1},{2,3},{4,5},{6,7},{8,9},{10,11},{12,13},{14,15},{16,17},{18,... | collective-permute-start | bytes 294920 | tf_op jit(solution)/shard_map/ppermute | solution.py:392
  36.3 24.0 %collective-permute-start.1 = (f32[32,768]{1,0:T(8,128)S(1)}, f32[32,768]{1,0:T(8,128)S(1)}, u32[]{:S(2)}, u32[]{:S(2)}) collective-permute-start(f32[32,768]{1,0:T(8,128)S(1)} %get-tuple-element.18), channel_id=1, source_target_pairs={{1,2},{3,4},{5,6},{7,8},{9,10},{11,12},{13,14},{15,16},{17,18},{19... | collective-permute-start | bytes 294920 | tf_op jit(solution)/shard_map/ppermute | solution.py:392
  43.2 17.0 %copy-start = (f32[256,256]{1,0:T(8,128)S(1)}, f32[256,256]{1,0:T(8,128)}, u32[]{:S(2)}) copy-start(f32[256,256]{1,0:T(8,128)} %constant.18.clone.dy_hbm.dy_ref) | copy-start | bytes 786436
  43.2 17.0 %copy-start.1 = (f32[256,256]{1,0:T(8,128)S(1)}, f32[256,256]{1,0:T(8,128)}, u32[]{:S(2)}) copy-start(f32[256,256]{1,0:T(8,128)} %constant.17.clone.dx_hbm.dx_ref) | copy-start | bytes 786436
  62.7 4.7 %collective-permute-start.2 = (f32[32,768]{1,0:T(8,128)S(1)}, f32[32,768]{1,0:T(8,128)S(1)}, u32[]{:S(2)}, u32[]{:S(2)}) collective-permute-start(f32[32,768]{1,0:T(8,128)S(1)} %get-tuple-element.24), channel_id=1, source_target_pairs={{0,1},{2,3},{4,5},{6,7},{8,9},{10,11},{12,13},{14,15},{16,17},{18,... | collective-permute-start | bytes 294920 | tf_op jit(solution)/shard_map/ppermute | solution.py:392
  62.8 9.6 %collective-permute-start.3 = (f32[32,768]{1,0:T(8,128)S(1)}, f32[32,768]{1,0:T(8,128)S(1)}, u32[]{:S(2)}, u32[]{:S(2)}) collective-permute-start(f32[32,768]{1,0:T(8,128)S(1)} %get-tuple-element.25), channel_id=1, source_target_pairs={{1,2},{3,4},{5,6},{7,8},{9,10},{11,12},{13,14},{15,16},{17,18},{19... | collective-permute-start | bytes 294920 | tf_op jit(solution)/shard_map/ppermute | solution.py:392
  74.8 4.7 %collective-permute-start.4 = (f32[32,768]{1,0:T(8,128)S(1)}, f32[32,768]{1,0:T(8,128)S(1)}, u32[]{:S(2)}, u32[]{:S(2)}) collective-permute-start(f32[32,768]{1,0:T(8,128)S(1)} %get-tuple-element.27), channel_id=1, source_target_pairs={{0,1},{2,3},{4,5},{6,7},{8,9},{10,11},{12,13},{14,15},{16,17},{18,... | collective-permute-start | bytes 294920 | tf_op jit(solution)/shard_map/ppermute | solution.py:392
  74.9 9.6 %collective-permute-start.5 = (f32[32,768]{1,0:T(8,128)S(1)}, f32[32,768]{1,0:T(8,128)S(1)}, u32[]{:S(2)}, u32[]{:S(2)}) collective-permute-start(f32[32,768]{1,0:T(8,128)S(1)} %get-tuple-element.28), channel_id=1, source_target_pairs={{1,2},{3,4},{5,6},{7,8},{9,10},{11,12},{13,14},{15,16},{17,18},{19... | collective-permute-start | bytes 294920 | tf_op jit(solution)/shard_map/ppermute | solution.py:392

commit v7 on v6

--- a/solution.py
+++ b/solution.py
@@ -322,11 +322,12 @@
 
 def finish(l_ref, prev_ref, next_ref, in_ref, c_ref, done=lambda at: None):
     halo = jnp.concatenate([prev_ref[...], next_ref[...]], axis=0)
-    hh, hl = split2(jnp.transpose(halo)[0:TALL, :])
-    mass = l_ref[ROWS:TALL, :] + dot(hh[ROWS:TALL], in_ref[...]) + dot(hl[ROWS:TALL], in_ref[...])
+    both = jnp.concatenate(split2(jnp.transpose(halo)[0:TALL, :]), axis=1)
+    places = jnp.concatenate([in_ref[...], in_ref[...]], axis=0)
+    mass = l_ref[ROWS:TALL, :] + dot(both[ROWS:TALL], places)
     inverse = 1.0 / mass[0:1, :]
     for at in CHUNKS:
-        c_ref[at, :] = (l_ref[at, :] + dot(hh[at], in_ref[...]) + dot(hl[at], in_ref[...])) * inverse
+        c_ref[at, :] = (l_ref[at, :] + dot(both[at], places)) * inverse
         done(at)
 
 

time: 89.7 us -> 90 us (level)
  no operation moved by 1% of the time
where the time goes in v7:
time: 90 us; the launch traced here: 89.7 us
  starting transfers between devices  31.2 us (35%)
  Pallas kernels  29 us (32%)
  waiting for transfers between devices  28.6 us (32%)
  between operations  0.93 us (1%)
    ppermute x6, waiting for transfers between devices, swapped(): return lax.ppermute(array, AXES, pairs + [(j, i) for i, j in pairs])  28.6 us
    all_to_all x1, starting transfers between devices, step(): lax.all_to_all(send, AXES, split_axis=0, concat_axis=0, tiled=True)  19 us
    pallas_call x1, Pallas kernels, physics_call(): pl.pallas_call(physics_kernel, out_shape=shapes, in_specs=[SM] + [HB] * 9...  15.5 us
    ppermute x6, starting transfers between devices, swapped(): return lax.ppermute(array, AXES, pairs + [(j, i) for i, j in pairs])  12.2 us
    pallas_call x2, Pallas kernels, step(): call(next_kernel, [MOVED, HALO, HALO], [VM] * 9, [GRID] * 3)  5.03 us
    pallas_call x1, Pallas kernels, step(): call(place_kernel, [GRID], [HB], [((COLS // 4, 4, WIDE), F32), GRID], len...  3.36 us
    pallas_call x3, Pallas kernels, step(): total, = call(sum_kernel, [MOVED], [VM, VM])(m, whole)  2.87 us
  transfers between devices with their start and end apart: 7, of which 6 were waited for; matrix products, arithmetic and copies ran while one was open for 0% of the time, Pallas kernels for 11%

profile of v7, /device:TPU:0, one launch (start us, length us, event | category | flops | bytes accessed | tf_op | source)
XLA Modules:
  0.0 89.7 jit_solution(2344038448665924050)
XLA Ops:
  0.6 15.5 %physics.1 = (f32[128,4,768]{2,1,0:T(4,128)}, f32[720,512]{1,0:T(8,128)S(1)}, f32[728,512]{1,0:T(8,128)S(1)}, f32[32,768]{1,0:T(8,128)S(1)}, f32[32,768]{1,0:T(8...) custom-call(s32[1]{0:T(128)} %bitcast.me_ref, f32[10,10]{1,0:T(8,128)} %fcm_hbm.1, ...), custom_call_target="tpu_custom_call" | custom-call | tf_op jit(solution)/shard_map/physics/pallas_call | solution.py:213
  16.2 0.0 copy-start.2
  16.2 19.0 %all-to-all-start = ((f32[128,4,768]{2,1,0:T(4,128)}), f32[128,4,768]{2,1,0:T(4,128)}, u32[]{:S(2)}, u32[]{:S(2)}) async-start(f32[128,4,768]{2,1,0:T(4,128)} %get-tuple-element.29), calls=%async_computation | async-start | bytes 3145728 | tf_op jit(solution)/shard_map/all_to_all | solution.py:404
  35.2 1.1 %collective-permute-start = (f32[32,768]{1,0:T(8,128)S(1)}, f32[32,768]{1,0:T(8,128)S(1)}, u32[]{:S(2)}, u32[]{:S(2)}) collective-permute-start(f32[32,768]{1,0:T(8,128)S(1)} %get-tuple-element.17), channel_id=1, source_target_pairs={{0,1},{2,3},{4,5},{6,7},{8,9},{10,11},{12,13},{14,15},{16,17},{18,... | collective-permute-start | bytes 294920 | tf_op jit(solution)/shard_map/ppermute | solution.py:393
  36.3 6.3 %collective-permute-start.1 = (f32[32,768]{1,0:T(8,128)S(1)}, f32[32,768]{1,0:T(8,128)S(1)}, u32[]{:S(2)}, u32[]{:S(2)}) collective-permute-start(f32[32,768]{1,0:T(8,128)S(1)} %get-tuple-element.18), channel_id=1, source_target_pairs={{1,2},{3,4},{5,6},{7,8},{9,10},{11,12},{13,14},{15,16},{17,18},{19... | collective-permute-start | bytes 294920 | tf_op jit(solution)/shard_map/ppermute | solution.py:393
  42.6 0.0 copy-done.2
  42.6 0.6 shard_map.104.whole_ref
  43.2 0.0 copy-start
  43.2 0.0 copy-start.1
  43.2 1.0 %shard_map.105.l_ref = f32[728,512]{1,0:T(8,128)S(1)} custom-call(f32[728,512]{1,0:T(8,128)S(1)} %get-tuple-element.16.m_ref, bf16[512,512]{1,0:T(8,128)(2,1)S(1)} %shard_map.104.whole_ref), custom_call_target="tpu_custom_call" | custom-call | tf_op jit(solution)/shard_map/pallas_call | solution.py:408
  44.2 10.4 %collective-permute-done.prev_ref = f32[32,768]{1,0:T(8,128)S(1)} collective-permute-done((f32[32,768]{1,0:T(8,128)S(1)}, f32[32,768]{1,0:T(8,128)S(1)}, u32[]{:S(2)}, u32[]{:S(2)}) %collective-permute-start) | collective-permute-done | bytes 98336 | tf_op jit(solution)/shard_map/ppermute | solution.py:393
  54.6 5.6 %collective-permute-done.1.next_ref = f32[32,768]{1,0:T(8,128)S(1)} collective-permute-done((f32[32,768]{1,0:T(8,128)S(1)}, f32[32,768]{1,0:T(8,128)S(1)}, u32[]{:S(2)}, u32[]{:S(2)}) %collective-permute-start.1) | collective-permute-done | bytes 98336 | tf_op jit(solution)/shard_map/ppermute | solution.py:393
  60.3 0.0 copy-done
  60.3 0.0 copy-done.1
  60.3 2.5 %shard_map.106 = (f32[728,512]{1,0:T(8,128)S(1)}, f32[32,768]{1,0:T(8,128)S(1)}, f32[32,768]{1,0:T(8,128)S(1)}) custom-call(f32[728,512]{1,0:T(8,128)S(1)} %shard_map.105.l_ref, f32[32,768]{1,0:T(8,128)S(1)} %collective-permute-done.prev_ref, f32[32,768]{1,0:T(8,128)S(1)} %collective-permute-done.1.next_ref, bf16[64,512]{1,0:T(8,128)(2,1)S(1)} %get-tuple-element.19.in_ref, ...), custom_call_target="tpu_custom_call" | custom-call | tf_op jit(solution)/shard_map/pallas_call | solution.py:410
  62.8 0.1 collective-permute-start.2
  62.9 2.3 %collective-permute-start.3 = (f32[32,768]{1,0:T(8,128)S(1)}, f32[32,768]{1,0:T(8,128)S(1)}, u32[]{:S(2)}, u32[]{:S(2)}) collective-permute-start(f32[32,768]{1,0:T(8,128)S(1)} %get-tuple-element.25), channel_id=1, source_target_pairs={{1,2},{3,4},{5,6},{7,8},{9,10},{11,12},{13,14},{15,16},{17,18},{19... | collective-permute-start | bytes 294920 | tf_op jit(solution)/shard_map/ppermute | solution.py:393
  65.2 1.0 %shard_map.107.l_ref = f32[728,512]{1,0:T(8,128)S(1)} custom-call(f32[728,512]{1,0:T(8,128)S(1)} %get-tuple-element.23.m_ref, bf16[512,512]{1,0:T(8,128)(2,1)S(1)} %shard_map.104.whole_ref), custom_call_target="tpu_custom_call" | custom-call | tf_op jit(solution)/shard_map/pallas_call | solution.py:408
  66.2 1.3 %collective-permute-done.2.prev_ref = f32[32,768]{1,0:T(8,128)S(1)} collective-permute-done((f32[32,768]{1,0:T(8,128)S(1)}, f32[32,768]{1,0:T(8,128)S(1)}, u32[]{:S(2)}, u32[]{:S(2)}) %collective-permute-start.2) | collective-permute-done | bytes 98336 | tf_op jit(solution)/shard_map/ppermute | solution.py:393
  67.5 4.9 %collective-permute-done.3.next_ref = f32[32,768]{1,0:T(8,128)S(1)} collective-permute-done((f32[32,768]{1,0:T(8,128)S(1)}, f32[32,768]{1,0:T(8,128)S(1)}, u32[]{:S(2)}, u32[]{:S(2)}) %collective-permute-start.3) | collective-permute-done | bytes 98336 | tf_op jit(solution)/shard_map/ppermute | solution.py:393
  72.4 2.5 %shard_map.108 = (f32[728,512]{1,0:T(8,128)S(1)}, f32[32,768]{1,0:T(8,128)S(1)}, f32[32,768]{1,0:T(8,128)S(1)}) custom-call(f32[728,512]{1,0:T(8,128)S(1)} %shard_map.107.l_ref, f32[32,768]{1,0:T(8,128)S(1)} %collective-permute-done.2.prev_ref, f32[32,768]{1,0:T(8,128)S(1)} %collective-permute-done.3.next_ref, bf16[64,512]{1,0:T(8,128)(2,1)S(1)} %get-tuple-element.19.in_ref, ...), custom_call_target="tpu_custom_call" | custom-call | tf_op jit(solution)/shard_map/pallas_call | solution.py:410
  75.0 0.1 collective-permute-start.4
  75.1 2.3 %collective-permute-start.5 = (f32[32,768]{1,0:T(8,128)S(1)}, f32[32,768]{1,0:T(8,128)S(1)}, u32[]{:S(2)}, u32[]{:S(2)}) collective-permute-start(f32[32,768]{1,0:T(8,128)S(1)} %get-tuple-element.28), channel_id=1, source_target_pairs={{1,2},{3,4},{5,6},{7,8},{9,10},{11,12},{13,14},{15,16},{17,18},{19... | collective-permute-start | bytes 294920 | tf_op jit(solution)/shard_map/ppermute | solution.py:393
  77.4 1.0 %shard_map.109.l_ref = f32[728,512]{1,0:T(8,128)S(1)} custom-call(f32[728,512]{1,0:T(8,128)S(1)} %get-tuple-element.26.m_ref, bf16[512,512]{1,0:T(8,128)(2,1)S(1)} %shard_map.104.whole_ref), custom_call_target="tpu_custom_call" | custom-call | tf_op jit(solution)/shard_map/pallas_call | solution.py:408
  78.4 1.3 %collective-permute-done.4.prev_ref = f32[32,768]{1,0:T(8,128)S(1)} collective-permute-done((f32[32,768]{1,0:T(8,128)S(1)}, f32[32,768]{1,0:T(8,128)S(1)}, u32[]{:S(2)}, u32[]{:S(2)}) %collective-permute-start.4) | collective-permute-done | bytes 98336 | tf_op jit(solution)/shard_map/ppermute | solution.py:393
  79.7 4.9 %collective-permute-done.5.next_ref = f32[32,768]{1,0:T(8,128)S(1)} collective-permute-done((f32[32,768]{1,0:T(8,128)S(1)}, f32[32,768]{1,0:T(8,128)S(1)}, u32[]{:S(2)}, u32[]{:S(2)}) %collective-permute-start.5) | collective-permute-done | bytes 98336 | tf_op jit(solution)/shard_map/ppermute | solution.py:393
  84.6 1.5 %shard_map.110 = f32[720,512]{1,0:T(8,128)} custom-call(f32[728,512]{1,0:T(8,128)S(1)} %shard_map.109.l_ref, f32[32,768]{1,0:T(8,128)S(1)} %collective-permute-done.4.prev_ref, f32[32,768]{1,0:T(8,128)S(1)} %collective-permute-done.5.next_ref, bf16[64,512]{1,0:T(8,128)(2,1)S(1)} %get-tuple-element.19.in_ref), custom_call_target="tpu_custom_call" | custom-call | tf_op jit(solution)/shard_map/pallas_call | solution.py:414
  86.2 0.0 all-to-all-done.arrived_hbm
  86.2 3.4 %shard_map.111 = f32[720,512]{1,0:T(8,128)} custom-call(f32[128,4,768]{2,1,0:T(4,128)} %all-to-all-done.arrived_hbm), custom_call_target="tpu_custom_call" | custom-call | tf_op jit(solution)/shard_map/pallas_call | solution.py:412
Async XLA Ops:
  16.2 26.4 %copy-start.2 = (s32[4,32]{1,0:T(4,128)S(1)}, s32[4,32]{1,0:T(4,128)}, u32[]{:S(2)}) copy-start(s32[4,32]{1,0:T(4,128)} %neighbours_ref.1) | copy-start | bytes 1540
  16.2 70.0 %all-to-all-start = ((f32[128,4,768]{2,1,0:T(4,128)}), f32[128,4,768]{2,1,0:T(4,128)}, u32[]{:S(2)}, u32[]{:S(2)}) async-start(f32[128,4,768]{2,1,0:T(4,128)} %get-tuple-element.29), calls=%async_computation | async-start | bytes 3145728 | tf_op jit(solution)/shard_map/all_to_all | solution.py:404
  35.2 19.4 %collective-permute-start = (f32[32,768]{1,0:T(8,128)S(1)}, f32[32,768]{1,0:T(8,128)S(1)}, u32[]{:S(2)}, u32[]{:S(2)}) collective-permute-start(f32[32,768]{1,0:T(8,128)S(1)} %get-tuple-element.17), channel_id=1, source_target_pairs={{0,1},{2,3},{4,5},{6,7},{8,9},{10,11},{12,13},{14,15},{16,17},{18,... | collective-permute-start | bytes 294920 | tf_op jit(solution)/shard_map/ppermute | solution.py:393
  36.3 24.0 %collective-permute-start.1 = (f32[32,768]{1,0:T(8,128)S(1)}, f32[32,768]{1,0:T(8,128)S(1)}, u32[]{:S(2)}, u32[]{:S(2)}) collective-permute-start(f32[32,768]{1,0:T(8,128)S(1)} %get-tuple-element.18), channel_id=1, source_target_pairs={{1,2},{3,4},{5,6},{7,8},{9,10},{11,12},{13,14},{15,16},{17,18},{19... | collective-permute-start | bytes 294920 | tf_op jit(solution)/shard_map/ppermute | solution.py:393
  43.2 17.0 %copy-start = (f32[256,256]{1,0:T(8,128)S(1)}, f32[256,256]{1,0:T(8,128)}, u32[]{:S(2)}) copy-start(f32[256,256]{1,0:T(8,128)} %constant.18.clone.dy_hbm.dy_ref) | copy-start | bytes 786436
  43.2 17.0 %copy-start.1 = (f32[256,256]{1,0:T(8,128)S(1)}, f32[256,256]{1,0:T(8,128)}, u32[]{:S(2)}) copy-start(f32[256,256]{1,0:T(8,128)} %constant.17.clone.dx_hbm.dx_ref) | copy-start | bytes 786436
  62.8 4.7 %collective-permute-start.2 = (f32[32,768]{1,0:T(8,128)S(1)}, f32[32,768]{1,0:T(8,128)S(1)}, u32[]{:S(2)}, u32[]{:S(2)}) collective-permute-start(f32[32,768]{1,0:T(8,128)S(1)} %get-tuple-element.24), channel_id=1, source_target_pairs={{0,1},{2,3},{4,5},{6,7},{8,9},{10,11},{12,13},{14,15},{16,17},{18,... | collective-permute-start | bytes 294920 | tf_op jit(solution)/shard_map/ppermute | solution.py:393
  62.9 9.6 %collective-permute-start.3 = (f32[32,768]{1,0:T(8,128)S(1)}, f32[32,768]{1,0:T(8,128)S(1)}, u32[]{:S(2)}, u32[]{:S(2)}) collective-permute-start(f32[32,768]{1,0:T(8,128)S(1)} %get-tuple-element.25), channel_id=1, source_target_pairs={{1,2},{3,4},{5,6},{7,8},{9,10},{11,12},{13,14},{15,16},{17,18},{19... | collective-permute-start | bytes 294920 | tf_op jit(solution)/shard_map/ppermute | solution.py:393
  75.0 4.7 %collective-permute-start.4 = (f32[32,768]{1,0:T(8,128)S(1)}, f32[32,768]{1,0:T(8,128)S(1)}, u32[]{:S(2)}, u32[]{:S(2)}) collective-permute-start(f32[32,768]{1,0:T(8,128)S(1)} %get-tuple-element.27), channel_id=1, source_target_pairs={{0,1},{2,3},{4,5},{6,7},{8,9},{10,11},{12,13},{14,15},{16,17},{18,... | collective-permute-start | bytes 294920 | tf_op jit(solution)/shard_map/ppermute | solution.py:393
  75.1 9.6 %collective-permute-start.5 = (f32[32,768]{1,0:T(8,128)S(1)}, f32[32,768]{1,0:T(8,128)S(1)}, u32[]{:S(2)}, u32[]{:S(2)}) collective-permute-start(f32[32,768]{1,0:T(8,128)S(1)} %get-tuple-element.28), channel_id=1, source_target_pairs={{1,2},{3,4},{5,6},{7,8},{9,10},{11,12},{13,14},{15,16},{17,18},{19... | collective-permute-start | bytes 294920 | tf_op jit(solution)/shard_map/ppermute | solution.py:393

commit v8 on v6

--- a/solution.py
+++ b/solution.py
@@ -143,15 +143,13 @@
     rates(state_ref[...], dx_ref, dy_ref, dxs, dys)
     xh, xl = split2(x0[...])
     xhh = jnp.concatenate([xh, xh], axis=1)
-    for n in range(0, WIDE, 256):
-        at = slice(n, n + 256)
-        y = (dot(xl, kk[0:WIDE, at]) + dot(xhh, kk[:, at])) * (1.0 / PHYSICS_RATE)
-        yy[:, at] = y
-        t = jnp.tanh(y)
-        tt[:, at] = t
-        q = t.astype(BF16)
-        rr[:, at] = t - q.astype(F32)
-        qa[:, at] = q
+    y = (dot(xl, kk[0:WIDE, :]) + dot(xhh, kk[...])) * (1.0 / PHYSICS_RATE)
+    yy[...] = y
+    t = jnp.tanh(y)
+    tt[...] = t
+    q = t.astype(BF16)
+    rr[...] = t - q.astype(F32)
+    qa[...] = q
 
     def step(rows, live, old, new, low):
         deep = 2 * WIDE if low else WIDE
@@ -187,12 +185,12 @@
     lax.fori_loop(0, 8, two_sweeps, 0)
     q_send = jnp.where(iota((COLS, COLS), 0).astype(F32) == srank_sorted, 1.0, 0.0).astype(BF16)
     fh, fl = split2(x0[...] + PHYSICS_RATE * tt[...])
-    out = dot(q_send, fh) + dot(q_send, fl)
+    out = dot(jnp.concatenate([q_send, q_send], axis=1), jnp.concatenate([fh, fl], axis=0))
     send_ref[...] = out.reshape(COLS // 4, 4, WIDE)
     store_send = pltpu.make_async_copy(send_ref, send_hbm, sems.at[9])
     store_send.start()
     th, tl = split2(jnp.transpose(tt[...])[0:ROWS, :] * (PHYSICS_RATE / SUBSTEPS))
-    tend_ref[...] = dot(th, perm) + dot(tl, perm)
+    tend_ref[...] = dot(jnp.concatenate([th, tl], axis=1), jnp.concatenate([perm, perm], axis=0))
     move(lambda at, n: state_ref[pl.ds(at, n), :], tend_ref, mrow_ref, out_ref, dxs, dys, m_ref, mine_a_ref, mine_b_ref)
     store_send.wait()
 
@@ -294,9 +292,10 @@
     vh, vl = split2(value)
     for half in (0, 256):
         at = slice(half, half + 256)
+        parts = jnp.concatenate([vh[:, at], vl[:, at], vh[:, at]], axis=1)
         for d_ref, acc in ((dx_ref, dxs), (dy_ref, dys)):
             dh, dl = split2(d_ref[...])
-            acc[:, at] = dot(vh[:, at], dh) + dot(vl[:, at], dh) + dot(vh[:, at], dl)
+            acc[:, at] = dot(parts, jnp.concatenate([dh, dh, dl], axis=0))
 
 
 def move(read, tend_ref, mrow_ref, out_ref, dxs, dys, m_ref, mine_a_ref, mine_b_ref):

time: 89.7 us -> 89.7 us (level)
  no operation moved by 1% of the time
where the time goes in v8:
time: 89.7 us; the launch traced here: 89.5 us
  starting transfers between devices  31.2 us (35%)
  Pallas kernels  28.8 us (32%)
  waiting for transfers between devices  28.6 us (32%)
  between operations  0.93 us (1%)
    ppermute x6, waiting for transfers between devices, swapped(): return lax.ppermute(array, AXES, pairs + [(j, i) for i, j in pairs])  28.6 us
    all_to_all x1, starting transfers between devices, step(): lax.all_to_all(send, AXES, split_axis=0, concat_axis=0, tiled=True)  19 us
    pallas_call x1, Pallas kernels, physics_call(): pl.pallas_call(physics_kernel, out_shape=shapes, in_specs=[SM] + [HB] * 9...  15.5 us
    ppermute x6, starting transfers between devices, swapped(): return lax.ppermute(array, AXES, pairs + [(j, i) for i, j in pairs])  12.2 us
    pallas_call x2, Pallas kernels, step(): call(next_kernel, [MOVED, HALO, HALO], [VM] * 9, [GRID] * 3)  4.9 us
    pallas_call x1, Pallas kernels, step(): call(place_kernel, [GRID], [HB], [((COLS // 4, 4, WIDE), F32), GRID], len...  3.36 us
    pallas_call x3, Pallas kernels, step(): total, = call(sum_kernel, [MOVED], [VM, VM])(m, whole)  2.87 us
  transfers between devices with their start and end apart: 7, of which 6 were waited for; matrix products, arithmetic and copies ran while one was open for 0% of the time, Pallas kernels for 11%

profile of v8, /device:TPU:0, one launch (start us, length us, event | category | flops | bytes accessed | tf_op | source)
XLA Modules:
  0.0 89.5 jit_solution(18123216028104822462)
XLA Ops:
  0.6 15.5 %physics.1 = (f32[128,4,768]{2,1,0:T(4,128)}, f32[720,512]{1,0:T(8,128)S(1)}, f32[728,512]{1,0:T(8,128)S(1)}, f32[32,768]{1,0:T(8,128)S(1)}, f32[32,768]{1,0:T(8...) custom-call(s32[1]{0:T(128)} %bitcast.me_ref, f32[10,10]{1,0:T(8,128)} %fcm_hbm.1, ...), custom_call_target="tpu_custom_call" | custom-call | tf_op jit(solution)/shard_map/physics/pallas_call | solution.py:211
  16.2 0.0 copy-start.2
  16.2 19.0 %all-to-all-start = ((f32[128,4,768]{2,1,0:T(4,128)}), f32[128,4,768]{2,1,0:T(4,128)}, u32[]{:S(2)}, u32[]{:S(2)}) async-start(f32[128,4,768]{2,1,0:T(4,128)} %get-tuple-element.29), calls=%async_computation | async-start | bytes 3145728 | tf_op jit(solution)/shard_map/all_to_all | solution.py:402
  35.2 1.1 %collective-permute-start = (f32[32,768]{1,0:T(8,128)S(1)}, f32[32,768]{1,0:T(8,128)S(1)}, u32[]{:S(2)}, u32[]{:S(2)}) collective-permute-start(f32[32,768]{1,0:T(8,128)S(1)} %get-tuple-element.17), channel_id=1, source_target_pairs={{0,1},{2,3},{4,5},{6,7},{8,9},{10,11},{12,13},{14,15},{16,17},{18,... | collective-permute-start | bytes 294920 | tf_op jit(solution)/shard_map/ppermute | solution.py:391
  36.3 6.3 %collective-permute-start.1 = (f32[32,768]{1,0:T(8,128)S(1)}, f32[32,768]{1,0:T(8,128)S(1)}, u32[]{:S(2)}, u32[]{:S(2)}) collective-permute-start(f32[32,768]{1,0:T(8,128)S(1)} %get-tuple-element.18), channel_id=1, source_target_pairs={{1,2},{3,4},{5,6},{7,8},{9,10},{11,12},{13,14},{15,16},{17,18},{19... | collective-permute-start | bytes 294920 | tf_op jit(solution)/shard_map/ppermute | solution.py:391
  42.5 0.0 copy-done.2
  42.6 0.6 shard_map.104.whole_ref
  43.2 0.0 copy-start
  43.2 0.0 copy-start.1
  43.2 1.0 %shard_map.105.l_ref = f32[728,512]{1,0:T(8,128)S(1)} custom-call(f32[728,512]{1,0:T(8,128)S(1)} %get-tuple-element.16.m_ref, bf16[512,512]{1,0:T(8,128)(2,1)S(1)} %shard_map.104.whole_ref), custom_call_target="tpu_custom_call" | custom-call | tf_op jit(solution)/shard_map/pallas_call | solution.py:406
  44.2 10.4 %collective-permute-done.prev_ref = f32[32,768]{1,0:T(8,128)S(1)} collective-permute-done((f32[32,768]{1,0:T(8,128)S(1)}, f32[32,768]{1,0:T(8,128)S(1)}, u32[]{:S(2)}, u32[]{:S(2)}) %collective-permute-start) | collective-permute-done | bytes 98336 | tf_op jit(solution)/shard_map/ppermute | solution.py:391
  54.6 5.6 %collective-permute-done.1.next_ref = f32[32,768]{1,0:T(8,128)S(1)} collective-permute-done((f32[32,768]{1,0:T(8,128)S(1)}, f32[32,768]{1,0:T(8,128)S(1)}, u32[]{:S(2)}, u32[]{:S(2)}) %collective-permute-start.1) | collective-permute-done | bytes 98336 | tf_op jit(solution)/shard_map/ppermute | solution.py:391
  60.2 0.0 copy-done
  60.2 0.0 copy-done.1
  60.2 2.5 %shard_map.106 = (f32[728,512]{1,0:T(8,128)S(1)}, f32[32,768]{1,0:T(8,128)S(1)}, f32[32,768]{1,0:T(8,128)S(1)}) custom-call(f32[728,512]{1,0:T(8,128)S(1)} %shard_map.105.l_ref, f32[32,768]{1,0:T(8,128)S(1)} %collective-permute-done.prev_ref, f32[32,768]{1,0:T(8,128)S(1)} %collective-permute-done.1.next_ref, bf16[64,512]{1,0:T(8,128)(2,1)S(1)} %get-tuple-element.19.in_ref, ...), custom_call_target="tpu_custom_call" | custom-call | tf_op jit(solution)/shard_map/pallas_call | solution.py:408
  62.7 0.1 collective-permute-start.2
  62.8 2.3 %collective-permute-start.3 = (f32[32,768]{1,0:T(8,128)S(1)}, f32[32,768]{1,0:T(8,128)S(1)}, u32[]{:S(2)}, u32[]{:S(2)}) collective-permute-start(f32[32,768]{1,0:T(8,128)S(1)} %get-tuple-element.25), channel_id=1, source_target_pairs={{1,2},{3,4},{5,6},{7,8},{9,10},{11,12},{13,14},{15,16},{17,18},{19... | collective-permute-start | bytes 294920 | tf_op jit(solution)/shard_map/ppermute | solution.py:391
  65.1 1.0 %shard_map.107.l_ref = f32[728,512]{1,0:T(8,128)S(1)} custom-call(f32[728,512]{1,0:T(8,128)S(1)} %get-tuple-element.23.m_ref, bf16[512,512]{1,0:T(8,128)(2,1)S(1)} %shard_map.104.whole_ref), custom_call_target="tpu_custom_call" | custom-call | tf_op jit(solution)/shard_map/pallas_call | solution.py:406
  66.1 1.3 %collective-permute-done.2.prev_ref = f32[32,768]{1,0:T(8,128)S(1)} collective-permute-done((f32[32,768]{1,0:T(8,128)S(1)}, f32[32,768]{1,0:T(8,128)S(1)}, u32[]{:S(2)}, u32[]{:S(2)}) %collective-permute-start.2) | collective-permute-done | bytes 98336 | tf_op jit(solution)/shard_map/ppermute | solution.py:391
  67.4 4.9 %collective-permute-done.3.next_ref = f32[32,768]{1,0:T(8,128)S(1)} collective-permute-done((f32[32,768]{1,0:T(8,128)S(1)}, f32[32,768]{1,0:T(8,128)S(1)}, u32[]{:S(2)}, u32[]{:S(2)}) %collective-permute-start.3) | collective-permute-done | bytes 98336 | tf_op jit(solution)/shard_map/ppermute | solution.py:391
  72.4 2.4 %shard_map.108 = (f32[728,512]{1,0:T(8,128)S(1)}, f32[32,768]{1,0:T(8,128)S(1)}, f32[32,768]{1,0:T(8,128)S(1)}) custom-call(f32[728,512]{1,0:T(8,128)S(1)} %shard_map.107.l_ref, f32[32,768]{1,0:T(8,128)S(1)} %collective-permute-done.2.prev_ref, f32[32,768]{1,0:T(8,128)S(1)} %collective-permute-done.3.next_ref, bf16[64,512]{1,0:T(8,128)(2,1)S(1)} %get-tuple-element.19.in_ref, ...), custom_call_target="tpu_custom_call" | custom-call | tf_op jit(solution)/shard_map/pallas_call | solution.py:408
  74.8 0.1 collective-permute-start.4
  74.9 2.3 %collective-permute-start.5 = (f32[32,768]{1,0:T(8,128)S(1)}, f32[32,768]{1,0:T(8,128)S(1)}, u32[]{:S(2)}, u32[]{:S(2)}) collective-permute-start(f32[32,768]{1,0:T(8,128)S(1)} %get-tuple-element.28), channel_id=1, source_target_pairs={{1,2},{3,4},{5,6},{7,8},{9,10},{11,12},{13,14},{15,16},{17,18},{19... | collective-permute-start | bytes 294920 | tf_op jit(solution)/shard_map/ppermute | solution.py:391
  77.2 1.0 %shard_map.109.l_ref = f32[728,512]{1,0:T(8,128)S(1)} custom-call(f32[728,512]{1,0:T(8,128)S(1)} %get-tuple-element.26.m_ref, bf16[512,512]{1,0:T(8,128)(2,1)S(1)} %shard_map.104.whole_ref), custom_call_target="tpu_custom_call" | custom-call | tf_op jit(solution)/shard_map/pallas_call | solution.py:406
  78.2 1.3 %collective-permute-done.4.prev_ref = f32[32,768]{1,0:T(8,128)S(1)} collective-permute-done((f32[32,768]{1,0:T(8,128)S(1)}, f32[32,768]{1,0:T(8,128)S(1)}, u32[]{:S(2)}, u32[]{:S(2)}) %collective-permute-start.4) | collective-permute-done | bytes 98336 | tf_op jit(solution)/shard_map/ppermute | solution.py:391
  79.5 4.9 %collective-permute-done.5.next_ref = f32[32,768]{1,0:T(8,128)S(1)} collective-permute-done((f32[32,768]{1,0:T(8,128)S(1)}, f32[32,768]{1,0:T(8,128)S(1)}, u32[]{:S(2)}, u32[]{:S(2)}) %collective-permute-start.5) | collective-permute-done | bytes 98336 | tf_op jit(solution)/shard_map/ppermute | solution.py:391
  84.5 1.5 %shard_map.110 = f32[720,512]{1,0:T(8,128)} custom-call(f32[728,512]{1,0:T(8,128)S(1)} %shard_map.109.l_ref, f32[32,768]{1,0:T(8,128)S(1)} %collective-permute-done.4.prev_ref, f32[32,768]{1,0:T(8,128)S(1)} %collective-permute-done.5.next_ref, bf16[64,512]{1,0:T(8,128)(2,1)S(1)} %get-tuple-element.19.in_ref), custom_call_target="tpu_custom_call" | custom-call | tf_op jit(solution)/shard_map/pallas_call | solution.py:412
  85.9 0.0 all-to-all-done.arrived_hbm
  85.9 3.4 %shard_map.111 = f32[720,512]{1,0:T(8,128)} custom-call(f32[128,4,768]{2,1,0:T(4,128)} %all-to-all-done.arrived_hbm), custom_call_target="tpu_custom_call" | custom-call | tf_op jit(solution)/shard_map/pallas_call | solution.py:410
Async XLA Ops:
  16.2 26.4 %copy-start.2 = (s32[4,32]{1,0:T(4,128)S(1)}, s32[4,32]{1,0:T(4,128)}, u32[]{:S(2)}) copy-start(s32[4,32]{1,0:T(4,128)} %neighbours_ref.1) | copy-start | bytes 1540
  16.2 69.8 %all-to-all-start = ((f32[128,4,768]{2,1,0:T(4,128)}), f32[128,4,768]{2,1,0:T(4,128)}, u32[]{:S(2)}, u32[]{:S(2)}) async-start(f32[128,4,768]{2,1,0:T(4,128)} %get-tuple-element.29), calls=%async_computation | async-start | bytes 3145728 | tf_op jit(solution)/shard_map/all_to_all | solution.py:402
  35.2 19.4 %collective-permute-start = (f32[32,768]{1,0:T(8,128)S(1)}, f32[32,768]{1,0:T(8,128)S(1)}, u32[]{:S(2)}, u32[]{:S(2)}) collective-permute-start(f32[32,768]{1,0:T(8,128)S(1)} %get-tuple-element.17), channel_id=1, source_target_pairs={{0,1},{2,3},{4,5},{6,7},{8,9},{10,11},{12,13},{14,15},{16,17},{18,... | collective-permute-start | bytes 294920 | tf_op jit(solution)/shard_map/ppermute | solution.py:391
  36.3 24.0 %collective-permute-start.1 = (f32[32,768]{1,0:T(8,128)S(1)}, f32[32,768]{1,0:T(8,128)S(1)}, u32[]{:S(2)}, u32[]{:S(2)}) collective-permute-start(f32[32,768]{1,0:T(8,128)S(1)} %get-tuple-element.18), channel_id=1, source_target_pairs={{1,2},{3,4},{5,6},{7,8},{9,10},{11,12},{13,14},{15,16},{17,18},{19... | collective-permute-start | bytes 294920 | tf_op jit(solution)/shard_map/ppermute | solution.py:391
  43.2 17.0 %copy-start = (f32[256,256]{1,0:T(8,128)S(1)}, f32[256,256]{1,0:T(8,128)}, u32[]{:S(2)}) copy-start(f32[256,256]{1,0:T(8,128)} %constant.18.clone.dy_hbm.dy_ref) | copy-start | bytes 786436
  43.2 17.0 %copy-start.1 = (f32[256,256]{1,0:T(8,128)S(1)}, f32[256,256]{1,0:T(8,128)}, u32[]{:S(2)}) copy-start(f32[256,256]{1,0:T(8,128)} %constant.17.clone.dx_hbm.dx_ref) | copy-start | bytes 786436
  62.7 4.7 %collective-permute-start.2 = (f32[32,768]{1,0:T(8,128)S(1)}, f32[32,768]{1,0:T(8,128)S(1)}, u32[]{:S(2)}, u32[]{:S(2)}) collective-permute-start(f32[32,768]{1,0:T(8,128)S(1)} %get-tuple-element.24), channel_id=1, source_target_pairs={{0,1},{2,3},{4,5},{6,7},{8,9},{10,11},{12,13},{14,15},{16,17},{18,... | collective-permute-start | bytes 294920 | tf_op jit(solution)/shard_map/ppermute | solution.py:391
  62.8 9.6 %collective-permute-start.3 = (f32[32,768]{1,0:T(8,128)S(1)}, f32[32,768]{1,0:T(8,128)S(1)}, u32[]{:S(2)}, u32[]{:S(2)}) collective-permute-start(f32[32,768]{1,0:T(8,128)S(1)} %get-tuple-element.25), channel_id=1, source_target_pairs={{1,2},{3,4},{5,6},{7,8},{9,10},{11,12},{13,14},{15,16},{17,18},{19... | collective-permute-start | bytes 294920 | tf_op jit(solution)/shard_map/ppermute | solution.py:391
  74.8 4.7 %collective-permute-start.4 = (f32[32,768]{1,0:T(8,128)S(1)}, f32[32,768]{1,0:T(8,128)S(1)}, u32[]{:S(2)}, u32[]{:S(2)}) collective-permute-start(f32[32,768]{1,0:T(8,128)S(1)} %get-tuple-element.27), channel_id=1, source_target_pairs={{0,1},{2,3},{4,5},{6,7},{8,9},{10,11},{12,13},{14,15},{16,17},{18,... | collective-permute-start | bytes 294920 | tf_op jit(solution)/shard_map/ppermute | solution.py:391
  74.9 9.6 %collective-permute-start.5 = (f32[32,768]{1,0:T(8,128)S(1)}, f32[32,768]{1,0:T(8,128)S(1)}, u32[]{:S(2)}, u32[]{:S(2)}) collective-permute-start(f32[32,768]{1,0:T(8,128)S(1)} %get-tuple-element.28), channel_id=1, source_target_pairs={{1,2},{3,4},{5,6},{7,8},{9,10},{11,12},{13,14},{15,16},{17,18},{19... | collective-permute-start | bytes 294920 | tf_op jit(solution)/shard_map/ppermute | solution.py:391
